TPU v7x, 32 devices: a whole 2x2x4 slice. The times are simulated.
32 devices in a mesh: ctx: 4 (over z), exp: 8 (over y, x, core).
Axes of the slice: x: 2, y: 2, z: 4, core: 2. Of those that a mesh axis runs over, the one named last changes fastest.
Arguments:
- resid_input: bfloat16 [512, 4096], P(('ctx', 'exp')), may hold values from -80 to 80
- norm_gain: float32 [4096], replicated, may hold values from 0.1 to 1.9
- expert_ids: int32 [512, 2], P(('ctx', 'exp')), may hold values from 0 to 3, all different within a row
- route_probs: bfloat16 [512, 2], P(('ctx', 'exp')), may hold values from 0.19921875 to 0.796875
- gate_weight: bfloat16 [8, 6144, 4096], P('exp', 'ctx'), may hold values from -0.09375 to 0.09375
- up_weight: bfloat16 [8, 6144, 4096], P('exp', 'ctx'), may hold values from -0.09375 to 0.09375
- down_weight: bfloat16 [8, 6144, 4096], P('exp', 'ctx'), may hold values from -0.09375 to 0.09375
- grad_output: bfloat16 [512, 4096], P('ctx', 'exp'), may hold values from -6 to 6
- mixer_input: bfloat16 [512, 4096], P('ctx', 'exp'), may hold values from -0.29882812 to 0.29882812
- state_input: bfloat16 [512, 2048], P('ctx', 'exp'), may hold values from -0.5 to 0.5
- state_output: bfloat16 [512, 2048], P('ctx', 'exp'), may hold values from -0.119628906 to 0.119628906
- step_size: float32 [512, 64], P('ctx', 'exp'), may hold values from 0.3 to 1.5
- log_retention: float32 [512, 64], P('ctx', 'exp'), may hold values from -1.5 to 0, as said below
- skip_gain: float32 [64], P('exp'), may hold values from 0.5 to 1.5
Outputs:
- resid_grad: bfloat16 [512, 4096], P('ctx', 'exp')
- mixer_grad: bfloat16 [512, 4096], P('ctx', 'exp')
- state_input_grad: float32 [512, 2048], P('ctx', 'exp')
Inputs may be any that keep to these rules, and one draw needn't show every extreme that they name: `expert_ids`: each token names 2 different experts. `log_retention`: strictly negative.
All inputs are finite; a program needn't handle non-finite values.
Results may differ from a plain program's by a relative error of at most 0.009.
Values may be sent and summed in bfloat16 or wider, within the bound.
No kernel may reach another device: no remote copies, remote signals or barrier semaphores. Data moves between devices by JAX's collectives and lax.ppermute only.
A program may use at most 128 MiB of HBM per device.

v0:
```python
from functools import partial

import jax
import jax.numpy as jnp
from jax import lax
from jax.sharding import PartitionSpec as P

N = 128


highest = lax.Precision.HIGHEST
norm_epsilon = 1e-05


def carried_in(shard, axis, join, neutral):
    count = lax.axis_size(axis)
    place = lax.axis_index(axis)
    ahead = count - 1 - place
    gathered = jax.tree.map(
        lambda a, kind: lax.all_gather(a.astype(kind), axis), shard, (jnp.bfloat16, jnp.bfloat16)
    )
    state = jax.tree.map(lambda a, e: jnp.zeros_like(a) + jnp.asarray(e, a.dtype), shard, neutral)

    def one(hop, state):
        source = count - 1 - hop
        return join(
            state,
            jax.tree.map(
                lambda a, own: lax.dynamic_index_in_dim(a, source, 0, False).astype(own.dtype),
                gathered,
                shard,
            ),
        )

    return lax.fori_loop(0, ahead, one, state)


def expert_slots(flat_ids, expert, capacity):
    matches = (flat_ids == expert).astype(jnp.int32)
    position = jnp.cumsum(matches) - matches
    slot_numbers = jnp.arange(capacity, dtype=jnp.int32)[:, None]
    picked = (position[None, :] == slot_numbers) & (matches[None, :] > 0)
    return picked.astype(jnp.bfloat16)


def mixer_setup(input_states, output_states, log_retention):
    token_count = log_retention.shape[0]
    cumulative = jnp.cumsum(log_retention, axis=0)
    later_mask = jnp.arange(token_count)[None, :] >= jnp.arange(token_count)[:, None]
    difference = cumulative.T[:, None, :] - cumulative.T[:, :, None]
    decay_matrix = jnp.where(
        later_mask[None], jnp.exp(jnp.where(later_mask[None], difference, 0.0)), 0.0
    )
    intersection = jnp.einsum(
        "tgn,sgn->gts", input_states, output_states, preferred_element_type=jnp.float32
    )
    return (cumulative, decay_matrix, intersection)


def mixer_local(
    upstream, inputs_float, step_size, output_float, cumulative, decay_matrix, intersection
):
    token_count, group_count, state_size = output_float.shape
    head_count = upstream.shape[1]
    head_size = upstream.shape[2]
    head_groups = head_count // group_count
    grouped_up = upstream.reshape(token_count, group_count, head_groups, head_size)
    mixed_weights = (
        decay_matrix.reshape(group_count, head_groups, token_count, token_count)
        * intersection[:, None]
    )
    intra_x = jnp.einsum("gjts,sgjp->tgjp", mixed_weights, grouped_up, precision=highest)
    intra_x = intra_x.reshape(token_count, head_count, head_size)
    inner_product = jnp.einsum("thp,shp->hts", inputs_float, upstream, precision=highest)
    weighted = decay_matrix * inner_product * step_size.T[:, :, None]
    grouped = weighted.reshape(group_count, head_groups, token_count, token_count).sum(axis=1)
    intra_b = jnp.einsum("gts,sgn->tgn", grouped, output_float, precision=highest)
    head_decay = jnp.exp(cumulative).reshape(token_count, group_count, head_groups)
    local_state = jnp.einsum(
        "sgj,sgn,sgjp->gjnp", head_decay, output_float, grouped_up, precision=highest
    )
    return (intra_x, intra_b, local_state.reshape(head_count, state_size, head_size))


def chain_combine(earlier, later):
    return (later[0] * earlier[0], later[1] + later[0][:, None, None] * earlier[1])


def body(
    resid_input,
    norm_gain,
    expert_ids,
    route_probs,
    gate_weight,
    up_weight,
    down_weight,
    grad_output,
    mixer_input,
    state_input,
    state_output,
    step_size,
    log_retention,
    skip_gain,
):
    exp_count = lax.axis_size("exp")
    exp_index = lax.axis_index("exp")
    expert_count = exp_count // 2
    token_rows = resid_input.shape[0]
    row_tokens = token_rows * exp_count
    capacity = 2 * row_tokens // expert_count
    model_width = resid_input.shape[1]
    token_count = mixer_input.shape[0]
    head_count = skip_gain.shape[0]
    head_size = mixer_input.shape[1] // head_count
    group_count = state_input.shape[1] // N
    head_groups = head_count // group_count
    input_states = state_input.reshape(token_count, group_count, N)
    output_states = state_output.reshape(token_count, group_count, N)
    input_float = input_states.astype(jnp.float32)
    output_float = output_states.astype(jnp.float32)
    inputs_float = mixer_input.astype(jnp.float32).reshape(token_count, head_count, head_size)
    cumulative, decay_matrix, intersection = mixer_setup(input_states, output_states, log_retention)
    grad_float = grad_output.astype(jnp.float32)
    all_grad = lax.all_gather(grad_output, "exp", axis=1, tiled=True)
    resid_float = resid_input.astype(jnp.float32)
    inverse_rms = lax.rsqrt(
        jnp.mean(resid_float * resid_float, axis=1, keepdims=True) + norm_epsilon
    )
    scaled_input = resid_float * inverse_rms
    normed_rows = (scaled_input * norm_gain[None, :]).astype(jnp.bfloat16)
    all_normed, all_probs = (
        lax.all_gather(normed_rows, "exp", axis=0, tiled=True),
        lax.all_gather(route_probs, "exp", axis=0, tiled=True),
    )
    all_ids = lax.all_gather(expert_ids, "exp", axis=0, tiled=True)
    flat_ids = all_ids.reshape(-1)
    own_expert = exp_index // 2
    selector = expert_slots(flat_ids, own_expert, capacity)
    token_selector = selector.reshape(capacity, row_tokens, 2).sum(axis=2)
    slot_normed = jnp.dot(token_selector, all_normed, preferred_element_type=jnp.float32).astype(
        jnp.bfloat16
    )
    slot_grad = jnp.dot(token_selector, all_grad, preferred_element_type=jnp.float32).astype(
        jnp.bfloat16
    )
    slot_prob = jnp.dot(selector, all_probs.reshape(-1), preferred_element_type=jnp.float32).astype(
        jnp.bfloat16
    )
    rows_normed, rows_grad, rows_prob = (
        lax.all_gather(slot_normed, "ctx", axis=0, tiled=True),
        lax.all_gather(slot_grad, "ctx", axis=0, tiled=True),
        lax.all_gather(slot_prob, "ctx", axis=0, tiled=True),
    )
    gate_rows = gate_weight[0]
    up_rows = up_weight[0]
    down_rows = down_weight[0]
    contract = (((1,), (1,)), ((), ()))
    gate_pre = lax.dot_general(rows_normed, gate_rows, contract, preferred_element_type=jnp.float32)
    up_pre = lax.dot_general(rows_normed, up_rows, contract, preferred_element_type=jnp.float32)
    hidden_grad = lax.dot_general(
        rows_grad, down_rows, contract, preferred_element_type=jnp.float32
    )
    hidden_grad = hidden_grad * rows_prob.astype(jnp.float32)[:, None]
    sigmoid_gate = jax.nn.sigmoid(gate_pre)
    gate_grad = (
        hidden_grad * up_pre * sigmoid_gate * (1.0 + gate_pre * (1.0 - sigmoid_gate))
    ).astype(jnp.bfloat16)
    up_grad = (hidden_grad * gate_pre * sigmoid_gate).astype(jnp.bfloat16)
    half_sum = lax.psum_scatter(
        (
            jnp.dot(gate_grad, gate_rows, preferred_element_type=jnp.float32)
            + jnp.dot(up_grad, up_rows, preferred_element_type=jnp.float32)
        ).astype(jnp.bfloat16),
        "ctx",
        scatter_dimension=0,
        tiled=True,
    ).astype(jnp.float32)
    all_tables = jax.vmap(partial(expert_slots, flat_ids, capacity=capacity))(
        jnp.arange(expert_count, dtype=jnp.int32)
    )
    token_tables = all_tables.reshape(expert_count, capacity, row_tokens, 2).sum(axis=3)
    own_tables = lax.dynamic_slice_in_dim(token_tables, exp_index * token_rows, token_rows, 2)
    parts = lax.all_gather(half_sum.astype(jnp.bfloat16), "exp", axis=0, tiled=True).astype(
        half_sum.dtype
    )
    owner_tables = jnp.repeat(own_tables, 2, axis=0).astype(jnp.float32)
    route_sum = jnp.einsum(
        "xct,xcd->td",
        owner_tables,
        parts.reshape(exp_count, capacity, model_width),
        precision=highest,
    )
    scaled_grad = route_sum * norm_gain[None, :]
    projection = jnp.mean(scaled_grad * scaled_input, axis=1, keepdims=True)
    moe_grad = (inverse_rms * (scaled_grad - scaled_input * projection)).astype(jnp.bfloat16)
    moe_heads = lax.all_to_all(moe_grad, "exp", split_axis=1, concat_axis=0, tiled=True)
    moe_float = moe_heads.astype(jnp.float32)
    upstream = grad_float + moe_float
    resid_grad = upstream.astype(jnp.bfloat16)
    upstream_heads = upstream.reshape(token_count, head_count, head_size)
    intra_x, intra_b, local_state = mixer_local(
        upstream_heads,
        inputs_float,
        step_size,
        output_float,
        cumulative,
        decay_matrix,
        intersection,
    )
    total_decay = jnp.exp(cumulative[-1])
    carried = carried_in(
        (total_decay, local_state),
        "ctx",
        chain_combine,
        (jnp.ones_like(total_decay), jnp.zeros_like(local_state)),
    )
    incoming = carried[1]
    tail_decay = jnp.exp(cumulative[-1][None, :] - cumulative)
    grouped_far = incoming.reshape(group_count, head_groups, N, head_size)
    far_x = jnp.einsum("tgn,gjnp->tgjp", input_float, grouped_far, precision=highest).reshape(
        token_count, head_count, head_size
    )
    far_x = far_x * tail_decay[:, :, None]
    mixer_grad = (
        step_size[:, :, None] * (intra_x + far_x) + skip_gain[None, :, None] * upstream_heads
    )
    mixer_grad = mixer_grad.astype(jnp.bfloat16).reshape(token_count, head_count * head_size)
    far_weight = (inputs_float * (step_size * tail_decay)[:, :, None]).reshape(
        token_count, group_count, head_groups, head_size
    )
    far_b = jnp.einsum("gjnp,tgjp->tgn", grouped_far, far_weight, precision=highest)
    state_input_grad = (intra_b + far_b).reshape(token_count, group_count * N)
    return (resid_grad, mixer_grad, state_input_grad)


def solution(mesh):
    in_specs = (
        P(("ctx", "exp"), None),
        P(),
        P(("ctx", "exp"), None),
        P(("ctx", "exp"), None),
        P("exp", "ctx", None),
        P("exp", "ctx", None),
        P("exp", "ctx", None),
        P("ctx", "exp"),
        P("ctx", "exp"),
        P("ctx", "exp"),
        P("ctx", "exp"),
        P("ctx", "exp"),
        P("ctx", "exp"),
        P("exp"),
    )
    out_specs = (P("ctx", "exp"), P("ctx", "exp"), P("ctx", "exp"))
    return jax.shard_map(body, mesh=mesh, in_specs=in_specs, out_specs=out_specs, check_vma=False)
```

profile of v0, /device:TPU:0, one launch (start us, length us, event | category | flops | bytes accessed | tf_op | source)
XLA Modules:
  0.0 321.4 jit_solution(16942792425635660093)
XLA Ops:
  7.2 1.1 fusion.52
  8.3 1.7 fusion.47
  10.8 10.6 %all-gather = s32[8,16,2]{1,2,0:T(2,128)S(1)} all-gather(s32[1,16,2]{1,2,0:T(2,128)} %bitcast.167), channel_id=1, replica_groups=mesh['ctx'=4,'exp'=8] {'exp'}, dimensions={0}, use_global_device_ids=true | all-gather | bytes 1152 | tf_op jit(solution)/shard_map/all_gather | solution.py:135
  22.7 13.9 %all-gather.13.cloned.1.call-done = bf16[128,4096]{1,0:T(8,128)(2,1)} async-done(((bf16[16,4096]{1,0:T(8,128)(2,1)}), bf16[128,4096]{1,0:T(8,128)(2,1)}) %all-gather.13.cloned.1.call-update) | async-done | bytes 1048592 | tf_op jit(solution)/shard_map/all_gather | solution.py:132
  36.6 2.3 convolution_convert_fusion
  39.0 23.0 %all-gather.9.cloned.1.call-done = bf16[128,4096]{1,0:T(8,128)(2,1)} async-done(((bf16[128,512]{1,0:T(8,128)(2,1)}), bf16[128,4096]{1,0:T(8,128)(2,1)}) %all-gather.9.cloned.1.call-update) | async-done | bytes 1048592 | tf_op jit(solution)/shard_map/all_gather | solution.py:124
  62.0 2.3 convolution_convert_fusion.1
  64.6 8.7 %all-gather.1 = bf16[8,16,2]{1,2,0:T(2,128)(2,1)S(1)} all-gather(bf16[1,16,2]{1,2,0:T(2,128)(2,1)S(1)} %bitcast.169), channel_id=1, replica_groups=mesh['ctx'=4,'exp'=8] {'exp'}, dimensions={0}, use_global_device_ids=true | all-gather | bytes 576 | tf_op jit(solution)/shard_map/all_gather | solution.py:133
  75.3 12.5 %all-reduce = bf16[256]{0:T(256)(128)(2,1)S(1)} all-reduce(bf16[256]{0:T(256)(128)(2,1)S(1)} %dynamic-update-slice), channel_id=1, replica_groups=mesh['ctx'=4,'exp'=8] {'ctx'}, use_global_device_ids=true, to_apply=%add | all-reduce | flops 256 | bytes 1024
  87.8 21.7 %all-gather.15.cloned.1.call-done = bf16[256,4096]{1,0:T(8,128)(2,1)} async-done(((bf16[64,4096]{1,0:T(8,128)(2,1)}), bf16[256,4096]{1,0:T(8,128)(2,1)}) %all-gather.15.cloned.1.call-update) | async-done | bytes 2097168 | tf_op jit(solution)/shard_map/all_gather | solution.py:150
  109.5 9.8 %fusion.2 = f32[256,1536]{1,0:T(8,128)} fusion(bf16[256,4096]{1,0:T(8,128)(2,1)} %all-gather.15.cloned.1.call-done, bf16[1,1536,4096]{2,1,0:T(8,128)(2,1)} %param.20), kind=kOutput, calls=%fused_computation.5 | convolution fusion | flops 3221225472 | bytes 16252928 | tf_op jit(solution)/shard_map/dot_general | solution.py:158
  119.3 36.1 %all-gather.11.cloned.1.call-done = bf16[256,4096]{1,0:T(8,128)(2,1)} async-done(((bf16[64,4096]{1,0:T(8,128)(2,1)}), bf16[256,4096]{1,0:T(8,128)(2,1)}) %all-gather.11.cloned.1.call-update) | async-done | bytes 2097168 | tf_op jit(solution)/shard_map/all_gather | solution.py:151
  155.4 9.9 %fusion.17 = f32[256,1536]{1,0:T(8,128)} fusion(bf16[256,4096]{1,0:T(8,128)(2,1)} %all-gather.11.cloned.1.call-done, bf16[1,1536,4096]{2,1,0:T(8,128)(2,1)} %param.22, f32[256]{0:T(256)S(1)} %convert_element_type.157), kind=kOutput, calls=%fused_computation.19 | convolution fusion | flops 3221618688 | bytes 16253952 | tf_op jit(solution)/shard_map/dot_general | solution.py:160
  165.3 16.3 %fusion = f32[256,4096]{1,0:T(8,128)} fusion(bf16[1,1536,4096]{2,1,0:T(8,128)(2,1)} %param.20, f32[256,1536]{1,0:T(8,128)} %fusion.17, bf16[256,4096]{1,0:T(8,128)(2,1)S(1)} %copy-done.10, bf16[1,1536,4096]{2,1,0:T(8,128)(2,1)} %param.21, f32[256,1536]{1,0:T(8,128)} %fusion.2), kind=kOutput, calls=%fused_computation.3 | convolution fusion | flops 6446383104 | bytes 34603008 | tf_op jit(solution)/shard_map/dot_general | solution.py:171
  181.6 11.5 %fusion.13 = bf16[256,4096]{1,0:T(8,128)(2,1)} fusion(f32[256,4096]{1,0:T(8,128)} %fusion, bf16[1,1536,4096]{2,1,0:T(8,128)(2,1)} %param.21, f32[256,1536]{1,0:T(8,128)} %fusion.17, f32[256,1536]{1,0:T(8,128)} %fusion.2), kind=kOutput, calls=%fused_computation.14 | convolution fusion | flops 3225681920 | bytes 22020096 | tf_op jit(solution)/shard_map/dot_general | solution.py:172
  193.2 42.6 %reduce-scatter.2.cloned.1.call-done = bf16[64,4096]{1,0:T(8,128)(2,1)} async-done(((bf16[256,4096]{1,0:T(8,128)(2,1)}), bf16[64,4096]{1,0:T(8,128)(2,1)}) %reduce-scatter.2.cloned.1.call-update) | async-done | bytes 524304 | tf_op jit(solution)/shard_map/reduce_scatter | solution.py:169
  235.8 1.2 reduce-window.15
  238.7 34.7 %all-gather.17.cloned.1.call-done = bf16[512,4096]{1,0:T(8,128)(2,1)} async-done(((bf16[64,4096]{1,0:T(8,128)(2,1)}), bf16[512,4096]{1,0:T(8,128)(2,1)}) %all-gather.17.cloned.1.call-update) | async-done | bytes 4194320 | tf_op jit(solution)/shard_map/all_gather | solution.py:183
  273.4 3.0 fusion.48
  277.3 3.4 %all-to-all-start = ((bf16[16,8,512]{2,0,1:T(8,128)(2,1)}), bf16[16,8,512]{2,0,1:T(8,128)(2,1)S(1)}, u32[]{:S(2)}, u32[]{:S(2)}) async-start(bf16[16,8,512]{2,0,1:T(8,128)(2,1)} %bitcast.136), calls=%async_computation.1 | async-start | bytes 262144 | tf_op jit(solution)/shard_map/all_to_all | solution.py:196
  280.8 10.9 %all-gather.2 = bf16[4,1,8]{2,1,0:T(2,128)(2,1)S(1)} all-gather(bf16[1,1,8]{2,1,0:T(2,128)(2,1)S(1)} %get-tuple-element.139), channel_id=1, replica_groups=mesh['ctx'=4,'exp'=8] {'ctx'}, dimensions={0}, use_global_device_ids=true | all-gather | bytes 80 | tf_op jit(solution)/shard_map/all_gather | solution.py:20
  293.2 14.9 %all_gather.40 = bf16[4,8,128,64]{2,3,1,0:T(8,128)(2,1)S(1)} all-gather(bf16[1,8,128,64]{2,3,1,0:T(8,128)(2,1)S(1)} %bitcast.153), channel_id=1, replica_groups=mesh['ctx'=4,'exp'=8] {'ctx'}, dimensions={0}, use_global_device_ids=true | all-gather | bytes 655360 | tf_op jit(solution)/shard_map/all_gather | solution.py:20
  308.2 1.2 while.14
  312.4 1.2 fusion.38
  (133 shorter events, 12.8 us)
Async XLA Ops:
  7.2 29.4 %all-gather.13.cloned.1.call-start = ((), (), s32[]{:S(2)}) async-start(), calls=%async_computation.4 | async-start | bytes 1179648 | tf_op jit(solution)/shard_map/all_gather | solution.py:132
  10.0 52.0 %all-gather.9.cloned.1.call-start = ((), (), s32[]{:S(2)}) async-start(), calls=%async_computation.2 | async-start | bytes 1179648 | tf_op jit(solution)/shard_map/all_gather | solution.py:124
  10.7 98.8 %all-gather.15.cloned.1.call-start = ((), (), s32[]{:S(2)}) async-start(), calls=%async_computation.5 | async-start | bytes 2621440 | tf_op jit(solution)/shard_map/all_gather | solution.py:150
  22.6 42.0 %copy-start.8 = (bf16[16,2]{0,1:T(2,128)(2,1)S(1)}, bf16[16,2]{0,1:T(2,128)(2,1)}, u32[]{:S(2)}) copy-start(bf16[16,2]{0,1:T(2,128)(2,1)} %param.19) | copy-start | bytes 196
  22.7 51.0 %copy-start.11 = (u32[32]{0:T(128)S(1)}, u32[32]{0:T(128)}, u32[]{:S(2)}) copy-start(u32[32]{0:T(128)} %constant.95) | copy-start | bytes 388
  38.9 116.5 %all-gather.11.cloned.1.call-start = ((), (), s32[]{:S(2)}) async-start(), calls=%async_computation.3 | async-start | bytes 2621440 | tf_op jit(solution)/shard_map/all_gather | solution.py:151
  64.3 171.5 %reduce-scatter.2.cloned.1.call-start = ((), (), s32[]{:S(2)}) async-start(), calls=%async_computation.6 | async-start | bytes 2621440 | tf_op jit(solution)/shard_map/reduce_scatter | solution.py:169
  119.3 46.0 %copy-start.10 = (bf16[256,4096]{1,0:T(8,128)(2,1)S(1)}, bf16[256,4096]{1,0:T(8,128)(2,1)}, u32[]{:S(2)}) copy-start(bf16[256,4096]{1,0:T(8,128)(2,1)} %all-gather.15.cloned.1.call-done) | copy-start | bytes 6291460
  193.2 44.9 %copy-start.7 = (f32[128,8]{0,1:T(8,128)S(1)}, f32[128,8]{0,1:T(8,128)}, u32[]{:S(2)}) copy-start(f32[128,8]{0,1:T(8,128)} %param.28) | copy-start | bytes 12292
  193.2 45.0 %copy-start.6 = (f32[128,8]{0,1:T(8,128)S(1)}, f32[128,8]{0,1:T(8,128)}, u32[]{:S(2)}) copy-start(f32[128,8]{0,1:T(8,128)} %param.27) | copy-start | bytes 12292
  193.2 45.1 %copy-start.5 = (bf16[128,256]{1,0:T(8,128)(2,1)S(1)}, bf16[128,256]{1,0:T(8,128)(2,1)}, u32[]{:S(2)}) copy-start(bf16[128,256]{1,0:T(8,128)(2,1)} %param.26) | copy-start | bytes 196612
  193.2 80.2 %copy-start = (bf16[16,4096]{1,0:T(8,128)(2,1)S(1)}, bf16[16,4096]{1,0:T(8,128)(2,1)}, u32[]{:S(2)}) copy-start(bf16[16,4096]{1,0:T(8,128)(2,1)} %param.16) | copy-start | bytes 393220
  193.2 80.2 %copy-start.4 = (f32[4096]{0:T(1024)S(1)}, f32[4096]{0:T(1024)}, u32[]{:S(2)}) copy-start(f32[4096]{0:T(1024)} %param.17) | copy-start | bytes 49156
  193.2 80.2 %all-gather.17.cloned.1.call-start = ((), (), s32[]{:S(2)}) async-start(), calls=%async_computation.7 | async-start | bytes 4718592 | tf_op jit(solution)/shard_map/all_gather | solution.py:183
  273.4 7.3 %copy-start.2 = (bf16[128,256]{1,0:T(8,128)(2,1)S(1)}, bf16[128,256]{1,0:T(8,128)(2,1)}, u32[]{:S(2)}) copy-start(bf16[128,256]{1,0:T(8,128)(2,1)} %param.25) | copy-start | bytes 196612
  273.4 18.4 %copy-start.3 = (bf16[128,512]{1,0:T(8,128)(2,1)S(1)}, bf16[128,512]{1,0:T(8,128)(2,1)}, u32[]{:S(2)}) copy-start(bf16[128,512]{1,0:T(8,128)(2,1)} %param.24) | copy-start | bytes 393220
  276.4 16.2 %copy-start.9 = (f32[8]{0:T(128)S(1)}, f32[8]{0:T(128)}, u32[]{:S(2)}) copy-start(f32[8]{0:T(128)} %param.29) | copy-start | bytes 100
  276.4 16.3 %copy-start.1 = (bf16[128,512]{1,0:T(8,128)(2,1)S(1)}, bf16[128,512]{1,0:T(8,128)(2,1)}, u32[]{:S(2)}) copy-start(bf16[128,512]{1,0:T(8,128)(2,1)} %param.23) | copy-start | bytes 393220
  277.3 15.5 %all-to-all-start = ((bf16[16,8,512]{2,0,1:T(8,128)(2,1)}), bf16[16,8,512]{2,0,1:T(8,128)(2,1)S(1)}, u32[]{:S(2)}, u32[]{:S(2)}) async-start(bf16[16,8,512]{2,0,1:T(8,128)(2,1)} %bitcast.136), calls=%async_computation.1 | async-start | bytes 262144 | tf_op jit(solution)/shard_map/all_to_all | solution.py:196
Sparse Core Ops, SparseCore 0:
  10.4 26.1 all-gather.12
  38.5 23.4 all-gather.8
  63.5 45.9 all-gather.14
  110.9 44.4 all-gather.10
  193.3 42.4 reduce-scatter.1
  237.6 35.7 all-gather.16
where the time goes:
time: 322 us; the launch traced here: 321 us
  waiting for transfers between devices  173 us (54%)
  matrix products  59 us (18%)
  blocking collectives  57.6 us (18%)
  between operations  15.2 us (5%)
  local copies, waits for them, and re-layouts  6.84 us (2%)
  other arithmetic  6.27 us (2%)
  starting transfers between devices  3.62 us (1%)
    reduce_scatter x1, waiting for transfers between devices, body(): lax.psum_scatter((jnp.dot(gate_grad, gate_rows, preferred_element_type=jn...  42.6 us
    all_gather x1, waiting for transfers between devices, body(): lax.all_gather(slot_grad, 'ctx', axis=0, tiled=True)  36.1 us
    all_gather x1, waiting for transfers between devices, body(): lax.all_gather(half_sum.astype(jnp.bfloat16), 'exp', axis=0, tiled=True)  34.7 us
    all_gather x2, blocking collectives, carried_in(): lax.all_gather(a.astype(kind), axis)  25.8 us
    all_gather x1, waiting for transfers between devices, body(): all_grad = lax.all_gather(grad_output, 'exp', axis=1, tiled=True)  23 us
    all_gather x1, waiting for transfers between devices, body(): lax.all_gather(slot_normed, 'ctx', axis=0, tiled=True)  21.7 us
    dot_general x1, matrix products, body(): jnp.dot(gate_grad, gate_rows, preferred_element_type=jnp.float32)  16.3 us
    all_gather x1, waiting for transfers between devices, body(): lax.all_gather(normed_rows, 'exp', axis=0, tiled=True)  13.9 us
  transfers between devices with their start and end apart: 7, of which 6 were waited for; matrix products, arithmetic and copies ran while one was open for 7% of the time, Pallas kernels for 0%

commit v1 on v0

v1 whole, which is shorter than its diff:
```python
from functools import partial

import jax
import jax.numpy as jnp
from jax import lax
from jax.experimental import pallas as pl
from jax.experimental.pallas import tpu as pltpu
from jax.sharding import PartitionSpec as P

N = 128
LANES = 128
norm_epsilon = 1e-05
f32 = jnp.float32
bf16 = jnp.bfloat16
highest = lax.Precision.HIGHEST
vmem_bytes = 56 * 1024 * 1024


def params(steps=0):
    return pltpu.CompilerParams(
        dimension_semantics=("arbitrary",) * steps, vmem_limit_bytes=vmem_bytes
    )


def whole(shape):
    return pl.BlockSpec(shape, lambda *_: (0,) * len(shape))


def iota(shape, dim):
    return lax.broadcasted_iota(jnp.int32, shape, dim)


def dot(a, b, ca, cb, precision=None):
    return lax.dot_general(
        a, b, (((ca,), (cb,)), ((), ())), precision=precision, preferred_element_type=f32
    )


def dispatch_kernel(packed, grad, table, probs, rows_x, rows_g, *, experts, capacity):
    tokens, width = grad.shape
    meta = packed[:, width:].astype(f32)
    lane = iota((tokens, LANES), 1).astype(f32)
    first = meta[:, 0:1] == lane
    second = meta[:, 1:2] == lane
    member = jnp.where(first | second, 1.0, 0.0).astype(bf16)
    weight = (jnp.where(first, meta[:, 2:3], 0.0) + jnp.where(second, meta[:, 3:4], 0.0)).astype(bf16)
    row = iota((tokens, tokens), 0)
    col = iota((tokens, tokens), 1)
    before = jnp.where(row < col, 1.0, 0.0).astype(bf16)
    same = jnp.where(row == col, 1.0, 0.0).astype(bf16)
    position = dot(member, before, 0, 0)
    member_t = dot(member, same, 0, 0)
    weight_t = dot(weight, same, 0, 0)
    slot = iota((capacity, tokens), 0).astype(f32)
    for e in range(experts):
        hit = (slot == position[e : e + 1, :]) & (member_t[e : e + 1, :] > 0.5)
        entry = jnp.where(hit, 1.0, 0.0)
        table[e * capacity : (e + 1) * capacity, :] = entry.astype(bf16)
        share = jnp.sum(entry * weight_t[e : e + 1, :], axis=1, keepdims=True)
        probs[e * capacity : (e + 1) * capacity, :] = jnp.broadcast_to(share, (capacity, LANES))
    sel = table[...]
    out_x = dot(sel, packed[:, :width], 1, 0).astype(bf16)
    out_g = dot(sel, grad[...], 1, 0).astype(bf16)
    for c in range(rows_x.shape[0]):
        rows_x[c] = out_x
        rows_g[c] = out_g


def gate_up_kernel(own, other, gain, gate_w, up_w, coef_gate, coef_up, normed):
    ctx, peers, slots, width = own.shape
    half = ctx * slots
    model = peers * width

    @pl.when(pl.program_id(0) == 0)
    def _():
        for side, ref in enumerate((own, other)):
            total = jnp.zeros((half, 1), f32)
            for j in range(peers):
                x = ref[:, j].reshape(half, width).astype(f32)
                total = total + jnp.sum(x * x, axis=1, keepdims=True)
            inverse = lax.rsqrt(total * (1.0 / model) + norm_epsilon)
            for j in range(peers):
                x = ref[:, j].reshape(half, width).astype(f32)
                cols = slice(j * width, (j + 1) * width)
                normed[side * half : (side + 1) * half, cols] = (x * inverse * gain[:, cols]).astype(bf16)

    rows = normed[...]
    gate = dot(rows, gate_w[0], 1, 1)
    up = dot(rows, up_w[0], 1, 1)
    sig = jax.nn.sigmoid(gate)
    coef_gate[...] = up * sig * (1.0 + gate * (1.0 - sig))
    coef_up[...] = gate * sig


def hidden_kernel(own, other, coef_gate, coef_up, down_w, gate_grad, up_grad, grads):
    ctx, peers, slots, width = own.shape
    half = ctx * slots

    @pl.when(pl.program_id(0) == 0)
    def _():
        for side, ref in enumerate((own, other)):
            for j in range(peers):
                cols = slice(j * width, (j + 1) * width)
                grads[side * half : (side + 1) * half, cols] = ref[:, j].reshape(half, width)

    hidden = dot(grads[...], down_w[0], 1, 1)
    gate_grad[...] = (hidden * coef_gate[...]).astype(bf16)
    up_grad[...] = (hidden * coef_up[...]).astype(bf16)


def output_kernel(gate_grad, up_grad, gate_w, up_w, out):
    out[...] = (
        dot(gate_grad[...], gate_w[0], 1, 0) + dot(up_grad[...], up_w[0], 1, 0)
    ).astype(bf16)


def slot_kernel(place, parts, probs, gain, x_rows, out):
    ctx, slots, model = parts.shape
    peers, width = x_rows.shape[1], x_rows.shape[3]
    prob = probs[:, 0:1]
    squares = jnp.zeros((slots, 1), f32)
    product = jnp.zeros((slots, 1), f32)
    for j in range(peers):
        cols = slice(j * width, (j + 1) * width)
        total = parts[0, :, cols].astype(f32)
        for c in range(1, ctx):
            total = total + parts[c, :, cols].astype(f32)
        x = x_rows[0, j].astype(f32)
        squares = squares + jnp.sum(x * x, axis=1, keepdims=True)
        product = product + jnp.sum(total * gain[:, cols] * x, axis=1, keepdims=True)
    inverse = lax.rsqrt(squares * (1.0 / model) + norm_epsilon)
    scale = prob * inverse
    shift = scale * product * inverse * inverse * (1.0 / model)
    for j in range(peers):
        cols = slice(j * width, (j + 1) * width)
        total = parts[0, :, cols].astype(f32)
        for c in range(1, ctx):
            total = total + parts[c, :, cols].astype(f32)
        x = x_rows[0, j].astype(f32)
        out[j] = (total * gain[:, cols] * scale - x * shift).astype(bf16)


def mixer_setup_kernel(
    log_ret, step, state_in, state_out, mix, weigh, step_l, tail_l, head_l, total_l, *, groups
):
    tokens, heads = log_ret.shape
    width = step_l.shape[1]
    size = width // heads
    row = iota((tokens, tokens), 0)
    col = iota((tokens, tokens), 1)
    upto = jnp.where(row <= col, 1.0, 0.0)
    logs = log_ret[...]
    cum_t = dot(logs, upto, 0, 0, highest)
    cum = dot(upto, logs, 0, 0, highest)
    last = cum[tokens - 1 : tokens, :]
    spread = jnp.where(iota((heads, width), 0) == iota((heads, width), 1) // size, 1.0, 0.0)
    steps = step[...]
    step_l[...] = dot(steps, spread, 1, 0, highest)
    tail_l[...] = dot(steps * jnp.exp(last - cum), spread, 1, 0, highest)
    head_l[...] = dot(jnp.exp(cum), spread, 1, 0, highest)
    total_l[...] = dot(jnp.broadcast_to(last, (8, heads)), spread, 1, 0, highest)
    later = col >= row
    for g in range(groups):
        cols = slice(g * N, (g + 1) * N)
        inter = dot(state_in[:, cols], state_out[:, cols], 1, 1)
        for h in range(g * heads // groups, (g + 1) * heads // groups):
            gap = cum_t[h : h + 1, :] - cum[:, h : h + 1]
            decay = jnp.where(later, jnp.exp(jnp.where(later, gap, 0.0)), 0.0)
            mix[h] = decay * inter
            weigh[h] = decay * steps[:, h : h + 1]


def mixer_local_kernel(
    moved, table, grad, mixer, state_out, mix, weigh, step_l, head_l, skip, resid_grad, base, local_b, state
):
    tokens, width = grad.shape
    heads = mix.shape[0]
    size = width // heads
    groups = state_out.shape[1] // N
    moe = dot(table[...], moved[...], 0, 0).astype(bf16)
    upstream = grad[...].astype(f32) + moe.astype(f32)
    resid_grad[...] = upstream.astype(bf16)
    span = width // groups
    for g in range(groups):
        cols = slice(g * N, (g + 1) * N)
        wide = slice(g * span, (g + 1) * span)
        scaled = upstream[:, wide] * head_l[:, wide]
        state[:, wide] = dot(state_out[:, cols].astype(f32), scaled, 0, 0, highest).astype(bf16)
        weighted = jnp.zeros((tokens, tokens), f32)
        for h in range(g * heads // groups, (g + 1) * heads // groups):
            part = slice(h * size, (h + 1) * size)
            up_h = upstream[:, part]
            mixed = dot(mix[h], up_h, 1, 0, highest)
            base[:, part] = step_l[:, part] * mixed + skip[:, part] * up_h
            inner = dot(mixer[:, part].astype(f32), up_h, 1, 1, highest)
            weighted = weighted + weigh[h] * inner
        local_b[:, cols] = dot(weighted, state_out[:, cols].astype(f32), 1, 0, highest)


def mixer_far_kernel(place, states, totals, base, local_b, mixer, state_in, tail_l, mixer_grad, input_grad):
    ctx = states.shape[0]
    groups = state_in.shape[1] // N
    width = base.shape[1]
    span = width // groups
    here = place[0]
    incoming = jnp.zeros(states.shape[1:], f32)
    for c in range(ctx - 1, 0, -1):
        joined = states[c].astype(f32) + jnp.exp(totals[c, 0:1, :]) * incoming
        incoming = jnp.where(here < c, joined, incoming)
    for g in range(groups):
        cols = slice(g * N, (g + 1) * N)
        wide = slice(g * span, (g + 1) * span)
        far = dot(state_in[:, cols].astype(f32), incoming[:, wide], 1, 0, highest)
        mixer_grad[:, wide] = (base[:, wide] + tail_l[:, wide] * far).astype(bf16)
        scaled = mixer[:, wide].astype(f32) * tail_l[:, wide]
        input_grad[:, cols] = local_b[:, cols] + dot(scaled, incoming[:, wide], 1, 1, highest)


def block_of(total, most):
    size = min(total, most)
    while total % size:
        size -= LANES if size > LANES else 1
    return size


def body(
    resid_input,
    norm_gain,
    expert_ids,
    route_probs,
    gate_weight,
    up_weight,
    down_weight,
    grad_output,
    mixer_input,
    state_input,
    state_output,
    step_size,
    log_retention,
    skip_gain,
):
    ctx = lax.axis_size("ctx")
    peers = lax.axis_size("exp")
    place = jnp.stack([lax.axis_index("ctx"), lax.axis_index("exp")]).astype(jnp.int32)
    experts = peers // 2
    token_rows, model = resid_input.shape
    tokens, width = grad_output.shape
    capacity = 2 * tokens // experts
    slots = capacity // 2
    heads = skip_gain.shape[0]
    groups = state_input.shape[1] // N
    hidden = gate_weight.shape[1]
    gain = norm_gain.reshape(1, model)
    skip = jnp.repeat(skip_gain, width // heads).reshape(1, width)
    partner = [(i, i ^ 1) for i in range(peers)]
    shape = jax.ShapeDtypeStruct

    meta = jnp.concatenate(
        [expert_ids.astype(bf16), route_probs, jnp.zeros((token_rows, LANES - 4), bf16)], axis=1
    )
    packed = jnp.concatenate(
        [
            resid_input.reshape(token_rows, peers, width),
            jnp.broadcast_to(meta[:, None, :], (token_rows, peers, LANES)),
        ],
        axis=2,
    ).reshape(token_rows, peers * (width + LANES))
    packed = lax.all_to_all(packed, "exp", split_axis=1, concat_axis=0, tiled=True)

    mix, weigh, step_l, tail_l, head_l, total_l = pl.pallas_call(
        partial(mixer_setup_kernel, groups=groups),
        out_shape=(
            shape((heads, tokens, tokens), f32),
            shape((heads, tokens, tokens), f32),
            shape((tokens, width), f32),
            shape((tokens, width), f32),
            shape((tokens, width), f32),
            shape((8, width), f32),
        ),
        compiler_params=params(),
    )(log_retention, step_size, state_input, state_output)
    totals = lax.all_to_all(
        jnp.broadcast_to(total_l[None], (ctx, 8, width)), "ctx", split_axis=0, concat_axis=0, tiled=True
    )

    table, probs, rows_x, rows_g = pl.pallas_call(
        partial(dispatch_kernel, experts=experts, capacity=capacity),
        out_shape=(
            shape((experts * capacity, tokens), bf16),
            shape((experts * capacity, LANES), f32),
            shape((ctx, experts * capacity, width), bf16),
            shape((ctx, experts * capacity, width), bf16),
        ),
        compiler_params=params(),
    )(packed, grad_output)

    def spread(rows):
        got = lax.all_to_all(
            rows.reshape(ctx * peers, slots, width), ("ctx", "exp"), split_axis=0, concat_axis=0, tiled=True
        ).reshape(ctx, peers, slots, width)
        return got, lax.ppermute(got, "exp", partner)

    own_x, other_x = spread(rows_x)
    own_g, other_g = spread(rows_g)
    rows = 2 * ctx * slots
    slab = (ctx, peers, slots, width)
    block = block_of(hidden, 256)
    steps = hidden // block
    weight_spec = pl.BlockSpec((1, block, model), lambda i: (0, i, 0))
    act_spec = pl.BlockSpec((rows, block), lambda i: (0, i))
    coef_gate, coef_up = pl.pallas_call(
        gate_up_kernel,
        grid=(steps,),
        in_specs=[whole(slab), whole(slab), whole((1, model)), weight_spec, weight_spec],
        out_specs=[act_spec, act_spec],
        out_shape=(shape((rows, hidden), f32), shape((rows, hidden), f32)),
        scratch_shapes=[pltpu.VMEM((rows, model), bf16)],
        compiler_params=params(1),
    )(own_x, other_x, gain, gate_weight, up_weight)
    gate_grad, up_grad = pl.pallas_call(
        hidden_kernel,
        grid=(steps,),
        in_specs=[whole(slab), whole(slab), act_spec, act_spec, weight_spec],
        out_specs=[act_spec, act_spec],
        out_shape=(shape((rows, hidden), bf16), shape((rows, hidden), bf16)),
        scratch_shapes=[pltpu.VMEM((rows, model), bf16)],
        compiler_params=params(1),
    )(own_g, other_g, coef_gate, coef_up, down_weight)
    column = block_of(model, 512)
    col_spec = pl.BlockSpec((1, hidden, column), lambda i: (0, 0, i))
    block_grad = pl.pallas_call(
        output_kernel,
        grid=(model // column,),
        in_specs=[whole((rows, hidden)), whole((rows, hidden)), col_spec, col_spec],
        out_specs=pl.BlockSpec((rows, column), lambda i: (0, i)),
        out_shape=shape((rows, model), bf16),
        compiler_params=params(1),
    )(gate_grad, up_grad, gate_weight, up_weight)

    half = rows // 2
    swapped = lax.ppermute(block_grad[half:], "exp", partner)
    summed = (block_grad[:half].astype(f32) + swapped.astype(f32)).astype(bf16)
    parts = lax.all_to_all(
        summed.reshape(ctx, slots, model), "ctx", split_axis=0, concat_axis=0, tiled=True
    )
    moved = pl.pallas_call(
        slot_kernel,
        grid_spec=pltpu.PrefetchScalarGridSpec(
            num_scalar_prefetch=1,
            grid=(1,),
            in_specs=[
                whole((ctx, slots, model)),
                pl.BlockSpec((slots, LANES), lambda i, at: (at[1], 0)),
                whole((1, model)),
                pl.BlockSpec((1, peers, slots, width), lambda i, at: (at[0], 0, 0, 0)),
            ],
            out_specs=whole((peers, slots, width)),
        ),
        out_shape=shape((peers, slots, width), bf16),
        compiler_params=params(1),
    )(place, parts, probs, gain, own_x)
    moved = lax.all_to_all(moved, "exp", split_axis=0, concat_axis=0, tiled=True).reshape(
        experts * capacity, width
    )

    resid_grad, base, local_b, state = pl.pallas_call(
        mixer_local_kernel,
        out_shape=(
            shape((tokens, width), bf16),
            shape((tokens, width), f32),
            shape((tokens, groups * N), f32),
            shape((N, width), bf16),
        ),
        compiler_params=params(),
    )(moved, table, grad_output, mixer_input, state_output, mix, weigh, step_l, head_l, skip)
    states = lax.all_to_all(
        jnp.broadcast_to(state[None], (ctx, N, width)), "ctx", split_axis=0, concat_axis=0, tiled=True
    )
    mixer_grad, state_input_grad = pl.pallas_call(
        mixer_far_kernel,
        grid_spec=pltpu.PrefetchScalarGridSpec(
            num_scalar_prefetch=1,
            grid=(1,),
            in_specs=[
                whole((ctx, N, width)),
                whole((ctx, 8, width)),
                whole((tokens, width)),
                whole((tokens, groups * N)),
                whole((tokens, width)),
                whole((tokens, groups * N)),
                whole((tokens, width)),
            ],
            out_specs=[whole((tokens, width)), whole((tokens, groups * N))],
        ),
        out_shape=(shape((tokens, width), bf16), shape((tokens, groups * N), f32)),
        compiler_params=params(1),
    )(place, states, totals, base, local_b, mixer_input, state_input, tail_l)
    return (resid_grad, mixer_grad, state_input_grad)


def solution(mesh):
    in_specs = (
        P(("ctx", "exp"), None),
        P(),
        P(("ctx", "exp"), None),
        P(("ctx", "exp"), None),
        P("exp", "ctx", None),
        P("exp", "ctx", None),
        P("exp", "ctx", None),
        P("ctx", "exp"),
        P("ctx", "exp"),
        P("ctx", "exp"),
        P("ctx", "exp"),
        P("ctx", "exp"),
        P("ctx", "exp"),
        P("exp"),
    )
    out_specs = (P("ctx", "exp"), P("ctx", "exp"), P("ctx", "exp"))
    return jax.shard_map(body, mesh=mesh, in_specs=in_specs, out_specs=out_specs, check_vma=False)
```

time: 322 us -> 204 us (0.63)
  waiting for transfers between devices: 173 us -> 57 us
  matrix products: 59 us -> 0 us
  Pallas kernels: 0 us -> 57.3 us
  between operations: 15.2 us -> 0.76 us
  starting transfers between devices: 3.62 us -> 15.1 us
  local copies, waits for them, and re-layouts: 6.84 us -> 10.8 us
  other arithmetic: 6.27 us -> 2.64 us
    all_gather x5 -> x0, waiting for transfers between devices: 129 us -> none  [the longest x1 36.1 us: body(): lax.all_gather(slot_grad, 'ctx', axis=0, tiled=True)]
    all_to_all x0 -> x3, blocking collectives: none -> 59.5 us  [the longest x1 30.2 us: spread(): lax.all_to_all(rows.reshape(ctx * peers, slots, width), ('ctx', 'exp'), s...]
    dot_general x15 -> x0, matrix products: 59 us -> none  [the longest x1 16.3 us: body(): jnp.dot(gate_grad, gate_rows, preferred_element_type=jnp.float32)]
    pallas_call x0 -> x8, Pallas kernels: none -> 57.3 us  [the longest x1 15.2 us: body(): pl.pallas_call(gate_up_kernel, grid=(steps,), in_specs=[whole(slab), whol...]
    all_to_all x1 -> x4, waiting for transfers between devices: 0.01 us -> 54.7 us  [the longest x1 25.9 us: body(): lax.all_to_all(summed.reshape(ctx, slots, model), 'ctx', split_axis=0, co...]
    all_gather x4 -> x0, blocking collectives: 45.1 us -> none  [the longest x2 25.8 us: carried_in(): lax.all_gather(a.astype(kind), axis)]
    reduce_scatter x1 -> x0, waiting for transfers between devices: 42.6 us -> none  [body(): lax.psum_scatter((jnp.dot(gate_grad, gate_rows, preferred_element_type=jn...]
    unnamed x1 -> x0, blocking collectives: 12.5 us -> none
  transfers between devices with their start and end apart: 7 -> 7, of which waited for: 6 -> 5; matrix products, arithmetic and copies ran while one was open for 7% -> 1% of each run, Pallas kernels for 0% -> 11%
where the time goes in v1:
time: 204 us; the launch traced here: 203 us
  blocking collectives  59.5 us (29%)
  Pallas kernels  57.3 us (28%)
  waiting for transfers between devices  57 us (28%)
  starting transfers between devices  15.1 us (7%)
  local copies, waits for them, and re-layouts  10.8 us (5%)
  other arithmetic  2.64 us (1%)
    all_to_all x1, blocking collectives, spread(): lax.all_to_all(rows.reshape(ctx * peers, slots, width), ('ctx', 'exp'), s...  30.2 us
    all_to_all x1, waiting for transfers between devices, body(): lax.all_to_all(summed.reshape(ctx, slots, model), 'ctx', split_axis=0, co...  25.9 us
    all_to_all x1, waiting for transfers between devices, spread(): lax.all_to_all(rows.reshape(ctx * peers, slots, width), ('ctx', 'exp'), s...  25.9 us
    all_to_all x1, blocking collectives, body(): lax.all_to_all(jnp.broadcast_to(state[None], (ctx, N, width)), 'ctx', spl...  18.4 us
    pallas_call x1, Pallas kernels, body(): pl.pallas_call(gate_up_kernel, grid=(steps,), in_specs=[whole(slab), whol...  15.2 us
    pallas_call x1, Pallas kernels, body(): pl.pallas_call(output_kernel, grid=(model // column,), in_specs=[whole((r...  14.7 us
    all_to_all x1, blocking collectives, body(): lax.all_to_all(packed, 'exp', split_axis=1, concat_axis=0, tiled=True)  11 us
    pallas_call x1, Pallas kernels, body(): pl.pallas_call(hidden_kernel, grid=(steps,), in_specs=[whole(slab), whole...  10.6 us
  transfers between devices with their start and end apart: 7, of which 5 were waited for; matrix products, arithmetic and copies ran while one was open for 1% of the time, Pallas kernels for 11%

profile of v1, /device:TPU:0, one launch (start us, length us, event | category | flops | bytes accessed | tf_op | source)
XLA Modules:
  0.0 203.1 jit_solution(14930952200712398362)
XLA Ops:
  3.3 11.0 %all_to_all.46 = bf16[16,8,640]{2,0,1:T(8,128)(2,1)} all-to-all(bf16[16,8,640]{2,0,1:T(8,128)(2,1)S(1)} %pad_maximum_fusion), channel_id=1, replica_groups=mesh['ctx'=4,'exp'=8] {'exp'}, dimensions={1} | all-to-all | bytes 327680 | tf_op jit(solution)/shard_map/all_to_all | solution.py:268
  14.2 2.9 %shard_map.157 = (bf16[256,128]{1,0:T(8,128)(2,1)}, f32[256,128]{1,0:T(8,128)}, bf16[4,256,512]{2,1,0:T(8,128)(2,1)}, bf16[4,256,512]{2,1,0:T(8,128)(2,1)}) custom-call(bf16[128,640]{1,0:T(8,128)(2,1)} %bitcast.23, bf16[128,512]{1,0:T(8,128)(2,1)} %grad.3), custom_call_target="tpu_custom_call" | custom-call | tf_op jit(solution)/shard_map/pallas_call | solution.py:286
  17.1 30.2 %all_to_all.47 = bf16[32,32,512]{2,1,0:T(8,128)(2,1)S(1)} all-to-all(bf16[32,32,512]{2,1,0:T(8,128)(2,1)} %bitcast.22), channel_id=1, replica_groups=mesh['ctx'=4,'exp'=8] {'ctx','exp'}, dimensions={0} | all-to-all | bytes 2097152 | tf_op jit(solution)/shard_map/all_to_all | solution.py:298
  47.3 3.6 %all-to-all-start.1 = ((bf16[32,32,512]{2,1,0:T(8,128)(2,1)}), bf16[32,32,512]{2,1,0:T(8,128)(2,1)S(1)}, u32[]{:S(2)}, u32[]{:S(2)}) async-start(bf16[32,32,512]{2,1,0:T(8,128)(2,1)} %bitcast.4), calls=%async_computation.1 | async-start | bytes 2097152 | tf_op jit(solution)/shard_map/all_to_all | solution.py:298
  51.2 25.9 %all-to-all-done.1 = bf16[32,32,512]{2,1,0:T(8,128)(2,1)S(1)} async-done(((bf16[32,32,512]{2,1,0:T(8,128)(2,1)}), bf16[32,32,512]{2,1,0:T(8,128)(2,1)S(1)}, u32[]{:S(2)}, u32[]{:S(2)}) %all-to-all-start.1) | async-done | bytes 1048608 | tf_op jit(solution)/shard_map/all_to_all | solution.py:298
  77.1 1.0 copy-done.4
  78.1 15.2 %shard_map.158 = (f32[256,1536]{1,0:T(8,128)}, f32[256,1536]{1,0:T(8,128)}) custom-call(bf16[4,8,32,512]{3,2,1,0:T(8,128)(2,1)} %bitcast.17, bf16[4,8,32,512]{3,2,1,0:T(8,128)(2,1)} %copy-done.4, f32[1,4096]{1,0:T(1,128)} %bitcast.26, bf16[1,1536,4096]{2,1,0:T(8,128)(2,1)} %gate_w.3, bf16[1,1536,4096]{2,1,0:T(8,128)(2,1)} %up_w.3), custom_call_target="tpu_custom_call" | custom-call | tf_op jit(solution)/shard_map/pallas_call | solution.py:311
  94.4 10.6 %shard_map.159 = (bf16[256,1536]{1,0:T(8,128)(2,1)}, bf16[256,1536]{1,0:T(8,128)(2,1)}) custom-call(bf16[4,8,32,512]{3,2,1,0:T(8,128)(2,1)} %bitcast.20, bf16[4,8,32,512]{3,2,1,0:T(8,128)(2,1)} %copy-done.5, f32[256,1536]{1,0:T(8,128)} %get-tuple-element.25.coef_gate, f32[256,1536]{1,0:T(8,128)} %get-tuple-element.26.coef_up, bf16[1,1536,4096]{2,1,0:T(8,128)(2,1)} %down_w.1), custom_call_target="tpu_custom_call" | custom-call | tf_op jit(solution)/shard_map/pallas_call | solution.py:320
  105.0 14.7 %shard_map.160 = bf16[256,4096]{1,0:T(8,128)(2,1)} custom-call(bf16[256,1536]{1,0:T(8,128)(2,1)} %get-tuple-element.27.gate_grad, bf16[256,1536]{1,0:T(8,128)(2,1)} %get-tuple-element.28.up_grad, bf16[1,1536,4096]{2,1,0:T(8,128)(2,1)} %gate_w.3, bf16[1,1536,4096]{2,1,0:T(8,128)(2,1)} %up_w.3), custom_call_target="tpu_custom_call" | custom-call | tf_op jit(solution)/shard_map/pallas_call | solution.py:331
  119.6 1.4 slice.9
  121.6 2.3 %collective-permute-done.2 = bf16[128,4096]{1,0:T(8,128)(2,1)S(1)} collective-permute-done((bf16[128,4096]{1,0:T(8,128)(2,1)S(1)}, bf16[128,4096]{1,0:T(8,128)(2,1)S(1)}, u32[]{:S(2)}, u32[]{:S(2)}) %collective-permute-start.2) | collective-permute-done | bytes 1048608 | tf_op jit(solution)/shard_map/ppermute | solution.py:341
  123.9 1.3 add_convert_fusion
  125.2 3.6 %all-to-all-start.3 = ((bf16[4,32,4096]{2,1,0:T(8,128)(2,1)}), bf16[4,32,4096]{2,1,0:T(8,128)(2,1)S(1)}, u32[]{:S(2)}, u32[]{:S(2)}) async-start(bf16[4,32,4096]{2,1,0:T(8,128)(2,1)} %bitcast.9), calls=%async_computation.3 | async-start | bytes 2097152 | tf_op jit(solution)/shard_map/all_to_all | solution.py:343
  129.5 25.9 %all-to-all-done.3.parts = bf16[4,32,4096]{2,1,0:T(8,128)(2,1)S(1)} async-done(((bf16[4,32,4096]{2,1,0:T(8,128)(2,1)}), bf16[4,32,4096]{2,1,0:T(8,128)(2,1)S(1)}, u32[]{:S(2)}, u32[]{:S(2)}) %all-to-all-start.3) | async-done | bytes 1048608 | tf_op jit(solution)/shard_map/all_to_all | solution.py:343
  155.4 1.0 copy-done.3
  156.4 3.1 %shard_map.161 = bf16[8,32,512]{2,1,0:T(8,128)(2,1)} custom-call(s32[2]{0:T(128)} %pad_add_fusion.place, bf16[4,32,4096]{2,1,0:T(8,128)(2,1)} %copy-done.3, f32[256,128]{1,0:T(8,128)} %get-tuple-element.29.probs, f32[1,4096]{1,0:T(1,128)} %bitcast.27, bf16[4,8,32,512]{3,2,1,0:T(8,128)(2,1)} %bitcast.18), custom_call_target="tpu_custom_call" | custom-call | tf_op jit(solution)/shard_map/pallas_call | solution.py:346
  159.5 3.7 %all-to-all-start.4 = ((bf16[8,32,512]{2,1,0:T(8,128)(2,1)}), bf16[8,32,512]{2,1,0:T(8,128)(2,1)S(1)}, u32[]{:S(2)}, u32[]{:S(2)}) async-start(bf16[8,32,512]{2,1,0:T(8,128)(2,1)} %shard_map.161), calls=%async_computation.4 | async-start | bytes 524288 | tf_op jit(solution)/shard_map/all_to_all | solution.py:362
  164.6 2.8 %shard_map.162 = (f32[8,128,128]{2,1,0:T(8,128)}, f32[8,128,128]{2,1,0:T(8,128)}, f32[128,512]{1,0:T(8,128)}, f32[128,512]{1,0:T(8,128)}, f32[128,512]{1,0:T(8,128)}, /*index=5*/f32[8,512]{1,0:T(8,128)}) custom-call(f32[128,8]{1,0:T(8,128)} %copy.20.log_ret, f32[128,8]{1,0:T(8,128)} %copy.21.step, bf16[128,256]{1,0:T(8,128)(2,1)} %state_in.3, ...), custom_call_target="tpu_custom_call" | custom-call | tf_op jit(solution)/shard_map/pallas_call | solution.py:270
  167.4 2.7 %all-to-all-done.4 = bf16[8,32,512]{2,1,0:T(8,128)(2,1)S(1)} async-done(((bf16[8,32,512]{2,1,0:T(8,128)(2,1)}), bf16[8,32,512]{2,1,0:T(8,128)(2,1)S(1)}, u32[]{:S(2)}, u32[]{:S(2)}) %all-to-all-start.4) | async-done | bytes 262176 | tf_op jit(solution)/shard_map/all_to_all | solution.py:362
  170.1 1.3 broadcast_in_dim.28
  171.4 3.3 %all-to-all-start.6 = ((f32[4,8,512]{2,1,0:T(8,128)}), f32[4,8,512]{2,1,0:T(8,128)S(1)}, u32[]{:S(2)}, u32[]{:S(2)}) async-start(f32[4,8,512]{2,1,0:T(8,128)} %broadcast_in_dim.28), calls=%async_computation.6 | async-start | bytes 131072 | tf_op jit(solution)/shard_map/all_to_all | solution.py:282
  175.4 4.7 %shard_map.163 = (bf16[128,512]{1,0:T(8,128)(2,1)}, f32[128,512]{1,0:T(8,128)}, f32[128,256]{1,0:T(8,128)}, bf16[128,512]{1,0:T(8,128)(2,1)}) custom-call(bf16[256,512]{1,0:T(8,128)(2,1)} %bitcast.21, bf16[256,128]{1,0:T(8,128)(2,1)} %get-tuple-element.30.table, bf16[128,512]{1,0:T(8,128)(2,1)} %grad.3, bf16[128,512]{1,0:T(8,128)(2,1)} %mixer.3, ...), custom_call_target="tpu_custom_call" | custom-call | tf_op jit(solution)/shard_map/pallas_call | solution.py:366
  181.4 18.4 %all_to_all.48.states = bf16[4,128,512]{2,1,0:T(8,128)(2,1)} all-to-all(bf16[4,128,512]{2,1,0:T(8,128)(2,1)S(1)} %broadcast_in_dim.13), channel_id=1, replica_groups=mesh['ctx'=4,'exp'=8] {'ctx'}, dimensions={0} | all-to-all | bytes 1048576 | tf_op jit(solution)/shard_map/all_to_all | solution.py:376
  199.8 3.3 %shard_map.164 = (bf16[128,512]{1,0:T(8,128)(2,1)}, f32[128,256]{1,0:T(8,128)}) custom-call(s32[2]{0:T(128)} %pad_add_fusion.place, bf16[4,128,512]{2,1,0:T(8,128)(2,1)} %all_to_all.48.states, f32[4,8,512]{2,1,0:T(8,128)} %copy-done.7, f32[128,512]{1,0:T(8,128)} %get-tuple-element.38.base, f32[128,256]{1,0:T(8,128)} %get-tuple-element.39.local_b, ...), custom_call_target="tpu_custom_call" | custom-call | tf_op jit(solution)/shard_map/pallas_call | solution.py:379
  (41 shorter events, 8.5 us)
Async XLA Ops:
  47.3 29.9 %copy-start = (bf16[32,32,512]{2,1,0:T(8,128)(2,1)}, bf16[32,32,512]{2,1,0:T(8,128)(2,1)S(1)}, u32[]{:S(2)}) copy-start(bf16[32,32,512]{2,1,0:T(8,128)(2,1)S(1)} %all_to_all.47) | copy-start | bytes 3145732
  47.3 29.8 %all-to-all-start.1 = ((bf16[32,32,512]{2,1,0:T(8,128)(2,1)}), bf16[32,32,512]{2,1,0:T(8,128)(2,1)S(1)}, u32[]{:S(2)}, u32[]{:S(2)}) async-start(bf16[32,32,512]{2,1,0:T(8,128)(2,1)} %bitcast.4), calls=%async_computation.1 | async-start | bytes 2097152 | tf_op jit(solution)/shard_map/all_to_all | solution.py:298
  50.9 26.2 %collective-permute-start.1 = (bf16[4,8,32,512]{3,2,1,0:T(8,128)(2,1)S(1)}, bf16[4,8,32,512]{3,2,1,0:T(8,128)(2,1)S(1)}, u32[]{:S(2)}, u32[]{:S(2)}) collective-permute-start(bf16[4,8,32,512]{3,2,1,0:T(8,128)(2,1)S(1)} %bitcast.16), channel_id=1, source_target_pairs={{0,1},{1,0},{2,3},{3,2},{4,5},{5,4},{6,7},{7,6},{8,9},{9,8},{10,11... | collective-permute-start | bytes 3145736 | tf_op jit(solution)/shard_map/ppermute | solution.py:301
  77.1 16.3 %copy-start.2 = (bf16[32,32,512]{2,1,0:T(8,128)(2,1)}, bf16[32,32,512]{2,1,0:T(8,128)(2,1)S(1)}, u32[]{:S(2)}) copy-start(bf16[32,32,512]{2,1,0:T(8,128)(2,1)S(1)} %all-to-all-done.1) | copy-start | bytes 3145732
  77.1 16.3 %collective-permute-start = (bf16[4,8,32,512]{3,2,1,0:T(8,128)(2,1)S(1)}, bf16[4,8,32,512]{3,2,1,0:T(8,128)(2,1)S(1)}, u32[]{:S(2)}, u32[]{:S(2)}) collective-permute-start(bf16[4,8,32,512]{3,2,1,0:T(8,128)(2,1)S(1)} %bitcast.19), channel_id=1, source_target_pairs={{0,1},{1,0},{2,3},{3,2},{4,5},{5,4},{6,7},{7,6},{8,9},{9,8},{10,11... | collective-permute-start | bytes 3145736 | tf_op jit(solution)/shard_map/ppermute | solution.py:301
  77.1 1.0 copy-start.4
  93.4 1.0 copy-start.5
  119.6 4.3 %copy-start.1 = (bf16[256,4096]{1,0:T(8,128)(2,1)S(1)}, bf16[256,4096]{1,0:T(8,128)(2,1)}, u32[]{:S(2)}) copy-start(bf16[256,4096]{1,0:T(8,128)(2,1)} %shard_map.160) | copy-start | bytes 6291460
  121.1 2.8 %collective-permute-start.2 = (bf16[128,4096]{1,0:T(8,128)(2,1)S(1)}, bf16[128,4096]{1,0:T(8,128)(2,1)S(1)}, u32[]{:S(2)}, u32[]{:S(2)}) collective-permute-start(bf16[128,4096]{1,0:T(8,128)(2,1)S(1)} %slice.9), channel_id=1, source_target_pairs={{0,1},{1,0},{2,3},{3,2},{4,5},{5,4},{6,7},{7,6},{8,9},{9,8},{10,11... | collective-permute-start | bytes 3145736 | tf_op jit(solution)/shard_map/ppermute | solution.py:341
  125.2 38.0 %copy-start.8 = (f32[128,8]{0,1:T(8,128)S(1)}, f32[128,8]{0,1:T(8,128)}, u32[]{:S(2)}) copy-start(f32[128,8]{0,1:T(8,128)} %param.26) | copy-start | bytes 12292
  125.2 38.7 %copy-start.9 = (f32[128,8]{0,1:T(8,128)S(1)}, f32[128,8]{0,1:T(8,128)}, u32[]{:S(2)}) copy-start(f32[128,8]{0,1:T(8,128)} %param.25) | copy-start | bytes 12292
  125.2 30.2 %all-to-all-start.3 = ((bf16[4,32,4096]{2,1,0:T(8,128)(2,1)}), bf16[4,32,4096]{2,1,0:T(8,128)(2,1)S(1)}, u32[]{:S(2)}, u32[]{:S(2)}) async-start(bf16[4,32,4096]{2,1,0:T(8,128)(2,1)} %bitcast.9), calls=%async_computation.3 | async-start | bytes 2097152 | tf_op jit(solution)/shard_map/all_to_all | solution.py:343
  128.8 45.9 %copy-start.10 = (f32[8]{0:T(128)S(1)}, f32[8]{0:T(128)}, u32[]{:S(2)}) copy-start(f32[8]{0:T(128)} %param.27) | copy-start | bytes 100
  155.4 1.0 copy-start.3
  159.5 10.6 %all-to-all-start.4 = ((bf16[8,32,512]{2,1,0:T(8,128)(2,1)}), bf16[8,32,512]{2,1,0:T(8,128)(2,1)S(1)}, u32[]{:S(2)}, u32[]{:S(2)}) async-start(bf16[8,32,512]{2,1,0:T(8,128)(2,1)} %shard_map.161), calls=%async_computation.4 | async-start | bytes 524288 | tf_op jit(solution)/shard_map/all_to_all | solution.py:362
  170.1 5.4 %copy-start.6 = (bf16[8,32,512]{2,1,0:T(8,128)(2,1)}, bf16[8,32,512]{2,1,0:T(8,128)(2,1)S(1)}, u32[]{:S(2)}) copy-start(bf16[8,32,512]{2,1,0:T(8,128)(2,1)S(1)} %all-to-all-done.4) | copy-start | bytes 786436
  171.4 9.0 %all-to-all-start.6 = ((f32[4,8,512]{2,1,0:T(8,128)}), f32[4,8,512]{2,1,0:T(8,128)S(1)}, u32[]{:S(2)}, u32[]{:S(2)}) async-start(f32[4,8,512]{2,1,0:T(8,128)} %broadcast_in_dim.28), calls=%async_computation.6 | async-start | bytes 131072 | tf_op jit(solution)/shard_map/all_to_all | solution.py:282
  180.4 19.3 %copy-start.7 = (f32[4,8,512]{2,1,0:T(8,128)}, f32[4,8,512]{2,1,0:T(8,128)S(1)}, u32[]{:S(2)}) copy-start(f32[4,8,512]{2,1,0:T(8,128)S(1)} %all-to-all-done.6.totals) | copy-start | bytes 196612

commit v2 on v1

v2 whole, which is shorter than its diff:
```python
from functools import partial

import jax
import jax.numpy as jnp
from jax import lax
from jax.experimental import pallas as pl
from jax.experimental.pallas import tpu as pltpu
from jax.sharding import PartitionSpec as P


N = 128
LANES = 128
norm_epsilon = 1e-05
f32 = jnp.float32
bf16 = jnp.bfloat16
highest = lax.Precision.HIGHEST
vmem_bytes = 56 * 1024 * 1024


def params(steps=0):
    return pltpu.CompilerParams(
        dimension_semantics=("arbitrary",) * steps, vmem_limit_bytes=vmem_bytes
    )


def whole(shape):
    return pl.BlockSpec(shape, lambda *_: (0,) * len(shape))


def iota(shape, dim):
    return lax.broadcasted_iota(jnp.int32, shape, dim)


def dot(a, b, ca, cb, precision=None):
    return lax.dot_general(
        a, b, (((ca,), (cb,)), ((), ())), precision=precision, preferred_element_type=f32
    )


def pack_kernel(resid, ids_t, probs_t, out):
    peers, rows = out.shape[0], out.shape[1]
    width = out.shape[2] - LANES
    eye = jnp.where(iota((rows, rows), 0) == iota((rows, rows), 1), 1.0, 0.0).astype(bf16)
    ids = dot(eye, ids_t[...].astype(f32).astype(bf16), 1, 1)
    probs = dot(eye, probs_t[...], 1, 1)
    lane = iota((rows, LANES), 1)
    meta = jnp.where(lane == 0, ids[:, 0:1], 0.0) + jnp.where(lane == 1, ids[:, 1:2], 0.0)
    meta = meta + jnp.where(lane == 2, probs[:, 0:1], 0.0) + jnp.where(lane == 3, probs[:, 1:2], 0.0)
    meta = meta.astype(bf16)
    for j in range(peers):
        out[j, :, :width] = resid[:, j * width : (j + 1) * width]
        out[j, :, width:] = meta


def dispatch_kernel(packed, table, probs, rows_x, *, experts, capacity):
    tokens = packed.shape[0]
    width = packed.shape[1] - LANES
    meta = packed[:, width:].astype(f32)
    lane = iota((tokens, LANES), 1).astype(f32)
    first = meta[:, 0:1] == lane
    second = meta[:, 1:2] == lane
    member = jnp.where(first | second, 1.0, 0.0).astype(bf16)
    weight = (jnp.where(first, meta[:, 2:3], 0.0) + jnp.where(second, meta[:, 3:4], 0.0)).astype(bf16)
    row = iota((tokens, tokens), 0)
    col = iota((tokens, tokens), 1)
    before = jnp.where(row < col, 1.0, 0.0).astype(bf16)
    same = jnp.where(row == col, 1.0, 0.0).astype(bf16)
    position = dot(member, before, 0, 0)
    member_t = dot(member, same, 0, 0)
    weight_t = dot(weight, same, 0, 0)
    slot = iota((capacity, tokens), 0).astype(f32)
    for e in range(experts):
        hit = (slot == position[e : e + 1, :]) & (member_t[e : e + 1, :] > 0.5)
        entry = jnp.where(hit, 1.0, 0.0)
        table[e * capacity : (e + 1) * capacity, :] = entry.astype(bf16)
        share = jnp.sum(entry * weight_t[e : e + 1, :], axis=1, keepdims=True)
        probs[e * capacity : (e + 1) * capacity, :] = jnp.broadcast_to(share, (capacity, LANES))
    out_x = dot(table[...], packed[:, :width], 1, 0).astype(bf16)
    for c in range(rows_x.shape[0]):
        rows_x[c] = out_x


def select_kernel(table, grad, rows_g):
    out_g = dot(table[...], grad[...], 1, 0).astype(bf16)
    for c in range(rows_g.shape[0]):
        rows_g[c] = out_g


def gate_up_kernel(own, other, gain, gate_w, up_w, coef_gate, coef_up, normed):
    ctx, peers, slots, width = own.shape
    half = ctx * slots
    model = peers * width

    @pl.when(pl.program_id(0) == 0)
    def _():
        for side, ref in enumerate((own, other)):
            total = jnp.zeros((half, 1), f32)
            for j in range(peers):
                x = ref[:, j].reshape(half, width).astype(f32)
                total = total + jnp.sum(x * x, axis=1, keepdims=True)
            inverse = lax.rsqrt(total * (1.0 / model) + norm_epsilon)
            for j in range(peers):
                x = ref[:, j].reshape(half, width).astype(f32)
                cols = slice(j * width, (j + 1) * width)
                normed[side * half : (side + 1) * half, cols] = (x * inverse * gain[:, cols]).astype(bf16)

    rows = normed[...]
    gate = dot(rows, gate_w[0], 1, 1)
    up = dot(rows, up_w[0], 1, 1)
    sig = jax.nn.sigmoid(gate)
    coef_gate[...] = up * sig * (1.0 + gate * (1.0 - sig))
    coef_up[...] = gate * sig


def back_kernel(
    own, other, coef_gate, coef_up, gate_hbm, up_hbm, down_hbm, out_own, out_other,
    grads, gate_grad, up_grad, down_w, gate_w, up_w, staged, in_sems, out_sems,
):
    ctx, peers, slots, width = own.shape
    half = ctx * slots
    blocks, block, _ = down_w.shape
    columns, _, column = gate_w.shape

    def down_copy(i):
        return pltpu.make_async_copy(
            down_hbm.at[0, i * block : (i + 1) * block, :], down_w.at[i], in_sems.at[i]
        )

    def pair_copies(i):
        cols = slice(i * column, (i + 1) * column)
        at = blocks + 2 * i
        return (
            pltpu.make_async_copy(gate_hbm.at[0, :, cols], gate_w.at[i], in_sems.at[at]),
            pltpu.make_async_copy(up_hbm.at[0, :, cols], up_w.at[i], in_sems.at[at + 1]),
        )

    def out_copies(i):
        cols = slice(i * column, (i + 1) * column)
        return (
            pltpu.make_async_copy(staged.at[i, 0:half], out_own.at[:, cols], out_sems.at[2 * i]),
            pltpu.make_async_copy(staged.at[i, half : 2 * half], out_other.at[:, cols], out_sems.at[2 * i + 1]),
        )

    for i in range(blocks):
        down_copy(i).start()
    for i in range(columns):
        for copy in pair_copies(i):
            copy.start()
    for side, ref in enumerate((own, other)):
        for j in range(peers):
            cols = slice(j * width, (j + 1) * width)
            grads[side * half : (side + 1) * half, cols] = ref[:, j].reshape(half, width)
    rows = grads[...]
    for i in range(blocks):
        down_copy(i).wait()
        part = slice(i * block, (i + 1) * block)
        grad = dot(rows, down_w[i], 1, 1)
        gate_grad[:, part] = (grad * coef_gate[:, part]).astype(bf16)
        up_grad[:, part] = (grad * coef_up[:, part]).astype(bf16)
    for i in range(columns):
        for copy in pair_copies(i):
            copy.wait()
        staged[i] = (dot(gate_grad[...], gate_w[i], 1, 0) + dot(up_grad[...], up_w[i], 1, 0)).astype(bf16)
        for copy in out_copies(i):
            copy.start()
    for i in range(columns):
        for copy in out_copies(i):
            copy.wait()


def slot_kernel(place, parts, probs, gain, x_rows, out, sums):
    ctx, slots, model = parts.shape
    peers, width = x_rows.shape[1], x_rows.shape[3]
    prob = probs[:, 0:1]
    squares = jnp.zeros((slots, 1), f32)
    product = jnp.zeros((slots, 1), f32)
    for j in range(peers):
        cols = slice(j * width, (j + 1) * width)
        total = parts[0, :, cols].astype(f32)
        for c in range(1, ctx):
            total = total + parts[c, :, cols].astype(f32)
        total = total * gain[:, cols]
        sums[:, cols] = total
        x = x_rows[0, j].astype(f32)
        squares = squares + jnp.sum(x * x, axis=1, keepdims=True)
        product = product + jnp.sum(total * x, axis=1, keepdims=True)
    inverse = lax.rsqrt(squares * (1.0 / model) + norm_epsilon)
    scale = prob * inverse
    shift = scale * product * inverse * inverse * (1.0 / model)
    for j in range(peers):
        cols = slice(j * width, (j + 1) * width)
        out[j] = (sums[:, cols] * scale - x_rows[0, j].astype(f32) * shift).astype(bf16)


def mixer_setup_kernel(
    log_t, step_t, skip, state_in, state_out, mix, weigh, step_l, tail_l, head_l, skip_l, total_l, *, groups
):
    heads, tokens = log_t.shape
    width = step_l.shape[1]
    size = width // heads
    row = iota((tokens, tokens), 0)
    col = iota((tokens, tokens), 1)
    upto = jnp.where(row <= col, 1.0, 0.0)
    eye = jnp.where(row == col, 1.0, 0.0)
    cum_t = dot(log_t[...], upto, 1, 0, highest)
    cum = dot(upto, log_t[...], 0, 1, highest)
    steps = dot(eye, step_t[...], 1, 1, highest)
    last = cum[tokens - 1 : tokens, :]
    spread = jnp.where(iota((heads, width), 0) == iota((heads, width), 1) // size, 1.0, 0.0)
    step_l[...] = dot(steps, spread, 1, 0, highest)
    tail_l[...] = dot(steps * jnp.exp(last - cum), spread, 1, 0, highest)
    head_l[...] = dot(jnp.exp(cum), spread, 1, 0, highest)
    skip_l[...] = dot(jnp.broadcast_to(skip[...], (8, heads)), spread, 1, 0, highest)
    total_l[...] = dot(jnp.broadcast_to(jnp.exp(last), (8, heads)), spread, 1, 0, highest)
    later = col >= row
    for g in range(groups):
        cols = slice(g * N, (g + 1) * N)
        inter = dot(state_in[:, cols], state_out[:, cols], 1, 1)
        for h in range(g * heads // groups, (g + 1) * heads // groups):
            gap = cum_t[h : h + 1, :] - cum[:, h : h + 1]
            decay = jnp.where(later, jnp.exp(jnp.where(later, gap, 0.0)), 0.0)
            mix[h] = (decay * inter).astype(bf16)
            weigh[h] = decay * steps[:, h : h + 1]


def upstream_kernel(moved, table, grad, state_out, head_l, total_l, upstream, resid_grad, state):
    width = grad.shape[1]
    groups = state_out.shape[1] // N
    span = width // groups
    moe = dot(table[...], moved[...], 0, 0).astype(bf16)
    up = grad[...].astype(f32) + moe.astype(f32)
    upstream[...] = up
    resid_grad[...] = up.astype(bf16)
    for g in range(groups):
        cols = slice(g * N, (g + 1) * N)
        wide = slice(g * span, (g + 1) * span)
        scaled = (up[:, wide] * head_l[:, wide]).astype(bf16)
        state[0:N, wide] = dot(state_out[:, cols], scaled, 0, 0).astype(bf16)
    total = total_l[...]
    high = total.astype(bf16)
    low = (total - high.astype(f32)).astype(bf16)
    state[N : N + 8, :] = high
    state[N + 8 : N + 16, :] = low


def mixer_local_kernel(upstream, resid_grad, mixer, state_out, mix, weigh, step_l, skip_l, base, local_b):
    tokens, width = upstream.shape
    heads = mix.shape[0]
    size = width // heads
    groups = state_out.shape[1] // N
    for g in range(groups):
        cols = slice(g * N, (g + 1) * N)
        weighted = jnp.zeros((tokens, tokens), f32)
        for h in range(g * heads // groups, (g + 1) * heads // groups):
            part = slice(h * size, (h + 1) * size)
            up_h = resid_grad[:, part]
            mixed = dot(mix[h], up_h, 1, 0)
            base[:, part] = step_l[:, part] * mixed + skip_l[0:1, part] * upstream[:, part]
            weighted = weighted + weigh[h] * dot(mixer[:, part], up_h, 1, 1)
        local_b[:, cols] = dot(weighted.astype(bf16), state_out[:, cols], 1, 0)


def mixer_far_kernel(*refs):
    base, local_b, mixer, state_in, tail_l, mixer_grad, input_grad = refs[-7:]
    states = refs[:-7]
    groups = state_in.shape[1] // N
    width = base.shape[1]
    span = width // groups
    incoming = states[-1][0:N, :].astype(f32)
    for ref in states[-2::-1]:
        decay = ref[N : N + 1, :].astype(f32) + ref[N + 8 : N + 9, :].astype(f32)
        incoming = ref[0:N, :].astype(f32) + decay * incoming
    incoming = incoming.astype(bf16)
    for g in range(groups):
        cols = slice(g * N, (g + 1) * N)
        wide = slice(g * span, (g + 1) * span)
        far = dot(state_in[:, cols], incoming[:, wide], 1, 0)
        mixer_grad[:, wide] = (base[:, wide] + tail_l[:, wide] * far).astype(bf16)
        scaled = (mixer[:, wide].astype(f32) * tail_l[:, wide]).astype(bf16)
        input_grad[:, cols] = local_b[:, cols] + dot(scaled, incoming[:, wide], 1, 1)


def block_of(total, most):
    size = min(total, most)
    while total % size:
        size -= LANES if size > LANES else 1
    return size


def cost(flops, moved):
    return pl.CostEstimate(flops=flops, transcendentals=0, bytes_accessed=moved)


def body(
    resid_input,
    norm_gain,
    expert_ids,
    route_probs,
    gate_weight,
    up_weight,
    down_weight,
    grad_output,
    mixer_input,
    state_input,
    state_output,
    step_size,
    log_retention,
    skip_gain,
):
    ctx = lax.axis_size("ctx")
    peers = lax.axis_size("exp")
    place = jnp.stack([lax.axis_index("ctx"), lax.axis_index("exp")]).astype(jnp.int32)
    experts = peers // 2
    token_rows, model = resid_input.shape
    tokens, width = grad_output.shape
    capacity = 2 * tokens // experts
    slots = capacity // 2
    heads = skip_gain.shape[0]
    groups = state_input.shape[1] // N
    hidden = gate_weight.shape[1]
    gain = norm_gain.reshape(1, model)
    partner = [(i, i ^ 1) for i in range(peers)]
    shape = jax.ShapeDtypeStruct

    packed = pl.pallas_call(
        pack_kernel,
        out_shape=shape((peers, token_rows, width + LANES), bf16),
        compiler_params=params(),
        name="pack",
    )(resid_input, expert_ids.T, route_probs.T)
    packed = lax.all_to_all(packed, "exp", split_axis=0, concat_axis=0, tiled=True)

    mix, weigh, step_l, tail_l, head_l, skip_l, total_l = pl.pallas_call(
        partial(mixer_setup_kernel, groups=groups),
        out_shape=(
            shape((heads, tokens, tokens), bf16),
            shape((heads, tokens, tokens), f32),
            shape((tokens, width), f32),
            shape((tokens, width), f32),
            shape((tokens, width), f32),
            shape((8, width), f32),
            shape((8, width), f32),
        ),
        compiler_params=params(),
        cost_estimate=cost(2 * 10**9, 2 * 10**6),
        name="mixer_setup",
    )(log_retention.T, step_size.T, skip_gain.reshape(1, heads), state_input, state_output)

    table, probs, rows_x = pl.pallas_call(
        partial(dispatch_kernel, experts=experts, capacity=capacity),
        out_shape=(
            shape((experts * capacity, tokens), bf16),
            shape((experts * capacity, LANES), f32),
            shape((ctx, experts * capacity, width), bf16),
        ),
        compiler_params=params(),
        name="dispatch",
    )(packed.reshape(tokens, width + LANES))
    rows_g = pl.pallas_call(
        select_kernel,
        out_shape=shape((ctx, experts * capacity, width), bf16),
        compiler_params=params(),
        cost_estimate=cost(10**9, 2 * 10**6),
        name="select",
    )(table, grad_output)

    def spread(rows):
        got = lax.all_to_all(
            rows.reshape(ctx * peers, slots, width), ("ctx", "exp"), split_axis=0, concat_axis=0, tiled=True
        ).reshape(ctx, peers, slots, width)
        return got, lax.ppermute(got, "exp", partner)

    own_x, other_x = spread(rows_x)
    own_g, other_g = spread(rows_g)
    rows = 2 * ctx * slots
    half = rows // 2
    slab = (ctx, peers, slots, width)
    block = block_of(hidden, 256)
    blocks = hidden // block
    weight_spec = pl.BlockSpec((1, block, model), lambda i: (0, i, 0))
    act_spec = pl.BlockSpec((rows, block), lambda i: (0, i))
    product = 2 * rows * model * hidden
    coef_gate, coef_up = pl.pallas_call(
        gate_up_kernel,
        grid=(blocks,),
        in_specs=[whole(slab), whole(slab), whole((1, model)), weight_spec, weight_spec],
        out_specs=[act_spec, act_spec],
        out_shape=(shape((rows, hidden), f32), shape((rows, hidden), f32)),
        scratch_shapes=[pltpu.VMEM((rows, model), bf16)],
        compiler_params=params(1),
        cost_estimate=cost(2 * product, 4 * model * hidden),
        name="gate_up",
    )(own_x, other_x, gain, gate_weight, up_weight)
    column = block_of(model, 512)
    columns = model // column
    in_hbm = pl.BlockSpec(memory_space=pl.ANY)
    in_vmem = pl.BlockSpec(memory_space=pltpu.VMEM)
    out_own, out_other = pl.pallas_call(
        back_kernel,
        in_specs=[in_vmem, in_vmem, in_vmem, in_vmem, in_hbm, in_hbm, in_hbm],
        out_specs=[in_hbm, in_hbm],
        out_shape=(shape((half, model), bf16), shape((half, model), bf16)),
        scratch_shapes=[
            pltpu.VMEM((rows, model), bf16),
            pltpu.VMEM((rows, hidden), bf16),
            pltpu.VMEM((rows, hidden), bf16),
            pltpu.VMEM((blocks, block, model), bf16),
            pltpu.VMEM((columns, hidden, column), bf16),
            pltpu.VMEM((columns, hidden, column), bf16),
            pltpu.VMEM((columns, rows, column), bf16),
            pltpu.SemaphoreType.DMA((blocks + 2 * columns,)),
            pltpu.SemaphoreType.DMA((2 * columns,)),
        ],
        compiler_params=params(),
        cost_estimate=cost(3 * product, 6 * model * hidden),
        name="back",
    )(own_g, other_g, coef_gate, coef_up, gate_weight, up_weight, down_weight)

    swapped = lax.ppermute(out_other, "exp", partner)
    summed = (out_own.astype(f32) + swapped.astype(f32)).astype(bf16)
    parts = lax.all_to_all(
        summed.reshape(ctx, slots, model), "ctx", split_axis=0, concat_axis=0, tiled=True
    )
    moved = pl.pallas_call(
        slot_kernel,
        grid_spec=pltpu.PrefetchScalarGridSpec(
            num_scalar_prefetch=1,
            grid=(1,),
            in_specs=[
                whole((ctx, slots, model)),
                pl.BlockSpec((slots, LANES), lambda i, at: (at[1], 0)),
                whole((1, model)),
                pl.BlockSpec((1, peers, slots, width), lambda i, at: (at[0], 0, 0, 0)),
            ],
            out_specs=whole((peers, slots, width)),
            scratch_shapes=[pltpu.VMEM((slots, model), f32)],
        ),
        out_shape=shape((peers, slots, width), bf16),
        compiler_params=params(1),
        name="slot",
    )(place, parts, probs, gain, own_x)
    moved = lax.all_to_all(moved, "exp", split_axis=0, concat_axis=0, tiled=True).reshape(
        experts * capacity, width
    )

    upstream, resid_grad, state = pl.pallas_call(
        upstream_kernel,
        out_shape=(
            shape((tokens, width), f32),
            shape((tokens, width), bf16),
            shape((N + 16, width), bf16),
        ),
        compiler_params=params(),
        name="upstream",
    )(moved, table, grad_output, state_output, head_l, total_l)
    states = [
        lax.ppermute(state, "ctx", [(i, i - k) for i in range(k, ctx)]) for k in range(1, ctx)
    ]
    base, local_b = pl.pallas_call(
        mixer_local_kernel,
        out_shape=(shape((tokens, width), f32), shape((tokens, groups * N), f32)),
        compiler_params=params(),
        cost_estimate=cost(3 * 10**9, 2 * 10**6),
        name="mixer_local",
    )(upstream, resid_grad, mixer_input, state_output, mix, weigh, step_l, skip_l)
    mixer_grad, state_input_grad = pl.pallas_call(
        mixer_far_kernel,
        out_shape=(shape((tokens, width), bf16), shape((tokens, groups * N), f32)),
        compiler_params=params(),
        name="mixer_far",
    )(*states, base, local_b, mixer_input, state_input, tail_l)
    return (resid_grad, mixer_grad, state_input_grad)


def solution(mesh):
    in_specs = (
        P(("ctx", "exp"), None),
        P(),
        P(("ctx", "exp"), None),
        P(("ctx", "exp"), None),
        P("exp", "ctx", None),
        P("exp", "ctx", None),
        P("exp", "ctx", None),
        P("ctx", "exp"),
        P("ctx", "exp"),
        P("ctx", "exp"),
        P("ctx", "exp"),
        P("ctx", "exp"),
        P("ctx", "exp"),
        P("exp"),
    )
    out_specs = (P("ctx", "exp"), P("ctx", "exp"), P("ctx", "exp"))
    return jax.shard_map(body, mesh=mesh, in_specs=in_specs, out_specs=out_specs, check_vma=False)
```

time: 204 us -> 187 us (0.917)
  blocking collectives: 59.5 us -> 11.1 us
  waiting for transfers between devices: 57 us -> 91.5 us
  local copies, waits for them, and re-layouts: 10.8 us -> 4.36 us
  starting transfers between devices: 15.1 us -> 19.7 us
    all_to_all x3 -> x1, blocking collectives: 59.5 us -> 11.1 us  [body(): lax.all_to_all(packed, 'exp', split_axis=0, concat_axis=0, tiled=True)]
    all_to_all x1 -> x2, waiting for transfers between devices: 25.9 us -> 50 us  [spread(): lax.all_to_all(rows.reshape(ctx * peers, slots, width), ('ctx', 'exp'), s...]
    ppermute x1 -> x4, waiting for transfers between devices: 2.29 us -> 11.6 us  [the longest x3 9.1 us: body(): lax.ppermute(state, 'ctx', [(i, i - k) for i in range(k, ctx)])]
    all_to_all x1 -> x2, starting transfers between devices: 3.62 us -> 7.76 us  [spread(): lax.all_to_all(rows.reshape(ctx * peers, slots, width), ('ctx', 'exp'), s...]
    ppermute x1 -> x4, starting transfers between devices: 0.54 us -> 4.41 us  [the longest x3 3.86 us: body(): lax.ppermute(state, 'ctx', [(i, i - k) for i in range(k, ctx)])]
    all_to_all x1 -> x0, starting transfers between devices: 3.28 us -> none  [body(): lax.all_to_all(jnp.broadcast_to(total_l[None], (ctx, 8, width)), 'ctx', s...]
    broadcast_in_dim x5 -> x0, local copies, waits for them, and re-layouts: 2.38 us -> none  [the longest x1 1.34 us: body(): jnp.broadcast_to(total_l[None], (ctx, 8, width))]
    pallas_call x5 -> x7, Pallas kernels: 48.6 us -> 47 us  [the longest x1 20.6 us: body(): pl.pallas_call(back_kernel, in_specs=[in_vmem, in_vmem, in_vmem, in_vmem,...]
  transfers between devices with their start and end apart: 7 -> 10, of which waited for: 5 -> 7; matrix products, arithmetic and copies ran while one was open for 1% -> 0% of each run, Pallas kernels for 11% -> 12%
where the time goes in v2:
time: 187 us; the launch traced here: 186 us
  waiting for transfers between devices  91.5 us (49%)
  Pallas kernels  55.4 us (30%)
  starting transfers between devices  19.7 us (11%)
  blocking collectives  11.1 us (6%)
  local copies, waits for them, and re-layouts  4.36 us (2%)
  other arithmetic  3.07 us (2%)
    all_to_all x2, waiting for transfers between devices, spread(): lax.all_to_all(rows.reshape(ctx * peers, slots, width), ('ctx', 'exp'), s...  50 us
    all_to_all x1, waiting for transfers between devices, body(): lax.all_to_all(summed.reshape(ctx, slots, model), 'ctx', split_axis=0, co...  25.9 us
    pallas_call x1, Pallas kernels, body(): pl.pallas_call(back_kernel, in_specs=[in_vmem, in_vmem, in_vmem, in_vmem,...  20.6 us
    pallas_call x1, Pallas kernels, body(): pl.pallas_call(gate_up_kernel, grid=(blocks,), in_specs=[whole(slab), who...  15.3 us
    all_to_all x1, blocking collectives, body(): lax.all_to_all(packed, 'exp', split_axis=0, concat_axis=0, tiled=True)  11.1 us
    ppermute x3, waiting for transfers between devices, body(): lax.ppermute(state, 'ctx', [(i, i - k) for i in range(k, ctx)])  9.1 us
    all_to_all x2, starting transfers between devices, spread(): lax.all_to_all(rows.reshape(ctx * peers, slots, width), ('ctx', 'exp'), s...  7.76 us
    unnamed x18, local copies, waits for them, and re-layouts  4.36 us
  transfers between devices with their start and end apart: 10, of which 7 were waited for; matrix products, arithmetic and copies ran while one was open for 0% of the time, Pallas kernels for 12%

profile of v2, /device:TPU:0, one launch (start us, length us, event | category | flops | bytes accessed | tf_op | source)
XLA Modules:
  0.0 185.9 jit_solution(9685017129321948236)
XLA Ops:
  0.6 1.8 pack.1
  2.4 11.1 %all_to_all.25 = bf16[8,16,640]{2,1,0:T(8,128)(2,1)} all-to-all(bf16[8,16,640]{2,1,0:T(8,128)(2,1)} %pack.1), channel_id=1, replica_groups=mesh['ctx'=4,'exp'=8] {'exp'}, dimensions={0} | all-to-all | bytes 327680 | tf_op jit(solution)/shard_map/all_to_all | solution.py:331
  13.6 2.4 %dispatch.1 = (bf16[256,128]{1,0:T(8,128)(2,1)}, f32[256,128]{1,0:T(8,128)}, bf16[4,256,512]{2,1,0:T(8,128)(2,1)}) custom-call(bf16[128,640]{1,0:T(8,128)(2,1)} %bitcast.23), custom_call_target="tpu_custom_call" | custom-call | tf_op jit(solution)/shard_map/dispatch/pallas_call | solution.py:349
  16.0 4.1 %all-to-all-start.2 = ((bf16[32,32,512]{2,1,0:T(8,128)(2,1)}), bf16[32,32,512]{2,1,0:T(8,128)(2,1)S(1)}, u32[]{:S(2)}, u32[]{:S(2)}) async-start(bf16[32,32,512]{2,1,0:T(8,128)(2,1)} %bitcast.22), calls=%async_computation.2 | async-start | bytes 2097152 | tf_op jit(solution)/shard_map/all_to_all | solution.py:368
  20.1 2.1 %select.1 = bf16[4,256,512]{2,1,0:T(8,128)(2,1)} custom-call(bf16[256,128]{1,0:T(8,128)(2,1)} %get-tuple-element.24.table, bf16[128,512]{1,0:T(8,128)(2,1)} %grad.3), custom_call_target="tpu_custom_call" | custom-call | flops 1000000000 | bytes 2000000 | tf_op jit(solution)/shard_map/select/pallas_call | solution.py:359
  22.3 24.1 %all-to-all-done.2 = bf16[32,32,512]{2,1,0:T(8,128)(2,1)S(1)} async-done(((bf16[32,32,512]{2,1,0:T(8,128)(2,1)}), bf16[32,32,512]{2,1,0:T(8,128)(2,1)S(1)}, u32[]{:S(2)}, u32[]{:S(2)}) %all-to-all-start.2) | async-done | bytes 1048608 | tf_op jit(solution)/shard_map/all_to_all | solution.py:368
  46.4 3.6 %all-to-all-start.1 = ((bf16[32,32,512]{2,1,0:T(8,128)(2,1)}), bf16[32,32,512]{2,1,0:T(8,128)(2,1)S(1)}, u32[]{:S(2)}, u32[]{:S(2)}) async-start(bf16[32,32,512]{2,1,0:T(8,128)(2,1)} %bitcast.21), calls=%async_computation.1 | async-start | bytes 2097152 | tf_op jit(solution)/shard_map/all_to_all | solution.py:368
  50.3 25.9 %all-to-all-done.1 = bf16[32,32,512]{2,1,0:T(8,128)(2,1)S(1)} async-done(((bf16[32,32,512]{2,1,0:T(8,128)(2,1)}), bf16[32,32,512]{2,1,0:T(8,128)(2,1)S(1)}, u32[]{:S(2)}, u32[]{:S(2)}) %all-to-all-start.1) | async-done | bytes 1048608 | tf_op jit(solution)/shard_map/all_to_all | solution.py:368
  77.2 15.3 %gate_up.1 = (f32[256,1536]{1,0:T(8,128)}, f32[256,1536]{1,0:T(8,128)}) custom-call(bf16[4,8,32,512]{3,2,1,0:T(8,128)(2,1)} %bitcast.16, bf16[4,8,32,512]{3,2,1,0:T(8,128)(2,1)} %copy-done.3, f32[1,4096]{1,0:T(1,128)} %bitcast.24, bf16[1,1536,4096]{2,1,0:T(8,128)(2,1)} %gate_hbm.1, bf16[1,1536,4096]{2,1,0:T(8,128)(2,1)} %up_hbm.1), custom_call_target="tpu_custom_call" | custom-call | flops 6442450944 | bytes 25165824 | tf_op jit(solution)/shard_map/gate_up/pallas_call | solution.py:383
  93.4 20.6 %back.1 = (bf16[128,4096]{1,0:T(8,128)(2,1)}, bf16[128,4096]{1,0:T(8,128)(2,1)}) custom-call(bf16[4,8,32,512]{3,2,1,0:T(8,128)(2,1)} %bitcast.19, bf16[4,8,32,512]{3,2,1,0:T(8,128)(2,1)} %copy-done.5, f32[256,1536]{1,0:T(8,128)} %get-tuple-element.26.coef_gate, f32[256,1536]{1,0:T(8,128)} %get-tuple-element.27.coef_up, bf16[1,1536,4096]{2,1,0:T(8,128)(2,1)} %gate_hbm.1, ...), custom_call_target="tpu_custom_call" | custom-call | flops 9663676416 | bytes 37748736 | tf_op jit(solution)/shard_map/back/pallas_call | solution.py:398
  114.6 2.5 %collective-permute-done.2 = bf16[128,4096]{1,0:T(8,128)(2,1)S(1)} collective-permute-done((bf16[128,4096]{1,0:T(8,128)(2,1)}, bf16[128,4096]{1,0:T(8,128)(2,1)S(1)}, u32[]{:S(2)}, u32[]{:S(2)}) %collective-permute-start.2) | collective-permute-done | bytes 1048608 | tf_op jit(solution)/shard_map/ppermute | solution.py:419
  117.1 2.5 %add_convert_fusion = bf16[128,4096]{1,0:T(8,128)(2,1)} fusion(bf16[128,4096]{1,0:T(8,128)(2,1)S(1)} %collective-permute-done.2, bf16[128,4096]{1,0:T(8,128)(2,1)} %get-tuple-element.28), kind=kLoop, calls=%fused_computation | loop fusion | flops 2097152 | bytes 3145728 | tf_op jit(solution)/shard_map/convert_element_type | solution.py:420
  119.6 3.5 %all-to-all-start.3 = ((bf16[4,32,4096]{2,1,0:T(8,128)(2,1)}), bf16[4,32,4096]{2,1,0:T(8,128)(2,1)S(1)}, u32[]{:S(2)}, u32[]{:S(2)}) async-start(bf16[4,32,4096]{2,1,0:T(8,128)(2,1)} %bitcast.10), calls=%async_computation.3 | async-start | bytes 2097152 | tf_op jit(solution)/shard_map/all_to_all | solution.py:421
  123.7 25.9 %all-to-all-done.3.parts = bf16[4,32,4096]{2,1,0:T(8,128)(2,1)S(1)} async-done(((bf16[4,32,4096]{2,1,0:T(8,128)(2,1)}), bf16[4,32,4096]{2,1,0:T(8,128)(2,1)S(1)}, u32[]{:S(2)}, u32[]{:S(2)}) %all-to-all-start.3) | async-done | bytes 1048608 | tf_op jit(solution)/shard_map/all_to_all | solution.py:421
  150.6 3.1 %slot.1 = bf16[8,32,512]{2,1,0:T(8,128)(2,1)} custom-call(s32[2]{0:T(128)} %pad_add_fusion.place, bf16[4,32,4096]{2,1,0:T(8,128)(2,1)} %copy-done.1, f32[256,128]{1,0:T(8,128)} %get-tuple-element.30.probs, f32[1,4096]{1,0:T(1,128)} %bitcast.25, bf16[4,8,32,512]{3,2,1,0:T(8,128)(2,1)} %bitcast.17), custom_call_target="tpu_custom_call" | custom-call | tf_op jit(solution)/shard_map/slot/pallas_call | solution.py:424
  153.7 3.7 %all-to-all-start.4 = ((bf16[8,32,512]{2,1,0:T(8,128)(2,1)}), bf16[8,32,512]{2,1,0:T(8,128)(2,1)S(1)}, u32[]{:S(2)}, u32[]{:S(2)}) async-start(bf16[8,32,512]{2,1,0:T(8,128)(2,1)} %slot.1), calls=%async_computation.4 | async-start | bytes 524288 | tf_op jit(solution)/shard_map/all_to_all | solution.py:442
  157.4 2.9 %mixer_setup.1 = (bf16[8,128,128]{2,1,0:T(8,128)(2,1)}, f32[8,128,128]{2,1,0:T(8,128)}, f32[128,512]{1,0:T(8,128)}, f32[128,512]{1,0:T(8,128)}, f32[128,512]{1,0...) custom-call(f32[8,128]{1,0:T(8,128)} %bitcast.28, f32[8,128]{1,0:T(8,128)} %bitcast.29, f32[1,8]{1,0:T(1,128)} %bitcast.30, ...), custom_call_target="tpu_custom_call" | custom-call | flops 2000000000 | bytes 2000000 | tf_op jit(solution)/shard_map/mixer_setup/pallas_call | solution.py:333
  160.2 4.0 %all-to-all-done.4 = bf16[8,32,512]{2,1,0:T(8,128)(2,1)S(1)} async-done(((bf16[8,32,512]{2,1,0:T(8,128)(2,1)}), bf16[8,32,512]{2,1,0:T(8,128)(2,1)S(1)}, u32[]{:S(2)}, u32[]{:S(2)}) %all-to-all-start.4) | async-done | bytes 262176 | tf_op jit(solution)/shard_map/all_to_all | solution.py:442
  165.0 2.2 %upstream.1 = (f32[128,512]{1,0:T(8,128)}, bf16[128,512]{1,0:T(8,128)(2,1)}, bf16[144,512]{1,0:T(8,128)(2,1)}) custom-call(bf16[256,512]{1,0:T(8,128)(2,1)} %bitcast.20, bf16[256,128]{1,0:T(8,128)(2,1)} %get-tuple-element.24.table, bf16[128,512]{1,0:T(8,128)(2,1)} %grad.3, bf16[128,256]{1,0:T(8,128)(2,1)} %state_out.5, f32[128,512]{1,0:T(8,128)} %get-tuple-element.31.head_l, ...), custom_call_target="tpu_custom_call" | custom-call | tf_op jit(solution)/shard_map/upstream/pallas_call | solution.py:446
  168.5 1.3 collective-permute-start.4
  171.1 2.8 %mixer_local.1 = (f32[128,512]{1,0:T(8,128)}, f32[128,256]{1,0:T(8,128)}) custom-call(f32[128,512]{1,0:T(8,128)} %get-tuple-element.35.upstream, bf16[128,512]{1,0:T(8,128)(2,1)} %get-tuple-element.21.resid_grad, bf16[128,512]{1,0:T(8,128)(2,1)} %refs_5_.1, bf16[128,256]{1,0:T(8,128)(2,1)} %state_out.5, bf16[8,128,128]{2,1,0:T(8,128)(2,1)} %get-tuple-element.36.mix, ...), custom_call_target="tpu_custom_call" | custom-call | flops 3000000000 | bytes 2000000 | tf_op jit(solution)/shard_map/mixer_local/pallas_call | solution.py:459
  173.8 2.4 %collective-permute-done.3.refs_0_ = bf16[144,512]{1,0:T(8,128)(2,1)S(1)} collective-permute-done((bf16[144,512]{1,0:T(8,128)(2,1)}, bf16[144,512]{1,0:T(8,128)(2,1)S(1)}, u32[]{:S(2)}, u32[]{:S(2)}) %collective-permute-start.3) | collective-permute-done | bytes 147488 | tf_op jit(solution)/shard_map/ppermute | solution.py:457
  176.2 6.7 %collective-permute-done.4.refs_1_ = bf16[144,512]{1,0:T(8,128)(2,1)S(1)} collective-permute-done((bf16[144,512]{1,0:T(8,128)(2,1)}, bf16[144,512]{1,0:T(8,128)(2,1)S(1)}, u32[]{:S(2)}, u32[]{:S(2)}) %collective-permute-start.4) | collective-permute-done | bytes 147488 | tf_op jit(solution)/shard_map/ppermute | solution.py:457
  183.7 2.3 %mixer_far.1 = (bf16[128,512]{1,0:T(8,128)(2,1)}, f32[128,256]{1,0:T(8,128)}) custom-call(bf16[144,512]{1,0:T(8,128)(2,1)} %copy-done.6, bf16[144,512]{1,0:T(8,128)(2,1)} %copy-done.7, bf16[144,512]{1,0:T(8,128)(2,1)} %copy-done.8, f32[128,512]{1,0:T(8,128)} %get-tuple-element.40.refs_3_, f32[128,256]{1,0:T(8,128)} %get-tuple-element.41.refs_4_, ...), custom_call_target="tpu_custom_call" | custom-call | tf_op jit(solution)/shard_map/mixer_far/pallas_call | solution.py:466
  (27 shorter events, 8.4 us)
Async XLA Ops:
  16.0 30.4 %all-to-all-start.2 = ((bf16[32,32,512]{2,1,0:T(8,128)(2,1)}), bf16[32,32,512]{2,1,0:T(8,128)(2,1)S(1)}, u32[]{:S(2)}, u32[]{:S(2)}) async-start(bf16[32,32,512]{2,1,0:T(8,128)(2,1)} %bitcast.22), calls=%async_computation.2 | async-start | bytes 2097152 | tf_op jit(solution)/shard_map/all_to_all | solution.py:368
  46.3 29.9 %copy-start = (bf16[32,32,512]{2,1,0:T(8,128)(2,1)}, bf16[32,32,512]{2,1,0:T(8,128)(2,1)S(1)}, u32[]{:S(2)}) copy-start(bf16[32,32,512]{2,1,0:T(8,128)(2,1)S(1)} %all-to-all-done.2) | copy-start | bytes 3145732
  46.4 29.8 %all-to-all-start.1 = ((bf16[32,32,512]{2,1,0:T(8,128)(2,1)}), bf16[32,32,512]{2,1,0:T(8,128)(2,1)S(1)}, u32[]{:S(2)}, u32[]{:S(2)}) async-start(bf16[32,32,512]{2,1,0:T(8,128)(2,1)} %bitcast.21), calls=%async_computation.1 | async-start | bytes 2097152 | tf_op jit(solution)/shard_map/all_to_all | solution.py:368
  50.0 26.2 %collective-permute-start.1 = (bf16[4,8,32,512]{3,2,1,0:T(8,128)(2,1)S(1)}, bf16[4,8,32,512]{3,2,1,0:T(8,128)(2,1)S(1)}, u32[]{:S(2)}, u32[]{:S(2)}) collective-permute-start(bf16[4,8,32,512]{3,2,1,0:T(8,128)(2,1)S(1)} %bitcast.15), channel_id=1, source_target_pairs={{0,1},{1,0},{2,3},{3,2},{4,5},{5,4},{6,7},{7,6},{8,9},{9,8},{10,11... | collective-permute-start | bytes 3145736 | tf_op jit(solution)/shard_map/ppermute | solution.py:371
  76.2 16.3 %copy-start.2 = (bf16[32,32,512]{2,1,0:T(8,128)(2,1)}, bf16[32,32,512]{2,1,0:T(8,128)(2,1)S(1)}, u32[]{:S(2)}) copy-start(bf16[32,32,512]{2,1,0:T(8,128)(2,1)S(1)} %all-to-all-done.1) | copy-start | bytes 3145732
  76.2 16.3 %collective-permute-start = (bf16[4,8,32,512]{3,2,1,0:T(8,128)(2,1)S(1)}, bf16[4,8,32,512]{3,2,1,0:T(8,128)(2,1)S(1)}, u32[]{:S(2)}, u32[]{:S(2)}) collective-permute-start(bf16[4,8,32,512]{3,2,1,0:T(8,128)(2,1)S(1)} %bitcast.18), channel_id=1, source_target_pairs={{0,1},{1,0},{2,3},{3,2},{4,5},{5,4},{6,7},{7,6},{8,9},{9,8},{10,11... | collective-permute-start | bytes 3145736 | tf_op jit(solution)/shard_map/ppermute | solution.py:371
  76.2 1.0 copy-start.3
  92.5 1.0 copy-start.5
  114.0 3.0 %collective-permute-start.2 = (bf16[128,4096]{1,0:T(8,128)(2,1)}, bf16[128,4096]{1,0:T(8,128)(2,1)S(1)}, u32[]{:S(2)}, u32[]{:S(2)}) collective-permute-start(bf16[128,4096]{1,0:T(8,128)(2,1)} %get-tuple-element.29), channel_id=1, source_target_pairs={{0,1},{1,0},{2,3},{3,2},{4,5},{5,4},{6,7},{7,6},{8,9},{9,8},{10,11... | collective-permute-start | bytes 3145736 | tf_op jit(solution)/shard_map/ppermute | solution.py:419
  119.6 30.0 %all-to-all-start.3 = ((bf16[4,32,4096]{2,1,0:T(8,128)(2,1)}), bf16[4,32,4096]{2,1,0:T(8,128)(2,1)S(1)}, u32[]{:S(2)}, u32[]{:S(2)}) async-start(bf16[4,32,4096]{2,1,0:T(8,128)(2,1)} %bitcast.10), calls=%async_computation.3 | async-start | bytes 2097152 | tf_op jit(solution)/shard_map/all_to_all | solution.py:421
  149.6 1.0 copy-start.1
  153.7 10.6 %all-to-all-start.4 = ((bf16[8,32,512]{2,1,0:T(8,128)(2,1)}), bf16[8,32,512]{2,1,0:T(8,128)(2,1)S(1)}, u32[]{:S(2)}, u32[]{:S(2)}) async-start(bf16[8,32,512]{2,1,0:T(8,128)(2,1)} %slot.1), calls=%async_computation.4 | async-start | bytes 524288 | tf_op jit(solution)/shard_map/all_to_all | solution.py:442
  164.3 0.7 copy-start.4
  167.2 9.0 %collective-permute-start.3 = (bf16[144,512]{1,0:T(8,128)(2,1)}, bf16[144,512]{1,0:T(8,128)(2,1)S(1)}, u32[]{:S(2)}, u32[]{:S(2)}) collective-permute-start(bf16[144,512]{1,0:T(8,128)(2,1)} %get-tuple-element.34), channel_id=1, source_target_pairs={{8,0},{16,8},{24,16},{9,1},{17,9},{25,17},{10,2},{18,10},{26,18},{... | collective-permute-start | bytes 442376 | tf_op jit(solution)/shard_map/ppermute | solution.py:457
  168.5 14.5 %collective-permute-start.4 = (bf16[144,512]{1,0:T(8,128)(2,1)}, bf16[144,512]{1,0:T(8,128)(2,1)S(1)}, u32[]{:S(2)}, u32[]{:S(2)}) collective-permute-start(bf16[144,512]{1,0:T(8,128)(2,1)} %get-tuple-element.34), channel_id=1, source_target_pairs={{16,0},{24,8},{17,1},{25,9},{18,2},{26,10},{19,3},{27,11},{20,4},{... | collective-permute-start | bytes 442376 | tf_op jit(solution)/shard_map/ppermute | solution.py:457
  169.8 13.2 %collective-permute-start.5 = (bf16[144,512]{1,0:T(8,128)(2,1)}, bf16[144,512]{1,0:T(8,128)(2,1)S(1)}, u32[]{:S(2)}, u32[]{:S(2)}) collective-permute-start(bf16[144,512]{1,0:T(8,128)(2,1)} %get-tuple-element.34), channel_id=1, source_target_pairs={{24,0},{25,1},{26,2},{27,3},{28,4},{29,5},{30,6},{31,7}} | collective-permute-start | bytes 442376 | tf_op jit(solution)/shard_map/ppermute | solution.py:457
  176.2 6.7 %copy-start.6 = (bf16[144,512]{1,0:T(8,128)(2,1)}, bf16[144,512]{1,0:T(8,128)(2,1)S(1)}, u32[]{:S(2)}) copy-start(bf16[144,512]{1,0:T(8,128)(2,1)S(1)} %collective-permute-done.3.refs_0_) | copy-start | bytes 442372
  182.9 0.6 copy-start.7
  182.9 0.7 copy-start.8

commit v3 on v2

--- a/solution.py
+++ b/solution.py
@@ -1,3 +1,4 @@
+import math
 from functools import partial
 
 import jax
@@ -15,6 +16,7 @@
 bf16 = jnp.bfloat16
 highest = lax.Precision.HIGHEST
 vmem_bytes = 56 * 1024 * 1024
+resident_bytes = 1024 * 1024
 
 
 def params(steps=0):
@@ -52,7 +54,7 @@
         out[j, :, width:] = meta
 
 
-def dispatch_kernel(packed, table, probs, rows_x, *, experts, capacity):
+def dispatch_kernel(packed, table, shares, rows_x, *, experts, capacity):
     tokens = packed.shape[0]
     width = packed.shape[1] - LANES
     meta = packed[:, width:].astype(f32)
@@ -73,8 +75,7 @@
         hit = (slot == position[e : e + 1, :]) & (member_t[e : e + 1, :] > 0.5)
         entry = jnp.where(hit, 1.0, 0.0)
         table[e * capacity : (e + 1) * capacity, :] = entry.astype(bf16)
-        share = jnp.sum(entry * weight_t[e : e + 1, :], axis=1, keepdims=True)
-        probs[e * capacity : (e + 1) * capacity, :] = jnp.broadcast_to(share, (capacity, LANES))
+        shares[e * capacity : (e + 1) * capacity, :] = (entry * weight_t[e : e + 1, :]).astype(bf16)
     out_x = dot(table[...], packed[:, :width], 1, 0).astype(bf16)
     for c in range(rows_x.shape[0]):
         rows_x[c] = out_x
@@ -86,7 +87,7 @@
         rows_g[c] = out_g
 
 
-def gate_up_kernel(own, other, gain, gate_w, up_w, coef_gate, coef_up, normed):
+def gate_up_kernel(own, other, gain, gate_w, up_w, coef_gate, coef_up, inverses, normed):
     ctx, peers, slots, width = own.shape
     half = ctx * slots
     model = peers * width
@@ -99,6 +100,8 @@
                 x = ref[:, j].reshape(half, width).astype(f32)
                 total = total + jnp.sum(x * x, axis=1, keepdims=True)
             inverse = lax.rsqrt(total * (1.0 / model) + norm_epsilon)
+            if side == 0:
+                inverses[...] = jnp.broadcast_to(inverse, (half, LANES))
             for j in range(peers):
                 x = ref[:, j].reshape(half, width).astype(f32)
                 cols = slice(j * width, (j + 1) * width)
@@ -113,8 +116,8 @@
 
 
 def back_kernel(
-    own, other, coef_gate, coef_up, gate_hbm, up_hbm, down_hbm, out_own, out_other,
-    grads, gate_grad, up_grad, down_w, gate_w, up_w, staged, in_sems, out_sems,
+    own, other, coef_gate_hbm, coef_up_hbm, gate_hbm, up_hbm, down_hbm, out_own, out_other,
+    grads, coef_gate, coef_up, gate_grad, up_grad, down_w, gate_w, up_w, sems,
 ):
     ctx, peers, slots, width = own.shape
     half = ctx * slots
@@ -122,26 +125,24 @@
     columns, _, column = gate_w.shape
 
     def down_copy(i):
-        return pltpu.make_async_copy(
-            down_hbm.at[0, i * block : (i + 1) * block, :], down_w.at[i], in_sems.at[i]
-        )
+        return pltpu.make_async_copy(down_hbm.at[0, i * block : (i + 1) * block, :], down_w.at[i], sems.at[i])
 
     def pair_copies(i):
         cols = slice(i * column, (i + 1) * column)
         at = blocks + 2 * i
         return (
-            pltpu.make_async_copy(gate_hbm.at[0, :, cols], gate_w.at[i], in_sems.at[at]),
-            pltpu.make_async_copy(up_hbm.at[0, :, cols], up_w.at[i], in_sems.at[at + 1]),
+            pltpu.make_async_copy(gate_hbm.at[0, :, cols], gate_w.at[i], sems.at[at]),
+            pltpu.make_async_copy(up_hbm.at[0, :, cols], up_w.at[i], sems.at[at + 1]),
         )
 
-    def out_copies(i):
-        cols = slice(i * column, (i + 1) * column)
-        return (
-            pltpu.make_async_copy(staged.at[i, 0:half], out_own.at[:, cols], out_sems.at[2 * i]),
-            pltpu.make_async_copy(staged.at[i, half : 2 * half], out_other.at[:, cols], out_sems.at[2 * i + 1]),
-        )
-
-    for i in range(blocks):
+    coef_copies = (
+        pltpu.make_async_copy(coef_gate_hbm, coef_gate, sems.at[blocks + 2 * columns]),
+        pltpu.make_async_copy(coef_up_hbm, coef_up, sems.at[blocks + 2 * columns + 1]),
+    )
+    down_copy(0).start()
+    for copy in coef_copies:
+        copy.start()
+    for i in range(1, blocks):
         down_copy(i).start()
     for i in range(columns):
         for copy in pair_copies(i):
@@ -155,41 +156,37 @@
         down_copy(i).wait()
         part = slice(i * block, (i + 1) * block)
         grad = dot(rows, down_w[i], 1, 1)
+        if i == 0:
+            for copy in coef_copies:
+                copy.wait()
         gate_grad[:, part] = (grad * coef_gate[:, part]).astype(bf16)
         up_grad[:, part] = (grad * coef_up[:, part]).astype(bf16)
     for i in range(columns):
         for copy in pair_copies(i):
             copy.wait()
-        staged[i] = (dot(gate_grad[...], gate_w[i], 1, 0) + dot(up_grad[...], up_w[i], 1, 0)).astype(bf16)
-        for copy in out_copies(i):
-            copy.start()
-    for i in range(columns):
-        for copy in out_copies(i):
-            copy.wait()
-
-
-def slot_kernel(place, parts, probs, gain, x_rows, out, sums):
-    ctx, slots, model = parts.shape
-    peers, width = x_rows.shape[1], x_rows.shape[3]
-    prob = probs[:, 0:1]
-    squares = jnp.zeros((slots, 1), f32)
-    product = jnp.zeros((slots, 1), f32)
+        cols = slice(i * column, (i + 1) * column)
+        out = (dot(gate_grad[...], gate_w[i], 1, 0) + dot(up_grad[...], up_w[i], 1, 0)).astype(bf16)
+        out_own[:, cols] = out[:half]
+        out_other[:, cols] = out[half:]
+
+
+def slot_kernel(own, swapped, gain, inverses, x_rows, out, sums):
+    ctx, peers, slots, width = x_rows.shape
+    half = ctx * slots
+    model = peers * width
+    product = jnp.zeros((half, 1), f32)
     for j in range(peers):
         cols = slice(j * width, (j + 1) * width)
-        total = parts[0, :, cols].astype(f32)
-        for c in range(1, ctx):
-            total = total + parts[c, :, cols].astype(f32)
-        total = total * gain[:, cols]
+        total = (own[:, cols].astype(f32) + swapped[:, cols].astype(f32)) * gain[:, cols]
         sums[:, cols] = total
-        x = x_rows[0, j].astype(f32)
-        squares = squares + jnp.sum(x * x, axis=1, keepdims=True)
+        x = x_rows[:, j].reshape(half, width).astype(f32)
         product = product + jnp.sum(total * x, axis=1, keepdims=True)
-    inverse = lax.rsqrt(squares * (1.0 / model) + norm_epsilon)
-    scale = prob * inverse
-    shift = scale * product * inverse * inverse * (1.0 / model)
+    inverse = inverses[:, 0:1]
+    shift = inverse * inverse * inverse * product * (1.0 / model)
     for j in range(peers):
         cols = slice(j * width, (j + 1) * width)
-        out[j] = (sums[:, cols] * scale - x_rows[0, j].astype(f32) * shift).astype(bf16)
+        x = x_rows[:, j].reshape(half, width).astype(f32)
+        out[:, j] = (sums[:, cols] * inverse - x * shift).astype(bf16).reshape(ctx, slots, width)
 
 
 def mixer_setup_kernel(
@@ -223,11 +220,14 @@
             weigh[h] = decay * steps[:, h : h + 1]
 
 
-def upstream_kernel(moved, table, grad, state_out, head_l, total_l, upstream, resid_grad, state):
+def upstream_kernel(moved, shares, grad, state_out, head_l, total_l, upstream, resid_grad, state):
     width = grad.shape[1]
     groups = state_out.shape[1] // N
     span = width // groups
-    moe = dot(table[...], moved[...], 0, 0).astype(bf16)
+    moe = dot(shares[...], moved[0], 0, 0)
+    for c in range(1, moved.shape[0]):
+        moe = moe + dot(shares[...], moved[c], 0, 0)
+    moe = moe.astype(bf16)
     up = grad[...].astype(f32) + moe.astype(f32)
     upstream[...] = up
     resid_grad[...] = up.astype(bf16)
@@ -287,6 +287,18 @@
     return size
 
 
+def small(dims, dtype):
+    return math.prod(dims) * jnp.dtype(dtype).itemsize <= resident_bytes
+
+
+def in_vmem(x):
+    return pltpu.with_memory_space_constraint(x, pltpu.VMEM) if small(x.shape, x.dtype) else x
+
+
+def vmem_out(dims, dtype):
+    return pltpu.VMEM(dims, dtype) if small(dims, dtype) else jax.ShapeDtypeStruct(dims, dtype)
+
+
 def cost(flops, moved):
     return pl.CostEstimate(flops=flops, transcendentals=0, bytes_accessed=moved)
 
@@ -309,7 +321,6 @@
 ):
     ctx = lax.axis_size("ctx")
     peers = lax.axis_size("exp")
-    place = jnp.stack([lax.axis_index("ctx"), lax.axis_index("exp")]).astype(jnp.int32)
     experts = peers // 2
     token_rows, model = resid_input.shape
     tokens, width = grad_output.shape
@@ -346,16 +357,16 @@
         name="mixer_setup",
     )(log_retention.T, step_size.T, skip_gain.reshape(1, heads), state_input, state_output)
 
-    table, probs, rows_x = pl.pallas_call(
+    table, shares, rows_x = pl.pallas_call(
         partial(dispatch_kernel, experts=experts, capacity=capacity),
         out_shape=(
             shape((experts * capacity, tokens), bf16),
-            shape((experts * capacity, LANES), f32),
+            shape((experts * capacity, tokens), bf16),
             shape((ctx, experts * capacity, width), bf16),
         ),
         compiler_params=params(),
         name="dispatch",
-    )(packed.reshape(tokens, width + LANES))
+    )(in_vmem(packed.reshape(tokens, width + LANES)))
     rows_g = pl.pallas_call(
         select_kernel,
         out_shape=shape((ctx, experts * capacity, width), bf16),
@@ -380,68 +391,53 @@
     weight_spec = pl.BlockSpec((1, block, model), lambda i: (0, i, 0))
     act_spec = pl.BlockSpec((rows, block), lambda i: (0, i))
     product = 2 * rows * model * hidden
-    coef_gate, coef_up = pl.pallas_call(
+    coef_gate, coef_up, inverses = pl.pallas_call(
         gate_up_kernel,
         grid=(blocks,),
         in_specs=[whole(slab), whole(slab), whole((1, model)), weight_spec, weight_spec],
-        out_specs=[act_spec, act_spec],
-        out_shape=(shape((rows, hidden), f32), shape((rows, hidden), f32)),
+        out_specs=[act_spec, act_spec, whole((half, LANES))],
+        out_shape=(shape((rows, hidden), f32), shape((rows, hidden), f32), shape((half, LANES), f32)),
         scratch_shapes=[pltpu.VMEM((rows, model), bf16)],
         compiler_params=params(1),
         cost_estimate=cost(2 * product, 4 * model * hidden),
         name="gate_up",
-    )(own_x, other_x, gain, gate_weight, up_weight)
+    )(in_vmem(own_x), in_vmem(other_x), gain, gate_weight, up_weight)
     column = block_of(model, 512)
     columns = model // column
-    in_hbm = pl.BlockSpec(memory_space=pl.ANY)
-    in_vmem = pl.BlockSpec(memory_space=pltpu.VMEM)
+    any_spec = pl.BlockSpec(memory_space=pl.ANY)
+    vmem_spec = pl.BlockSpec(memory_space=pltpu.VMEM)
     out_own, out_other = pl.pallas_call(
         back_kernel,
-        in_specs=[in_vmem, in_vmem, in_vmem, in_vmem, in_hbm, in_hbm, in_hbm],
-        out_specs=[in_hbm, in_hbm],
-        out_shape=(shape((half, model), bf16), shape((half, model), bf16)),
+        in_specs=[vmem_spec, vmem_spec] + [any_spec] * 5,
+        out_specs=[vmem_spec, vmem_spec],
+        out_shape=(vmem_out((half, model), bf16), vmem_out((half, model), bf16)),
         scratch_shapes=[
             pltpu.VMEM((rows, model), bf16),
+            pltpu.VMEM((rows, hidden), f32),
+            pltpu.VMEM((rows, hidden), f32),
             pltpu.VMEM((rows, hidden), bf16),
             pltpu.VMEM((rows, hidden), bf16),
             pltpu.VMEM((blocks, block, model), bf16),
             pltpu.VMEM((columns, hidden, column), bf16),
             pltpu.VMEM((columns, hidden, column), bf16),
-            pltpu.VMEM((columns, rows, column), bf16),
-            pltpu.SemaphoreType.DMA((blocks + 2 * columns,)),
-            pltpu.SemaphoreType.DMA((2 * columns,)),
+            pltpu.SemaphoreType.DMA((blocks + 2 * columns + 2,)),
         ],
         compiler_params=params(),
         cost_estimate=cost(3 * product, 6 * model * hidden),
         name="back",
-    )(own_g, other_g, coef_gate, coef_up, gate_weight, up_weight, down_weight)
+    )(in_vmem(own_g), in_vmem(other_g), coef_gate, coef_up, gate_weight, up_weight, down_weight)
 
     swapped = lax.ppermute(out_other, "exp", partner)
-    summed = (out_own.astype(f32) + swapped.astype(f32)).astype(bf16)
-    parts = lax.all_to_all(
-        summed.reshape(ctx, slots, model), "ctx", split_axis=0, concat_axis=0, tiled=True
-    )
     moved = pl.pallas_call(
         slot_kernel,
-        grid_spec=pltpu.PrefetchScalarGridSpec(
-            num_scalar_prefetch=1,
-            grid=(1,),
-            in_specs=[
-                whole((ctx, slots, model)),
-                pl.BlockSpec((slots, LANES), lambda i, at: (at[1], 0)),
-                whole((1, model)),
-                pl.BlockSpec((1, peers, slots, width), lambda i, at: (at[0], 0, 0, 0)),
-            ],
-            out_specs=whole((peers, slots, width)),
-            scratch_shapes=[pltpu.VMEM((slots, model), f32)],
-        ),
-        out_shape=shape((peers, slots, width), bf16),
-        compiler_params=params(1),
+        out_shape=shape((ctx, peers, slots, width), bf16),
+        scratch_shapes=[pltpu.VMEM((half, model), f32)],
+        compiler_params=params(),
         name="slot",
-    )(place, parts, probs, gain, own_x)
-    moved = lax.all_to_all(moved, "exp", split_axis=0, concat_axis=0, tiled=True).reshape(
-        experts * capacity, width
-    )
+    )(in_vmem(out_own), in_vmem(swapped), gain, inverses, own_x)
+    moved = lax.all_to_all(
+        moved.reshape(ctx * peers, slots, width), ("ctx", "exp"), split_axis=0, concat_axis=0, tiled=True
+    ).reshape(ctx, experts * capacity, width)
 
     upstream, resid_grad, state = pl.pallas_call(
         upstream_kernel,
@@ -452,7 +448,7 @@
         ),
         compiler_params=params(),
         name="upstream",
-    )(moved, table, grad_output, state_output, head_l, total_l)
+    )(in_vmem(moved), shares, grad_output, state_output, head_l, total_l)
     states = [
         lax.ppermute(state, "ctx", [(i, i - k) for i in range(k, ctx)]) for k in range(1, ctx)
     ]
@@ -468,7 +464,7 @@
         out_shape=(shape((tokens, width), bf16), shape((tokens, groups * N), f32)),
         compiler_params=params(),
         name="mixer_far",
-    )(*states, base, local_b, mixer_input, state_input, tail_l)
+    )(*map(in_vmem, states), base, local_b, mixer_input, state_input, tail_l)
     return (resid_grad, mixer_grad, state_input_grad)
 
 

time: 187 us -> 166 us (0.89)
  waiting for transfers between devices: 91.5 us -> 86.6 us
  Pallas kernels: 55.4 us -> 50.7 us
  local copies, waits for them, and re-layouts: 4.36 us -> 0.01 us
  starting transfers between devices: 19.7 us -> 16 us
  other arithmetic: 3.07 us -> 0 us
    all_to_all x2 -> x1, waiting for transfers between devices: 29.9 us -> 23.3 us  [body(): lax.all_to_all(moved.reshape(ctx * peers, slots, width), ('ctx', 'exp'),...]
    unnamed x18 -> x2, local copies, waits for them, and re-layouts: 4.36 us -> 0.01 us
    all_to_all x2 -> x1, starting transfers between devices: 7.19 us -> 3.62 us  [body(): lax.all_to_all(moved.reshape(ctx * peers, slots, width), ('ctx', 'exp'),...]
    pallas_call x2, Pallas kernels: 23.7 us -> 20.7 us  [the longest x1 17.5 us: body(): pl.pallas_call(back_kernel, in_specs=[vmem_spec, vmem_spec] + [any_spec]...]
    convert_element_type x1 -> x0, other arithmetic: 2.48 us -> none  [body(): summed = (out_own.astype(f32) + swapped.astype(f32)).astype(bf16)]
    ppermute x3, waiting for transfers between devices: 9.1 us -> 11.1 us  [body(): lax.ppermute(state, 'ctx', [(i, i - k) for i in range(k, ctx)])]
  transfers between devices with their start and end apart: 10 -> 9, of which waited for: 7 -> 6; matrix products, arithmetic and copies ran while one was open for 0% -> 0% of each run, Pallas kernels for 12% -> 14%
where the time goes in v3:
time: 166 us; the launch traced here: 165 us
  waiting for transfers between devices  86.6 us (52%)
  Pallas kernels  50.7 us (31%)
  starting transfers between devices  16 us (10%)
  blocking collectives  11 us (7%)
    all_to_all x2, waiting for transfers between devices, spread(): lax.all_to_all(rows.reshape(ctx * peers, slots, width), ('ctx', 'exp'), s...  50 us
    all_to_all x1, waiting for transfers between devices, body(): lax.all_to_all(moved.reshape(ctx * peers, slots, width), ('ctx', 'exp'),...  23.3 us
    pallas_call x1, Pallas kernels, body(): pl.pallas_call(back_kernel, in_specs=[vmem_spec, vmem_spec] + [any_spec]...  17.5 us
    pallas_call x1, Pallas kernels, body(): pl.pallas_call(gate_up_kernel, grid=(blocks,), in_specs=[whole(slab), who...  14.6 us
    ppermute x3, waiting for transfers between devices, body(): lax.ppermute(state, 'ctx', [(i, i - k) for i in range(k, ctx)])  11.1 us
    all_to_all x1, blocking collectives, body(): lax.all_to_all(packed, 'exp', split_axis=0, concat_axis=0, tiled=True)  11 us
    all_to_all x2, starting transfers between devices, spread(): lax.all_to_all(rows.reshape(ctx * peers, slots, width), ('ctx', 'exp'), s...  7.59 us
    ppermute x3, starting transfers between devices, body(): lax.ppermute(state, 'ctx', [(i, i - k) for i in range(k, ctx)])  3.86 us
  transfers between devices with their start and end apart: 9, of which 6 were waited for; matrix products, arithmetic and copies ran while one was open for 0% of the time, Pallas kernels for 14%

profile of v3, /device:TPU:0, one launch (start us, length us, event | category | flops | bytes accessed | tf_op | source)
XLA Modules:
  0.0 165.1 jit_solution(7783890874438584491)
XLA Ops:
  0.6 1.8 %pack.1 = bf16[8,16,640]{2,1,0:T(8,128)(2,1)} custom-call(bf16[16,4096]{1,0:T(8,128)(2,1)} %resid.1, s32[2,16]{1,0:T(2,128)} %bitcast.25, bf16[2,16]{1,0:T(2,128)(2,1)} %bitcast.26), custom_call_target="tpu_custom_call" | custom-call | tf_op jit(solution)/shard_map/pack/pallas_call | solution.py:336
  2.4 11.0 %all_to_all.20 = bf16[8,16,640]{2,1,0:T(8,128)(2,1)S(1)} all-to-all(bf16[8,16,640]{2,1,0:T(8,128)(2,1)} %pack.1), channel_id=1, replica_groups=mesh['ctx'=4,'exp'=8] {'exp'}, dimensions={0} | all-to-all | bytes 327680 | tf_op jit(solution)/shard_map/all_to_all | solution.py:342
  13.5 1.5 dispatch.1
  14.9 4.0 %all-to-all-start.2 = ((bf16[32,32,512]{2,1,0:T(8,128)(2,1)}), bf16[32,32,512]{2,1,0:T(8,128)(2,1)S(1)}, u32[]{:S(2)}, u32[]{:S(2)}) async-start(bf16[32,32,512]{2,1,0:T(8,128)(2,1)} %bitcast.22), calls=%async_computation.2 | async-start | bytes 2097152 | tf_op jit(solution)/shard_map/all_to_all | solution.py:379
  18.9 2.1 %select.1 = bf16[4,256,512]{2,1,0:T(8,128)(2,1)} custom-call(bf16[256,128]{1,0:T(8,128)(2,1)} %get-tuple-element.25.table, bf16[128,512]{1,0:T(8,128)(2,1)} %grad.3), custom_call_target="tpu_custom_call" | custom-call | flops 1000000000 | bytes 2000000 | tf_op jit(solution)/shard_map/select/pallas_call | solution.py:370
  21.0 24.1 %all-to-all-done.2 = bf16[32,32,512]{2,1,0:T(8,128)(2,1)S(1)} async-done(((bf16[32,32,512]{2,1,0:T(8,128)(2,1)}), bf16[32,32,512]{2,1,0:T(8,128)(2,1)S(1)}, u32[]{:S(2)}, u32[]{:S(2)}) %all-to-all-start.2) | async-done | bytes 1048608 | tf_op jit(solution)/shard_map/all_to_all | solution.py:379
  45.1 3.6 %all-to-all-start.1 = ((bf16[32,32,512]{2,1,0:T(8,128)(2,1)}), bf16[32,32,512]{2,1,0:T(8,128)(2,1)S(1)}, u32[]{:S(2)}, u32[]{:S(2)}) async-start(bf16[32,32,512]{2,1,0:T(8,128)(2,1)} %bitcast.21), calls=%async_computation.1 | async-start | bytes 2097152 | tf_op jit(solution)/shard_map/all_to_all | solution.py:379
  49.0 25.9 %all-to-all-done.1 = bf16[32,32,512]{2,1,0:T(8,128)(2,1)S(1)} async-done(((bf16[32,32,512]{2,1,0:T(8,128)(2,1)}), bf16[32,32,512]{2,1,0:T(8,128)(2,1)S(1)}, u32[]{:S(2)}, u32[]{:S(2)}) %all-to-all-start.1) | async-done | bytes 1048608 | tf_op jit(solution)/shard_map/all_to_all | solution.py:379
  74.9 14.6 %gate_up.1 = (f32[256,1536]{1,0:T(8,128)}, f32[256,1536]{1,0:T(8,128)}, f32[128,128]{1,0:T(8,128)}) custom-call(bf16[4,8,32,512]{3,2,1,0:T(8,128)(2,1)S(1)} %bitcast.14, bf16[4,8,32,512]{3,2,1,0:T(8,128)(2,1)S(1)} %collective-permute-done.1.other, f32[1,4096]{1,0:T(1,128)} %bitcast.23, bf16[1,1536,4096]{2,1,0:T(8,128)(2,1)} %gate_hbm.1, ...), custom_call_target="tpu_custom_call" | custom-call | flops 6442450944 | bytes 25165824 | tf_op jit(solution)/shard_map/gate_up/pallas_call | solution.py:394
  89.6 17.5 %back.1 = (bf16[128,4096]{1,0:T(8,128)(2,1)S(1)}, bf16[128,4096]{1,0:T(8,128)(2,1)S(1)}) custom-call(bf16[4,8,32,512]{3,2,1,0:T(8,128)(2,1)S(1)} %bitcast.18, bf16[4,8,32,512]{3,2,1,0:T(8,128)(2,1)S(1)} %collective-permute-done.other, f32[256,1536]{1,0:T(8,128)} %get-tuple-element.27.coef_gate_hbm, f32[256,1536]{1,0:T(8,128)} %get-tuple-element.28.coef_up_hbm, ...), custom_call_target="tpu_custom_call" | custom-call | flops 9663676416 | bytes 37748736 | tf_op jit(solution)/shard_map/back/pallas_call | solution.py:409
  107.1 0.6 collective-permute-start.2
  107.7 2.3 %collective-permute-done.2.swapped = bf16[128,4096]{1,0:T(8,128)(2,1)S(1)} collective-permute-done((bf16[128,4096]{1,0:T(8,128)(2,1)S(1)}, bf16[128,4096]{1,0:T(8,128)(2,1)S(1)}, u32[]{:S(2)}, u32[]{:S(2)}) %collective-permute-start.2) | collective-permute-done | bytes 1048608 | tf_op jit(solution)/shard_map/ppermute | solution.py:430
  110.0 3.2 %slot.1 = bf16[4,8,32,512]{3,2,1,0:T(8,128)(2,1)} custom-call(bf16[128,4096]{1,0:T(8,128)(2,1)S(1)} %get-tuple-element.29.own, bf16[128,4096]{1,0:T(8,128)(2,1)S(1)} %collective-permute-done.2.swapped, f32[1,4096]{1,0:T(1,128)} %bitcast.24, f32[128,128]{1,0:T(8,128)} %get-tuple-element.31.inverses, bf16[4,8,32,512]{3,2,1,0:T(8,128)(2,1)} %bitcast.15), custom_call_target="tpu_custom_call" | custom-call | tf_op jit(solution)/shard_map/slot/pallas_call | solution.py:431
  113.2 3.6 %all-to-all-start.3 = ((bf16[32,32,512]{2,1,0:T(8,128)(2,1)}), bf16[32,32,512]{2,1,0:T(8,128)(2,1)S(1)}, u32[]{:S(2)}, u32[]{:S(2)}) async-start(bf16[32,32,512]{2,1,0:T(8,128)(2,1)} %bitcast.20), calls=%async_computation.3 | async-start | bytes 2097152 | tf_op jit(solution)/shard_map/all_to_all | solution.py:438
  116.8 2.9 %mixer_setup.1 = (bf16[8,128,128]{2,1,0:T(8,128)(2,1)}, f32[8,128,128]{2,1,0:T(8,128)}, f32[128,512]{1,0:T(8,128)}, f32[128,512]{1,0:T(8,128)}, f32[128,512]{1,0...) custom-call(f32[8,128]{1,0:T(8,128)} %bitcast.27, f32[8,128]{1,0:T(8,128)} %bitcast.28, f32[1,8]{1,0:T(1,128)} %bitcast.29, ...), custom_call_target="tpu_custom_call" | custom-call | flops 2000000000 | bytes 2000000 | tf_op jit(solution)/shard_map/mixer_setup/pallas_call | solution.py:344
  119.7 23.3 %all-to-all-done.3 = bf16[32,32,512]{2,1,0:T(8,128)(2,1)S(1)} async-done(((bf16[32,32,512]{2,1,0:T(8,128)(2,1)}), bf16[32,32,512]{2,1,0:T(8,128)(2,1)S(1)}, u32[]{:S(2)}, u32[]{:S(2)}) %all-to-all-start.3) | async-done | bytes 1048608 | tf_op jit(solution)/shard_map/all_to_all | solution.py:438
  143.0 2.2 %upstream.1 = (f32[128,512]{1,0:T(8,128)}, bf16[128,512]{1,0:T(8,128)(2,1)}, bf16[144,512]{1,0:T(8,128)(2,1)}) custom-call(bf16[4,256,512]{2,1,0:T(8,128)(2,1)S(1)} %bitcast.16, bf16[256,128]{1,0:T(8,128)(2,1)} %get-tuple-element.32.shares, bf16[128,512]{1,0:T(8,128)(2,1)} %grad.3, bf16[128,256]{1,0:T(8,128)(2,1)} %state_out.5, ...), custom_call_target="tpu_custom_call" | custom-call | tf_op jit(solution)/shard_map/upstream/pallas_call | solution.py:442
  145.2 1.3 collective-permute-start.3
  146.5 1.3 collective-permute-start.4
  147.8 1.3 collective-permute-start.5
  149.1 2.8 %mixer_local.1 = (f32[128,512]{1,0:T(8,128)}, f32[128,256]{1,0:T(8,128)}) custom-call(f32[128,512]{1,0:T(8,128)} %get-tuple-element.37.upstream, bf16[128,512]{1,0:T(8,128)(2,1)} %get-tuple-element.22.resid_grad, bf16[128,512]{1,0:T(8,128)(2,1)} %refs_5_.1, bf16[128,256]{1,0:T(8,128)(2,1)} %state_out.5, bf16[8,128,128]{2,1,0:T(8,128)(2,1)} %get-tuple-element.38.mix, ...), custom_call_target="tpu_custom_call" | custom-call | flops 3000000000 | bytes 2000000 | tf_op jit(solution)/shard_map/mixer_local/pallas_call | solution.py:455
  151.9 0.6 collective-permute-done.3.refs_0_
  152.4 10.5 %collective-permute-done.4.refs_1_ = bf16[144,512]{1,0:T(8,128)(2,1)S(1)} collective-permute-done((bf16[144,512]{1,0:T(8,128)(2,1)}, bf16[144,512]{1,0:T(8,128)(2,1)S(1)}, u32[]{:S(2)}, u32[]{:S(2)}) %collective-permute-start.4) | collective-permute-done | bytes 147488 | tf_op jit(solution)/shard_map/ppermute | solution.py:453
  162.9 2.1 %mixer_far.1 = (bf16[128,512]{1,0:T(8,128)(2,1)}, f32[128,256]{1,0:T(8,128)}) custom-call(bf16[144,512]{1,0:T(8,128)(2,1)S(1)} %collective-permute-done.3.refs_0_, bf16[144,512]{1,0:T(8,128)(2,1)S(1)} %collective-permute-done.4.refs_1_, bf16[144,512]{1,0:T(8,128)(2,1)S(1)} %collective-permute-done.5.refs_2_, f32[128,512]{1,0:T(8,128)} %get-tuple-element.42.refs_3_, ...), custom_call_target="tpu_custom_call" | custom-call | tf_op jit(solution)/shard_map/mixer_far/pallas_call | solution.py:462
  (7 shorter events, 0.3 us)
Async XLA Ops:
  14.9 30.2 %all-to-all-start.2 = ((bf16[32,32,512]{2,1,0:T(8,128)(2,1)}), bf16[32,32,512]{2,1,0:T(8,128)(2,1)S(1)}, u32[]{:S(2)}, u32[]{:S(2)}) async-start(bf16[32,32,512]{2,1,0:T(8,128)(2,1)} %bitcast.22), calls=%async_computation.2 | async-start | bytes 2097152 | tf_op jit(solution)/shard_map/all_to_all | solution.py:379
  45.1 44.5 %copy-start = (bf16[32,32,512]{2,1,0:T(8,128)(2,1)}, bf16[32,32,512]{2,1,0:T(8,128)(2,1)S(1)}, u32[]{:S(2)}) copy-start(bf16[32,32,512]{2,1,0:T(8,128)(2,1)S(1)} %all-to-all-done.2) | copy-start | bytes 3145732
  45.1 29.8 %all-to-all-start.1 = ((bf16[32,32,512]{2,1,0:T(8,128)(2,1)}), bf16[32,32,512]{2,1,0:T(8,128)(2,1)S(1)}, u32[]{:S(2)}, u32[]{:S(2)}) async-start(bf16[32,32,512]{2,1,0:T(8,128)(2,1)} %bitcast.21), calls=%async_computation.1 | async-start | bytes 2097152 | tf_op jit(solution)/shard_map/all_to_all | solution.py:379
  48.7 26.2 %collective-permute-start.1 = (bf16[4,8,32,512]{3,2,1,0:T(8,128)(2,1)S(1)}, bf16[4,8,32,512]{3,2,1,0:T(8,128)(2,1)S(1)}, u32[]{:S(2)}, u32[]{:S(2)}) collective-permute-start(bf16[4,8,32,512]{3,2,1,0:T(8,128)(2,1)S(1)} %bitcast.13), channel_id=1, source_target_pairs={{0,1},{1,0},{2,3},{3,2},{4,5},{5,4},{6,7},{7,6},{8,9},{9,8},{10,11... | collective-permute-start | bytes 3145736 | tf_op jit(solution)/shard_map/ppermute | solution.py:382
  74.9 14.7 %collective-permute-start = (bf16[4,8,32,512]{3,2,1,0:T(8,128)(2,1)S(1)}, bf16[4,8,32,512]{3,2,1,0:T(8,128)(2,1)S(1)}, u32[]{:S(2)}, u32[]{:S(2)}) collective-permute-start(bf16[4,8,32,512]{3,2,1,0:T(8,128)(2,1)S(1)} %bitcast.17), channel_id=1, source_target_pairs={{0,1},{1,0},{2,3},{3,2},{4,5},{5,4},{6,7},{7,6},{8,9},{9,8},{10,11... | collective-permute-start | bytes 3145736 | tf_op jit(solution)/shard_map/ppermute | solution.py:382
  107.1 2.9 %collective-permute-start.2 = (bf16[128,4096]{1,0:T(8,128)(2,1)S(1)}, bf16[128,4096]{1,0:T(8,128)(2,1)S(1)}, u32[]{:S(2)}, u32[]{:S(2)}) collective-permute-start(bf16[128,4096]{1,0:T(8,128)(2,1)S(1)} %get-tuple-element.30), channel_id=1, source_target_pairs={{0,1},{1,0},{2,3},{3,2},{4,5},{5,4},{6,7},{7,6},{8,9},{9,8},{10,11... | collective-permute-start | bytes 3145736 | tf_op jit(solution)/shard_map/ppermute | solution.py:430
  113.2 29.8 %all-to-all-start.3 = ((bf16[32,32,512]{2,1,0:T(8,128)(2,1)}), bf16[32,32,512]{2,1,0:T(8,128)(2,1)S(1)}, u32[]{:S(2)}, u32[]{:S(2)}) async-start(bf16[32,32,512]{2,1,0:T(8,128)(2,1)} %bitcast.20), calls=%async_computation.3 | async-start | bytes 2097152 | tf_op jit(solution)/shard_map/all_to_all | solution.py:438
  145.2 7.2 %collective-permute-start.3 = (bf16[144,512]{1,0:T(8,128)(2,1)}, bf16[144,512]{1,0:T(8,128)(2,1)S(1)}, u32[]{:S(2)}, u32[]{:S(2)}) collective-permute-start(bf16[144,512]{1,0:T(8,128)(2,1)} %get-tuple-element.36), channel_id=1, source_target_pairs={{8,0},{16,8},{24,16},{9,1},{17,9},{25,17},{10,2},{18,10},{26,18},{... | collective-permute-start | bytes 442376 | tf_op jit(solution)/shard_map/ppermute | solution.py:453
  146.5 16.4 %collective-permute-start.4 = (bf16[144,512]{1,0:T(8,128)(2,1)}, bf16[144,512]{1,0:T(8,128)(2,1)S(1)}, u32[]{:S(2)}, u32[]{:S(2)}) collective-permute-start(bf16[144,512]{1,0:T(8,128)(2,1)} %get-tuple-element.36), channel_id=1, source_target_pairs={{16,0},{24,8},{17,1},{25,9},{18,2},{26,10},{19,3},{27,11},{20,4},{... | collective-permute-start | bytes 442376 | tf_op jit(solution)/shard_map/ppermute | solution.py:453
  147.8 15.2 %collective-permute-start.5 = (bf16[144,512]{1,0:T(8,128)(2,1)}, bf16[144,512]{1,0:T(8,128)(2,1)S(1)}, u32[]{:S(2)}, u32[]{:S(2)}) collective-permute-start(bf16[144,512]{1,0:T(8,128)(2,1)} %get-tuple-element.36), channel_id=1, source_target_pairs={{24,0},{25,1},{26,2},{27,3},{28,4},{29,5},{30,6},{31,7}} | collective-permute-start | bytes 442376 | tf_op jit(solution)/shard_map/ppermute | solution.py:453

commit v4 on v3

--- a/solution.py
+++ b/solution.py
@@ -19,10 +19,8 @@
 resident_bytes = 1024 * 1024
 
 
-def params(steps=0):
-    return pltpu.CompilerParams(
-        dimension_semantics=("arbitrary",) * steps, vmem_limit_bytes=vmem_bytes
-    )
+def params(steps=0, limit=vmem_bytes):
+    return pltpu.CompilerParams(dimension_semantics=("arbitrary",) * steps, vmem_limit_bytes=limit)
 
 
 def whole(shape):
@@ -237,10 +235,8 @@
         scaled = (up[:, wide] * head_l[:, wide]).astype(bf16)
         state[0:N, wide] = dot(state_out[:, cols], scaled, 0, 0).astype(bf16)
     total = total_l[...]
-    high = total.astype(bf16)
-    low = (total - high.astype(f32)).astype(bf16)
-    state[N : N + 8, :] = high
-    state[N + 8 : N + 16, :] = low
+    high = total.astype(bf16).astype(f32)
+    state[N : N + 8, :] = jnp.where(iota(total.shape, 0) == 0, high, total - high).astype(bf16)
 
 
 def mixer_local_kernel(upstream, resid_grad, mixer, state_out, mix, weigh, step_l, skip_l, base, local_b):
@@ -268,7 +264,7 @@
     span = width // groups
     incoming = states[-1][0:N, :].astype(f32)
     for ref in states[-2::-1]:
-        decay = ref[N : N + 1, :].astype(f32) + ref[N + 8 : N + 9, :].astype(f32)
+        decay = ref[N : N + 1, :].astype(f32) + ref[N + 1 : N + 2, :].astype(f32)
         incoming = ref[0:N, :].astype(f32) + decay * incoming
     incoming = incoming.astype(bf16)
     for g in range(groups):
@@ -335,7 +331,7 @@
 
     packed = pl.pallas_call(
         pack_kernel,
-        out_shape=shape((peers, token_rows, width + LANES), bf16),
+        out_shape=vmem_out((peers, token_rows, width + LANES), bf16),
         compiler_params=params(),
         name="pack",
     )(resid_input, expert_ids.T, route_probs.T)
@@ -362,7 +358,7 @@
         out_shape=(
             shape((experts * capacity, tokens), bf16),
             shape((experts * capacity, tokens), bf16),
-            shape((ctx, experts * capacity, width), bf16),
+            vmem_out((ctx, experts * capacity, width), bf16),
         ),
         compiler_params=params(),
         name="dispatch",
@@ -430,11 +426,11 @@
     swapped = lax.ppermute(out_other, "exp", partner)
     moved = pl.pallas_call(
         slot_kernel,
-        out_shape=shape((ctx, peers, slots, width), bf16),
+        out_shape=vmem_out((ctx, peers, slots, width), bf16),
         scratch_shapes=[pltpu.VMEM((half, model), f32)],
         compiler_params=params(),
         name="slot",
-    )(in_vmem(out_own), in_vmem(swapped), gain, inverses, own_x)
+    )(in_vmem(out_own), in_vmem(swapped), gain, in_vmem(inverses), in_vmem(own_x))
     moved = lax.all_to_all(
         moved.reshape(ctx * peers, slots, width), ("ctx", "exp"), split_axis=0, concat_axis=0, tiled=True
     ).reshape(ctx, experts * capacity, width)
@@ -442,29 +438,29 @@
     upstream, resid_grad, state = pl.pallas_call(
         upstream_kernel,
         out_shape=(
-            shape((tokens, width), f32),
-            shape((tokens, width), bf16),
-            shape((N + 16, width), bf16),
+            vmem_out((tokens, width), f32),
+            vmem_out((tokens, width), bf16),
+            vmem_out((N + 8, width), bf16),
         ),
         compiler_params=params(),
         name="upstream",
-    )(in_vmem(moved), shares, grad_output, state_output, head_l, total_l)
+    )(*map(in_vmem, (moved, shares, grad_output, state_output, head_l, total_l)))
     states = [
         lax.ppermute(state, "ctx", [(i, i - k) for i in range(k, ctx)]) for k in range(1, ctx)
     ]
     base, local_b = pl.pallas_call(
         mixer_local_kernel,
-        out_shape=(shape((tokens, width), f32), shape((tokens, groups * N), f32)),
+        out_shape=(vmem_out((tokens, width), f32), vmem_out((tokens, groups * N), f32)),
         compiler_params=params(),
         cost_estimate=cost(3 * 10**9, 2 * 10**6),
         name="mixer_local",
-    )(upstream, resid_grad, mixer_input, state_output, mix, weigh, step_l, skip_l)
+    )(*map(in_vmem, (upstream, resid_grad, mixer_input, state_output, mix, weigh, step_l, skip_l)))
     mixer_grad, state_input_grad = pl.pallas_call(
         mixer_far_kernel,
         out_shape=(shape((tokens, width), bf16), shape((tokens, groups * N), f32)),
         compiler_params=params(),
         name="mixer_far",
-    )(*map(in_vmem, states), base, local_b, mixer_input, state_input, tail_l)
+    )(*map(in_vmem, (*states, base, local_b, mixer_input, state_input, tail_l)))
     return (resid_grad, mixer_grad, state_input_grad)
 
 

time: 166 us -> 163 us (0.982)
  Pallas kernels: 50.7 us -> 44.6 us
  local copies, waits for them, and re-layouts: 0.01 us -> 6.01 us
  waiting for transfers between devices: 86.6 us -> 83.5 us
    unnamed x2 -> x27, local copies, waits for them, and re-layouts: 0.01 us -> 6.01 us
    pallas_call x4, Pallas kernels: 9.91 us -> 4.97 us  [the longest x1 2.65 us: body(): pl.pallas_call(slot_kernel, out_shape=vmem_out((ctx, peers, slots, width)...]
    ppermute x3, waiting for transfers between devices: 11.1 us -> 7.92 us  [body(): lax.ppermute(state, 'ctx', [(i, i - k) for i in range(k, ctx)])]
  transfers between devices with their start and end apart: 9 -> 9, of which waited for: 6 -> 5; matrix products, arithmetic and copies ran while one was open for 0% -> 0% of each run, Pallas kernels for 14% -> 13%
where the time goes in v4:
time: 163 us; the launch traced here: 162 us
  waiting for transfers between devices  83.5 us (51%)
  Pallas kernels  44.6 us (27%)
  starting transfers between devices  16 us (10%)
  blocking collectives  10.8 us (7%)
  local copies, waits for them, and re-layouts  6.01 us (4%)
    all_to_all x2, waiting for transfers between devices, spread(): lax.all_to_all(rows.reshape(ctx * peers, slots, width), ('ctx', 'exp'), s...  50 us
    all_to_all x1, waiting for transfers between devices, body(): lax.all_to_all(moved.reshape(ctx * peers, slots, width), ('ctx', 'exp'),...  23.3 us
    pallas_call x1, Pallas kernels, body(): pl.pallas_call(back_kernel, in_specs=[vmem_spec, vmem_spec] + [any_spec]...  17.6 us
    pallas_call x1, Pallas kernels, body(): pl.pallas_call(gate_up_kernel, grid=(blocks,), in_specs=[whole(slab), who...  14.6 us
    all_to_all x1, blocking collectives, body(): lax.all_to_all(packed, 'exp', split_axis=0, concat_axis=0, tiled=True)  10.8 us
    ppermute x3, waiting for transfers between devices, body(): lax.ppermute(state, 'ctx', [(i, i - k) for i in range(k, ctx)])  7.92 us
    all_to_all x2, starting transfers between devices, spread(): lax.all_to_all(rows.reshape(ctx * peers, slots, width), ('ctx', 'exp'), s...  7.59 us
    unnamed x27, local copies, waits for them, and re-layouts  6.01 us
  transfers between devices with their start and end apart: 9, of which 5 were waited for; matrix products, arithmetic and copies ran while one was open for 0% of the time, Pallas kernels for 13%

profile of v4, /device:TPU:0, one launch (start us, length us, event | category | flops | bytes accessed | tf_op | source)
XLA Modules:
  0.0 161.7 jit_solution(14046463554166784345)
XLA Ops:
  0.6 1.1 pack.1
  1.8 10.8 %all_to_all.20 = bf16[8,16,640]{2,1,0:T(8,128)(2,1)S(1)} all-to-all(bf16[8,16,640]{2,1,0:T(8,128)(2,1)S(1)} %pack.1), channel_id=1, replica_groups=mesh['ctx'=4,'exp'=8] {'exp'}, dimensions={0} | all-to-all | bytes 327680 | tf_op jit(solution)/shard_map/all_to_all | solution.py:338
  12.6 1.5 dispatch.1
  14.1 4.0 %all-to-all-start.2 = ((bf16[32,32,512]{2,1,0:T(8,128)(2,1)}), bf16[32,32,512]{2,1,0:T(8,128)(2,1)S(1)}, u32[]{:S(2)}, u32[]{:S(2)}) async-start(bf16[32,32,512]{2,1,0:T(8,128)(2,1)} %bitcast.5), calls=%async_computation.2 | async-start | bytes 2097152 | tf_op jit(solution)/shard_map/all_to_all | solution.py:375
  18.0 2.1 %select.1 = bf16[4,256,512]{2,1,0:T(8,128)(2,1)} custom-call(bf16[256,128]{1,0:T(8,128)(2,1)} %get-tuple-element.25.table, bf16[128,512]{1,0:T(8,128)(2,1)} %grad.3), custom_call_target="tpu_custom_call" | custom-call | flops 1000000000 | bytes 2000000 | tf_op jit(solution)/shard_map/select/pallas_call | solution.py:366
  20.2 24.1 %all-to-all-done.2 = bf16[32,32,512]{2,1,0:T(8,128)(2,1)S(1)} async-done(((bf16[32,32,512]{2,1,0:T(8,128)(2,1)}), bf16[32,32,512]{2,1,0:T(8,128)(2,1)S(1)}, u32[]{:S(2)}, u32[]{:S(2)}) %all-to-all-start.2) | async-done | bytes 1048608 | tf_op jit(solution)/shard_map/all_to_all | solution.py:375
  44.2 3.6 %all-to-all-start.1 = ((bf16[32,32,512]{2,1,0:T(8,128)(2,1)}), bf16[32,32,512]{2,1,0:T(8,128)(2,1)S(1)}, u32[]{:S(2)}, u32[]{:S(2)}) async-start(bf16[32,32,512]{2,1,0:T(8,128)(2,1)} %bitcast.20), calls=%async_computation.1 | async-start | bytes 2097152 | tf_op jit(solution)/shard_map/all_to_all | solution.py:375
  48.2 25.9 %all-to-all-done.1 = bf16[32,32,512]{2,1,0:T(8,128)(2,1)S(1)} async-done(((bf16[32,32,512]{2,1,0:T(8,128)(2,1)}), bf16[32,32,512]{2,1,0:T(8,128)(2,1)S(1)}, u32[]{:S(2)}, u32[]{:S(2)}) %all-to-all-start.1) | async-done | bytes 1048608 | tf_op jit(solution)/shard_map/all_to_all | solution.py:375
  74.1 14.6 %gate_up.1 = (f32[256,1536]{1,0:T(8,128)}, f32[256,1536]{1,0:T(8,128)}, f32[128,128]{1,0:T(8,128)}) custom-call(bf16[4,8,32,512]{3,2,1,0:T(8,128)(2,1)S(1)} %bitcast.14, bf16[4,8,32,512]{3,2,1,0:T(8,128)(2,1)S(1)} %collective-permute-done.1.other, f32[1,4096]{1,0:T(1,128)} %bitcast.21, bf16[1,1536,4096]{2,1,0:T(8,128)(2,1)} %gate_hbm.1, ...), custom_call_target="tpu_custom_call" | custom-call | flops 6442450944 | bytes 25165824 | tf_op jit(solution)/shard_map/gate_up/pallas_call | solution.py:390
  88.8 17.6 %back.1 = (bf16[128,4096]{1,0:T(8,128)(2,1)S(1)}, bf16[128,4096]{1,0:T(8,128)(2,1)S(1)}) custom-call(bf16[4,8,32,512]{3,2,1,0:T(8,128)(2,1)S(1)} %bitcast.18, bf16[4,8,32,512]{3,2,1,0:T(8,128)(2,1)S(1)} %collective-permute-done.other, f32[256,1536]{1,0:T(8,128)} %get-tuple-element.27.coef_gate_hbm, f32[256,1536]{1,0:T(8,128)} %get-tuple-element.28.coef_up_hbm, ...), custom_call_target="tpu_custom_call" | custom-call | flops 9663676416 | bytes 37748736 | tf_op jit(solution)/shard_map/back/pallas_call | solution.py:405
  106.9 2.3 %collective-permute-done.2.swapped = bf16[128,4096]{1,0:T(8,128)(2,1)S(1)} collective-permute-done((bf16[128,4096]{1,0:T(8,128)(2,1)S(1)}, bf16[128,4096]{1,0:T(8,128)(2,1)S(1)}, u32[]{:S(2)}, u32[]{:S(2)}) %collective-permute-start.2) | collective-permute-done | bytes 1048608 | tf_op jit(solution)/shard_map/ppermute | solution.py:426
  109.2 2.7 %slot.1 = bf16[4,8,32,512]{3,2,1,0:T(8,128)(2,1)} custom-call(bf16[128,4096]{1,0:T(8,128)(2,1)S(1)} %get-tuple-element.29.own, bf16[128,4096]{1,0:T(8,128)(2,1)S(1)} %collective-permute-done.2.swapped, f32[1,4096]{1,0:T(1,128)} %bitcast.22, f32[128,128]{1,0:T(8,128)S(1)} %copy-done.4, bf16[4,8,32,512]{3,2,1,0:T(8,128)(2,1)S(1)} %bitcast.15), custom_call_target="tpu_custom_call" | custom-call | tf_op jit(solution)/shard_map/slot/pallas_call | solution.py:427
  111.9 3.6 %all-to-all-start.3 = ((bf16[32,32,512]{2,1,0:T(8,128)(2,1)}), bf16[32,32,512]{2,1,0:T(8,128)(2,1)S(1)}, u32[]{:S(2)}, u32[]{:S(2)}) async-start(bf16[32,32,512]{2,1,0:T(8,128)(2,1)} %bitcast.8), calls=%async_computation.3 | async-start | bytes 2097152 | tf_op jit(solution)/shard_map/all_to_all | solution.py:434
  115.5 2.9 %mixer_setup.1 = (bf16[8,128,128]{2,1,0:T(8,128)(2,1)}, f32[8,128,128]{2,1,0:T(8,128)}, f32[128,512]{1,0:T(8,128)}, f32[128,512]{1,0:T(8,128)}, f32[128,512]{1,0...) custom-call(f32[8,128]{1,0:T(8,128)} %bitcast.25, f32[8,128]{1,0:T(8,128)} %bitcast.26, f32[1,8]{1,0:T(1,128)} %bitcast.27, ...), custom_call_target="tpu_custom_call" | custom-call | flops 2000000000 | bytes 2000000 | tf_op jit(solution)/shard_map/mixer_setup/pallas_call | solution.py:340
  118.4 23.3 %all-to-all-done.3 = bf16[32,32,512]{2,1,0:T(8,128)(2,1)S(1)} async-done(((bf16[32,32,512]{2,1,0:T(8,128)(2,1)}), bf16[32,32,512]{2,1,0:T(8,128)(2,1)S(1)}, u32[]{:S(2)}, u32[]{:S(2)}) %all-to-all-start.3) | async-done | bytes 1048608 | tf_op jit(solution)/shard_map/all_to_all | solution.py:434
  141.7 0.9 copy-done.1
  143.9 1.3 collective-permute-start.3
  145.2 1.3 collective-permute-start.4
  146.5 1.3 collective-permute-start.5
  147.8 1.0 copy-done.9
  148.9 0.9 copy-done.10
  149.8 0.9 copy-done.11
  152.8 7.9 %collective-permute-done.4.refs_1_ = bf16[136,512]{1,0:T(8,128)(2,1)S(1)} collective-permute-done((bf16[136,512]{1,0:T(8,128)(2,1)S(1)}, bf16[136,512]{1,0:T(8,128)(2,1)S(1)}, u32[]{:S(2)}, u32[]{:S(2)}) %collective-permute-start.4) | collective-permute-done | bytes 139296 | tf_op jit(solution)/shard_map/ppermute | solution.py:449
  160.8 0.9 mixer_far.1
  (32 shorter events, 4.2 us)
Async XLA Ops:
  14.1 30.2 %all-to-all-start.2 = ((bf16[32,32,512]{2,1,0:T(8,128)(2,1)}), bf16[32,32,512]{2,1,0:T(8,128)(2,1)S(1)}, u32[]{:S(2)}, u32[]{:S(2)}) async-start(bf16[32,32,512]{2,1,0:T(8,128)(2,1)} %bitcast.5), calls=%async_computation.2 | async-start | bytes 2097152 | tf_op jit(solution)/shard_map/all_to_all | solution.py:375
  44.2 29.8 %all-to-all-start.1 = ((bf16[32,32,512]{2,1,0:T(8,128)(2,1)}), bf16[32,32,512]{2,1,0:T(8,128)(2,1)S(1)}, u32[]{:S(2)}, u32[]{:S(2)}) async-start(bf16[32,32,512]{2,1,0:T(8,128)(2,1)} %bitcast.20), calls=%async_computation.1 | async-start | bytes 2097152 | tf_op jit(solution)/shard_map/all_to_all | solution.py:375
  47.9 26.2 %collective-permute-start.1 = (bf16[4,8,32,512]{3,2,1,0:T(8,128)(2,1)S(1)}, bf16[4,8,32,512]{3,2,1,0:T(8,128)(2,1)S(1)}, u32[]{:S(2)}, u32[]{:S(2)}) collective-permute-start(bf16[4,8,32,512]{3,2,1,0:T(8,128)(2,1)S(1)} %bitcast.13), channel_id=1, source_target_pairs={{0,1},{1,0},{2,3},{3,2},{4,5},{5,4},{6,7},{7,6},{8,9},{9,8},{10,11... | collective-permute-start | bytes 3145736 | tf_op jit(solution)/shard_map/ppermute | solution.py:378
  74.1 14.7 %collective-permute-start = (bf16[4,8,32,512]{3,2,1,0:T(8,128)(2,1)S(1)}, bf16[4,8,32,512]{3,2,1,0:T(8,128)(2,1)S(1)}, u32[]{:S(2)}, u32[]{:S(2)}) collective-permute-start(bf16[4,8,32,512]{3,2,1,0:T(8,128)(2,1)S(1)} %bitcast.17), channel_id=1, source_target_pairs={{0,1},{1,0},{2,3},{3,2},{4,5},{5,4},{6,7},{7,6},{8,9},{9,8},{10,11... | collective-permute-start | bytes 3145736 | tf_op jit(solution)/shard_map/ppermute | solution.py:378
  88.7 20.5 %copy-start.4 = (f32[128,128]{1,0:T(8,128)S(1)}, f32[128,128]{1,0:T(8,128)}, u32[]{:S(2)}) copy-start(f32[128,128]{1,0:T(8,128)} %get-tuple-element.31.inverses) | copy-start | bytes 196612
  106.3 35.4 %copy-start.2 = (bf16[128,512]{1,0:T(8,128)(2,1)S(1)}, bf16[128,512]{1,0:T(8,128)(2,1)}, u32[]{:S(2)}) copy-start(bf16[128,512]{1,0:T(8,128)(2,1)} %grad.3) | copy-start | bytes 393220
  106.3 35.4 %copy-start.5 = (bf16[128,256]{1,0:T(8,128)(2,1)S(1)}, bf16[128,256]{1,0:T(8,128)(2,1)}, u32[]{:S(2)}) copy-start(bf16[128,256]{1,0:T(8,128)(2,1)} %state_out.5) | copy-start | bytes 196612
  106.3 35.4 %copy-start.7 = (bf16[256,128]{1,0:T(8,128)(2,1)S(1)}, bf16[256,128]{1,0:T(8,128)(2,1)}, u32[]{:S(2)}) copy-start(bf16[256,128]{1,0:T(8,128)(2,1)} %get-tuple-element.32.shares) | copy-start | bytes 196612
  106.4 41.5 %copy-start.3 = (bf16[128,512]{1,0:T(8,128)(2,1)S(1)}, bf16[128,512]{1,0:T(8,128)(2,1)}, u32[]{:S(2)}) copy-start(bf16[128,512]{1,0:T(8,128)(2,1)} %refs_5_.1) | copy-start | bytes 393220
  106.4 2.9 %collective-permute-start.2 = (bf16[128,4096]{1,0:T(8,128)(2,1)S(1)}, bf16[128,4096]{1,0:T(8,128)(2,1)S(1)}, u32[]{:S(2)}, u32[]{:S(2)}) collective-permute-start(bf16[128,4096]{1,0:T(8,128)(2,1)S(1)} %get-tuple-element.30), channel_id=1, source_target_pairs={{0,1},{1,0},{2,3},{3,2},{4,5},{5,4},{6,7},{7,6},{8,9},{9,8},{10,11... | collective-permute-start | bytes 3145736 | tf_op jit(solution)/shard_map/ppermute | solution.py:426
  109.2 51.5 %copy-start.6 = (bf16[128,256]{1,0:T(8,128)(2,1)S(1)}, bf16[128,256]{1,0:T(8,128)(2,1)}, u32[]{:S(2)}) copy-start(bf16[128,256]{1,0:T(8,128)(2,1)} %refs_6_.1) | copy-start | bytes 196612
  111.9 29.8 %all-to-all-start.3 = ((bf16[32,32,512]{2,1,0:T(8,128)(2,1)}), bf16[32,32,512]{2,1,0:T(8,128)(2,1)S(1)}, u32[]{:S(2)}, u32[]{:S(2)}) async-start(bf16[32,32,512]{2,1,0:T(8,128)(2,1)} %bitcast.8), calls=%async_computation.3 | async-start | bytes 2097152 | tf_op jit(solution)/shard_map/all_to_all | solution.py:434
  118.4 42.4 %copy-start = (f32[128,512]{1,0:T(8,128)S(1)}, f32[128,512]{1,0:T(8,128)}, u32[]{:S(2)}) copy-start(f32[128,512]{1,0:T(8,128)} %get-tuple-element.44.refs_7_) | copy-start | bytes 786436
  141.7 1.0 copy-start.1
  142.7 0.7 copy-start.8
  143.9 8.9 %collective-permute-start.3 = (bf16[136,512]{1,0:T(8,128)(2,1)S(1)}, bf16[136,512]{1,0:T(8,128)(2,1)S(1)}, u32[]{:S(2)}, u32[]{:S(2)}) collective-permute-start(bf16[136,512]{1,0:T(8,128)(2,1)S(1)} %get-tuple-element.36), channel_id=1, source_target_pairs={{8,0},{16,8},{24,16},{9,1},{17,9},{25,17},{10,2},{18,10},{26,18},{... | collective-permute-start | bytes 417800 | tf_op jit(solution)/shard_map/ppermute | solution.py:449
  145.2 15.5 %collective-permute-start.4 = (bf16[136,512]{1,0:T(8,128)(2,1)S(1)}, bf16[136,512]{1,0:T(8,128)(2,1)S(1)}, u32[]{:S(2)}, u32[]{:S(2)}) collective-permute-start(bf16[136,512]{1,0:T(8,128)(2,1)S(1)} %get-tuple-element.36), channel_id=1, source_target_pairs={{16,0},{24,8},{17,1},{25,9},{18,2},{26,10},{19,3},{27,11},{20,4},{... | collective-permute-start | bytes 417800 | tf_op jit(solution)/shard_map/ppermute | solution.py:449
  146.5 14.2 %collective-permute-start.5 = (bf16[136,512]{1,0:T(8,128)(2,1)S(1)}, bf16[136,512]{1,0:T(8,128)(2,1)S(1)}, u32[]{:S(2)}, u32[]{:S(2)}) collective-permute-start(bf16[136,512]{1,0:T(8,128)(2,1)S(1)} %get-tuple-element.36), channel_id=1, source_target_pairs={{24,0},{25,1},{26,2},{27,3},{28,4},{29,5},{30,6},{31,7}} | collective-permute-start | bytes 417800 | tf_op jit(solution)/shard_map/ppermute | solution.py:449
  147.8 1.0 copy-start.9
  148.9 0.9 copy-start.10
  149.8 0.9 copy-start.11
  150.8 0.7 copy-start.12

commit v5 on v4

--- a/solution.py
+++ b/solution.py
@@ -16,15 +16,11 @@
 bf16 = jnp.bfloat16
 highest = lax.Precision.HIGHEST
 vmem_bytes = 56 * 1024 * 1024
-resident_bytes = 1024 * 1024
+resident_bytes = 2 * 1024 * 1024
 
 
 def params(steps=0, limit=vmem_bytes):
     return pltpu.CompilerParams(dimension_semantics=("arbitrary",) * steps, vmem_limit_bytes=limit)
-
-
-def whole(shape):
-    return pl.BlockSpec(shape, lambda *_: (0,) * len(shape))
 
 
 def iota(shape, dim):
@@ -37,7 +33,8 @@
     )
 
 
-def pack_kernel(resid, ids_t, probs_t, out):
+def pack_kernel(resid, ids_t, probs_t, grad, out, grad_early):
+    grad_early[...] = grad[:, : grad_early.shape[1]]
     peers, rows = out.shape[0], out.shape[1]
     width = out.shape[2] - LANES
     eye = jnp.where(iota((rows, rows), 0) == iota((rows, rows), 1), 1.0, 0.0).astype(bf16)
@@ -52,7 +49,7 @@
         out[j, :, width:] = meta
 
 
-def dispatch_kernel(packed, table, shares, rows_x, *, experts, capacity):
+def dispatch_kernel(packed, grad, table, shares, rows, *, experts, capacity):
     tokens = packed.shape[0]
     width = packed.shape[1] - LANES
     meta = packed[:, width:].astype(f32)
@@ -75,101 +72,158 @@
         table[e * capacity : (e + 1) * capacity, :] = entry.astype(bf16)
         shares[e * capacity : (e + 1) * capacity, :] = (entry * weight_t[e : e + 1, :]).astype(bf16)
     out_x = dot(table[...], packed[:, :width], 1, 0).astype(bf16)
-    for c in range(rows_x.shape[0]):
-        rows_x[c] = out_x
-
-
-def select_kernel(table, grad, rows_g):
     out_g = dot(table[...], grad[...], 1, 0).astype(bf16)
-    for c in range(rows_g.shape[0]):
-        rows_g[c] = out_g
-
-
-def gate_up_kernel(own, other, gain, gate_w, up_w, coef_gate, coef_up, inverses, normed):
-    ctx, peers, slots, width = own.shape
+    for c in range(rows.shape[0]):
+        rows[c, :, :width] = out_x
+        rows[c, :, width:] = out_g
+
+
+def select_kernel(table, grad, rows):
+    late = rows.shape[2]
+    out_g = dot(table[...], grad[:, grad.shape[1] - late :], 1, 0).astype(bf16)
+    for c in range(rows.shape[0]):
+        rows[c] = out_g
+
+
+def gather_rows(own, other, start, stop, out):
+    ctx, peers, slots = own.shape[:3]
+    half = ctx * slots
+    for side, ref in enumerate((own, other)):
+        for j in range(peers):
+            at = slice(j * (stop - start), (j + 1) * (stop - start))
+            out[side * half : (side + 1) * half, at] = ref[:, j, :, start:stop].reshape(half, stop - start)
+
+
+def packed_copies(hbm, rows, width, start, stop, out, sems, base):
+    size = stop - start
+    return [
+        pltpu.make_async_copy(
+            hbm.at[0, rows, j * width + start : j * width + stop],
+            out.at[rows, j * size : (j + 1) * size],
+            sems.at[base + j],
+        )
+        for j in range(out.shape[1] // size)
+    ]
+
+
+def launch(copies):
+    for copy in copies:
+        copy.start()
+    return copies
+
+
+def finish(copies):
+    for copy in copies:
+        copy.wait()
+
+
+def gate_up_kernel(
+    own, other, gain, gate_hbm, up_hbm, down_hbm, coef_gate_hbm, coef_up_hbm, hidden_hbm, inverses,
+    normed, grads, gate_w, up_w, down_w, coef_gate, coef_up, hidden_early, in_sems, out_sems, *, width, block,
+):
+    ctx, peers, slots, both = own.shape
     half = ctx * slots
     model = peers * width
-
-    @pl.when(pl.program_id(0) == 0)
-    def _():
-        for side, ref in enumerate((own, other)):
-            total = jnp.zeros((half, 1), f32)
-            for j in range(peers):
-                x = ref[:, j].reshape(half, width).astype(f32)
-                total = total + jnp.sum(x * x, axis=1, keepdims=True)
-            inverse = lax.rsqrt(total * (1.0 / model) + norm_epsilon)
-            if side == 0:
-                inverses[...] = jnp.broadcast_to(inverse, (half, LANES))
-            for j in range(peers):
-                x = ref[:, j].reshape(half, width).astype(f32)
-                cols = slice(j * width, (j + 1) * width)
-                normed[side * half : (side + 1) * half, cols] = (x * inverse * gain[:, cols]).astype(bf16)
-
-    rows = normed[...]
-    gate = dot(rows, gate_w[0], 1, 1)
-    up = dot(rows, up_w[0], 1, 1)
-    sig = jax.nn.sigmoid(gate)
-    coef_gate[...] = up * sig * (1.0 + gate * (1.0 - sig))
-    coef_up[...] = gate * sig
+    blocks = gate_w.shape[0] // block
+    parts = [slice(i * block, (i + 1) * block) for i in range(blocks)]
+    pairs = [
+        launch(
+            [
+                pltpu.make_async_copy(gate_hbm.at[0, part, :], gate_w.at[part, :], in_sems.at[2 * i]),
+                pltpu.make_async_copy(up_hbm.at[0, part, :], up_w.at[part, :], in_sems.at[2 * i + 1]),
+            ]
+        )
+        for i, part in enumerate(parts)
+    ]
+    downs = launch(
+        packed_copies(down_hbm, slice(0, gate_w.shape[0]), width, 0, both - width, down_w, in_sems, 2 * blocks)
+    )
+    for side, ref in enumerate((own, other)):
+        total = jnp.zeros((half, 1), f32)
+        for j in range(peers):
+            x = ref[:, j, :, :width].reshape(half, width).astype(f32)
+            total = total + jnp.sum(x * x, axis=1, keepdims=True)
+        inverse = lax.rsqrt(total * (1.0 / model) + norm_epsilon)
+        if side == 0:
+            inverses[...] = jnp.broadcast_to(inverse, (half, LANES))
+        for j in range(peers):
+            x = ref[:, j, :, :width].reshape(half, width).astype(f32)
+            cols = slice(j * width, (j + 1) * width)
+            normed[side * half : (side + 1) * half, cols] = (x * inverse * gain[:, cols]).astype(bf16)
+    gather_rows(own, other, width, both, grads)
+    outs = []
+    for i, part in enumerate(parts):
+        finish(pairs[i])
+        gate = dot(normed[...], gate_w[part, :], 1, 1)
+        up = dot(normed[...], up_w[part, :], 1, 1)
+        sig = jax.nn.sigmoid(gate)
+        coef_gate[:, part] = up * sig * (1.0 + gate * (1.0 - sig))
+        coef_up[:, part] = gate * sig
+        outs += launch(
+            [
+                pltpu.make_async_copy(coef_gate.at[:, part], coef_gate_hbm.at[:, part], out_sems.at[3 * i]),
+                pltpu.make_async_copy(coef_up.at[:, part], coef_up_hbm.at[:, part], out_sems.at[3 * i + 1]),
+            ]
+        )
+    finish(downs)
+    for i, part in enumerate(parts):
+        hidden_early[:, part] = dot(grads[...], down_w[part, :], 1, 1)
+        outs += launch(
+            [pltpu.make_async_copy(hidden_early.at[:, part], hidden_hbm.at[:, part], out_sems.at[3 * i + 2])]
+        )
+    finish(outs)
 
 
 def back_kernel(
-    own, other, coef_gate_hbm, coef_up_hbm, gate_hbm, up_hbm, down_hbm, out_own, out_other,
-    grads, coef_gate, coef_up, gate_grad, up_grad, down_w, gate_w, up_w, sems,
+    own, other, hidden_hbm, coef_gate_hbm, coef_up_hbm, gate_hbm, up_hbm, down_hbm, out_own, out_other,
+    grads, hidden_early, coef_gate, coef_up, gate_grad, up_grad, gate_w, up_w, down_w, sems, *, width, block,
 ):
-    ctx, peers, slots, width = own.shape
+    ctx, peers, slots, late = own.shape
     half = ctx * slots
-    blocks, block, _ = down_w.shape
-    columns, _, column = gate_w.shape
-
-    def down_copy(i):
-        return pltpu.make_async_copy(down_hbm.at[0, i * block : (i + 1) * block, :], down_w.at[i], sems.at[i])
-
-    def pair_copies(i):
-        cols = slice(i * column, (i + 1) * column)
-        at = blocks + 2 * i
-        return (
-            pltpu.make_async_copy(gate_hbm.at[0, :, cols], gate_w.at[i], sems.at[at]),
-            pltpu.make_async_copy(up_hbm.at[0, :, cols], up_w.at[i], sems.at[at + 1]),
+    columns, hidden, column = gate_w.shape
+    blocks = hidden // block
+    parts = [slice(i * block, (i + 1) * block) for i in range(blocks)]
+    used = 0
+
+    def copy(source, target):
+        nonlocal used
+        used += 1
+        return pltpu.make_async_copy(source, target, sems.at[used - 1])
+
+    waits = []
+    for part in parts:
+        downs = launch(packed_copies(down_hbm, part, width, width - late, width, down_w, sems, used))
+        used += peers
+        waits.append(
+            downs
+            + launch(
+                [
+                    copy(hidden_hbm.at[:, part], hidden_early.at[:, part]),
+                    copy(coef_gate_hbm.at[:, part], coef_gate.at[:, part]),
+                    copy(coef_up_hbm.at[:, part], coef_up.at[:, part]),
+                ]
+            )
         )
-
-    coef_copies = (
-        pltpu.make_async_copy(coef_gate_hbm, coef_gate, sems.at[blocks + 2 * columns]),
-        pltpu.make_async_copy(coef_up_hbm, coef_up, sems.at[blocks + 2 * columns + 1]),
-    )
-    down_copy(0).start()
-    for copy in coef_copies:
-        copy.start()
-    for i in range(1, blocks):
-        down_copy(i).start()
-    for i in range(columns):
-        for copy in pair_copies(i):
-            copy.start()
-    for side, ref in enumerate((own, other)):
-        for j in range(peers):
-            cols = slice(j * width, (j + 1) * width)
-            grads[side * half : (side + 1) * half, cols] = ref[:, j].reshape(half, width)
-    rows = grads[...]
-    for i in range(blocks):
-        down_copy(i).wait()
-        part = slice(i * block, (i + 1) * block)
-        grad = dot(rows, down_w[i], 1, 1)
-        if i == 0:
-            for copy in coef_copies:
-                copy.wait()
+    slabs = [slice(i * column, (i + 1) * column) for i in range(columns)]
+    pairs = [
+        launch([copy(gate_hbm.at[0, :, cols], gate_w.at[i]), copy(up_hbm.at[0, :, cols], up_w.at[i])])
+        for i, cols in enumerate(slabs)
+    ]
+    gather_rows(own, other, 0, late, grads)
+    for i, part in enumerate(parts):
+        finish(waits[i])
+        grad = hidden_early[:, part] + dot(grads[...], down_w[part, :], 1, 1)
         gate_grad[:, part] = (grad * coef_gate[:, part]).astype(bf16)
         up_grad[:, part] = (grad * coef_up[:, part]).astype(bf16)
-    for i in range(columns):
-        for copy in pair_copies(i):
-            copy.wait()
-        cols = slice(i * column, (i + 1) * column)
+    for i, cols in enumerate(slabs):
+        finish(pairs[i])
         out = (dot(gate_grad[...], gate_w[i], 1, 0) + dot(up_grad[...], up_w[i], 1, 0)).astype(bf16)
         out_own[:, cols] = out[:half]
         out_other[:, cols] = out[half:]
 
 
 def slot_kernel(own, swapped, gain, inverses, x_rows, out, sums):
-    ctx, peers, slots, width = x_rows.shape
+    ctx, peers, slots, width = out.shape
     half = ctx * slots
     model = peers * width
     product = jnp.zeros((half, 1), f32)
@@ -177,13 +231,13 @@
         cols = slice(j * width, (j + 1) * width)
         total = (own[:, cols].astype(f32) + swapped[:, cols].astype(f32)) * gain[:, cols]
         sums[:, cols] = total
-        x = x_rows[:, j].reshape(half, width).astype(f32)
+        x = x_rows[:, j, :, :width].reshape(half, width).astype(f32)
         product = product + jnp.sum(total * x, axis=1, keepdims=True)
     inverse = inverses[:, 0:1]
     shift = inverse * inverse * inverse * product * (1.0 / model)
     for j in range(peers):
         cols = slice(j * width, (j + 1) * width)
-        x = x_rows[:, j].reshape(half, width).astype(f32)
+        x = x_rows[:, j, :, :width].reshape(half, width).astype(f32)
         out[:, j] = (sums[:, cols] * inverse - x * shift).astype(bf16).reshape(ctx, slots, width)
 
 
@@ -256,6 +310,15 @@
         local_b[:, cols] = dot(weighted.astype(bf16), state_out[:, cols], 1, 0)
 
 
+def join_kernel(first, later, out):
+    decay = first[N : N + 1, :].astype(f32) + first[N + 1 : N + 2, :].astype(f32)
+    out[0:N, :] = (first[0:N, :].astype(f32) + decay * later[0:N, :].astype(f32)).astype(bf16)
+    total = decay * (later[N : N + 1, :].astype(f32) + later[N + 1 : N + 2, :].astype(f32))
+    total = jnp.broadcast_to(total, (8, total.shape[1]))
+    high = total.astype(bf16).astype(f32)
+    out[N : N + 8, :] = jnp.where(iota(total.shape, 0) == 0, high, total - high).astype(bf16)
+
+
 def mixer_far_kernel(*refs):
     base, local_b, mixer, state_in, tail_l, mixer_grad, input_grad = refs[-7:]
     states = refs[:-7]
@@ -325,16 +388,20 @@
     heads = skip_gain.shape[0]
     groups = state_input.shape[1] // N
     hidden = gate_weight.shape[1]
+    early = width // 2
     gain = norm_gain.reshape(1, model)
     partner = [(i, i ^ 1) for i in range(peers)]
     shape = jax.ShapeDtypeStruct
 
-    packed = pl.pallas_call(
+    packed, grad_early = pl.pallas_call(
         pack_kernel,
-        out_shape=vmem_out((peers, token_rows, width + LANES), bf16),
+        out_shape=(
+            vmem_out((peers, token_rows, width + LANES), bf16),
+            vmem_out((tokens, early), bf16),
+        ),
         compiler_params=params(),
         name="pack",
-    )(resid_input, expert_ids.T, route_probs.T)
+    )(resid_input, expert_ids.T, route_probs.T, grad_output)
     packed = lax.all_to_all(packed, "exp", split_axis=0, concat_axis=0, tiled=True)
 
     mix, weigh, step_l, tail_l, head_l, skip_l, total_l = pl.pallas_call(
@@ -353,19 +420,19 @@
         name="mixer_setup",
     )(log_retention.T, step_size.T, skip_gain.reshape(1, heads), state_input, state_output)
 
-    table, shares, rows_x = pl.pallas_call(
+    table, shares, rows_early = pl.pallas_call(
         partial(dispatch_kernel, experts=experts, capacity=capacity),
         out_shape=(
             shape((experts * capacity, tokens), bf16),
             shape((experts * capacity, tokens), bf16),
-            vmem_out((ctx, experts * capacity, width), bf16),
+            vmem_out((ctx, experts * capacity, width + early), bf16),
         ),
         compiler_params=params(),
         name="dispatch",
-    )(in_vmem(packed.reshape(tokens, width + LANES)))
-    rows_g = pl.pallas_call(
+    )(in_vmem(packed.reshape(tokens, width + LANES)), in_vmem(grad_early))
+    rows_late = pl.pallas_call(
         select_kernel,
-        out_shape=shape((ctx, experts * capacity, width), bf16),
+        out_shape=vmem_out((ctx, experts * capacity, width - early), bf16),
         compiler_params=params(),
         cost_estimate=cost(10**9, 2 * 10**6),
         name="select",
@@ -373,55 +440,64 @@
 
     def spread(rows):
         got = lax.all_to_all(
-            rows.reshape(ctx * peers, slots, width), ("ctx", "exp"), split_axis=0, concat_axis=0, tiled=True
-        ).reshape(ctx, peers, slots, width)
-        return got, lax.ppermute(got, "exp", partner)
-
-    own_x, other_x = spread(rows_x)
-    own_g, other_g = spread(rows_g)
+            rows.reshape(ctx * peers, slots, -1), ("ctx", "exp"), split_axis=0, concat_axis=0, tiled=True
+        ).reshape(ctx, peers, slots, -1)
+        return in_vmem(got), in_vmem(lax.ppermute(got, "exp", partner))
+
+    own_x, other_x = spread(rows_early)
+    own_g, other_g = spread(rows_late)
     rows = 2 * ctx * slots
     half = rows // 2
-    slab = (ctx, peers, slots, width)
-    block = block_of(hidden, 256)
+    block = block_of(hidden, 512)
     blocks = hidden // block
-    weight_spec = pl.BlockSpec((1, block, model), lambda i: (0, i, 0))
-    act_spec = pl.BlockSpec((rows, block), lambda i: (0, i))
-    product = 2 * rows * model * hidden
-    coef_gate, coef_up, inverses = pl.pallas_call(
-        gate_up_kernel,
-        grid=(blocks,),
-        in_specs=[whole(slab), whole(slab), whole((1, model)), weight_spec, weight_spec],
-        out_specs=[act_spec, act_spec, whole((half, LANES))],
-        out_shape=(shape((rows, hidden), f32), shape((rows, hidden), f32), shape((half, LANES), f32)),
-        scratch_shapes=[pltpu.VMEM((rows, model), bf16)],
-        compiler_params=params(1),
-        cost_estimate=cost(2 * product, 4 * model * hidden),
-        name="gate_up",
-    )(in_vmem(own_x), in_vmem(other_x), gain, gate_weight, up_weight)
     column = block_of(model, 512)
     columns = model // column
+    product = 2 * rows * model * hidden
     any_spec = pl.BlockSpec(memory_space=pl.ANY)
     vmem_spec = pl.BlockSpec(memory_space=pltpu.VMEM)
-    out_own, out_other = pl.pallas_call(
-        back_kernel,
-        in_specs=[vmem_spec, vmem_spec] + [any_spec] * 5,
-        out_specs=[vmem_spec, vmem_spec],
-        out_shape=(vmem_out((half, model), bf16), vmem_out((half, model), bf16)),
+    acts = pltpu.VMEM((rows, hidden), f32)
+    coef_gate, coef_up, hidden_early, inverses = pl.pallas_call(
+        partial(gate_up_kernel, width=width, block=block),
+        in_specs=[vmem_spec] * 3 + [any_spec] * 3,
+        out_specs=[any_spec] * 3 + [vmem_spec],
+        out_shape=[shape((rows, hidden), f32)] * 3 + [vmem_out((half, LANES), f32)],
         scratch_shapes=[
             pltpu.VMEM((rows, model), bf16),
-            pltpu.VMEM((rows, hidden), f32),
-            pltpu.VMEM((rows, hidden), f32),
+            pltpu.VMEM((rows, peers * early), bf16),
+            pltpu.VMEM((hidden, model), bf16),
+            pltpu.VMEM((hidden, model), bf16),
+            pltpu.VMEM((hidden, peers * early), bf16),
+            acts,
+            acts,
+            acts,
+            pltpu.SemaphoreType.DMA((2 * blocks + peers,)),
+            pltpu.SemaphoreType.DMA((3 * blocks,)),
+        ],
+        compiler_params=params(),
+        cost_estimate=cost(5 * product // 2, 4 * model * hidden),
+        name="gate_up",
+    )(own_x, other_x, in_vmem(gain), gate_weight, up_weight, down_weight)
+    out_own, out_other = pl.pallas_call(
+        partial(back_kernel, width=width, block=block),
+        in_specs=[vmem_spec] * 2 + [any_spec] * 6,
+        out_specs=[vmem_spec] * 2,
+        out_shape=[vmem_out((half, model), bf16)] * 2,
+        scratch_shapes=[
+            pltpu.VMEM((rows, peers * (width - early)), bf16),
+            acts,
+            acts,
+            acts,
             pltpu.VMEM((rows, hidden), bf16),
             pltpu.VMEM((rows, hidden), bf16),
-            pltpu.VMEM((blocks, block, model), bf16),
             pltpu.VMEM((columns, hidden, column), bf16),
             pltpu.VMEM((columns, hidden, column), bf16),
-            pltpu.SemaphoreType.DMA((blocks + 2 * columns + 2,)),
+            pltpu.VMEM((hidden, peers * (width - early)), bf16),
+            pltpu.SemaphoreType.DMA((blocks * (peers + 3) + 2 * columns,)),
         ],
         compiler_params=params(),
-        cost_estimate=cost(3 * product, 6 * model * hidden),
+        cost_estimate=cost(5 * product // 2, 6 * model * hidden),
         name="back",
-    )(in_vmem(own_g), in_vmem(other_g), coef_gate, coef_up, gate_weight, up_weight, down_weight)
+    )(own_g, other_g, hidden_early, coef_gate, coef_up, gate_weight, up_weight, down_weight)
 
     swapped = lax.ppermute(out_other, "exp", partner)
     moved = pl.pallas_call(
@@ -430,7 +506,7 @@
         scratch_shapes=[pltpu.VMEM((half, model), f32)],
         compiler_params=params(),
         name="slot",
-    )(in_vmem(out_own), in_vmem(swapped), gain, in_vmem(inverses), in_vmem(own_x))
+    )(in_vmem(out_own), in_vmem(swapped), in_vmem(gain), in_vmem(inverses), own_x)
     moved = lax.all_to_all(
         moved.reshape(ctx * peers, slots, width), ("ctx", "exp"), split_axis=0, concat_axis=0, tiled=True
     ).reshape(ctx, experts * capacity, width)
@@ -445,9 +521,28 @@
         compiler_params=params(),
         name="upstream",
     )(*map(in_vmem, (moved, shares, grad_output, state_output, head_l, total_l)))
-    states = [
-        lax.ppermute(state, "ctx", [(i, i - k) for i in range(k, ctx)]) for k in range(1, ctx)
-    ]
+
+    def from_later(window, k):
+        return in_vmem(lax.ppermute(window, "ctx", [(i, i - k) for i in range(k, ctx)]))
+
+    spans = [1 << b for b in range((ctx - 1).bit_length()) if (ctx - 1) >> b & 1]
+    window, length, windows = state, 1, {}
+    while spans and length <= spans[-1]:
+        offset = 1 + sum(span for span in spans if span > length)
+        again = 2 * length <= spans[-1]
+        near = from_later(window, length) if again else None
+        if length in spans:
+            far_window = near if again and offset == length else from_later(window, offset)
+            windows[offset] = far_window
+        if again:
+            window = pl.pallas_call(
+                join_kernel,
+                out_shape=vmem_out((N + 8, width), bf16),
+                compiler_params=params(),
+                name="join",
+            )(in_vmem(window), near)
+        length *= 2
+    states = [windows[offset] for offset in sorted(windows)]
     base, local_b = pl.pallas_call(
         mixer_local_kernel,
         out_shape=(vmem_out((tokens, width), f32), vmem_out((tokens, groups * N), f32)),

time: 163 us -> 156 us (0.957)
  blocking collectives: 10.8 us -> 71.2 us
  waiting for transfers between devices: 83.5 us -> 34.5 us
  starting transfers between devices: 16 us -> 7.4 us
  Pallas kernels: 44.6 us -> 38.2 us
  local copies, waits for them, and re-layouts: 6.01 us -> 2.37 us
    all_to_all x0 -> x2, blocking collectives: none -> 60.4 us  [spread(): lax.all_to_all(rows.reshape(ctx * peers, slots, -1), ('ctx', 'exp'), spli...]
    all_to_all x2 -> x0, waiting for transfers between devices: 50 us -> none  [spread(): lax.all_to_all(rows.reshape(ctx * peers, slots, width), ('ctx', 'exp'), s...]
    all_to_all x2 -> x0, starting transfers between devices: 7.59 us -> none  [spread(): lax.all_to_all(rows.reshape(ctx * peers, slots, width), ('ctx', 'exp'), s...]
    pallas_call x4 -> x5, Pallas kernels: 35.5 us -> 30.2 us  [the longest x1 14.1 us: body(): pl.pallas_call(partial(gate_up_kernel, width=width, block=block), in_spec...]
    unnamed x27, local copies, waits for them, and re-layouts: 6.01 us -> 2.37 us
  transfers between devices with their start and end apart: 9 -> 7, of which waited for: 5 -> 5; matrix products, arithmetic and copies ran while one was open for 0% -> 0% of each run, Pallas kernels for 13% -> 12%
where the time goes in v5:
time: 156 us; the launch traced here: 155 us
  blocking collectives  71.2 us (46%)
  Pallas kernels  38.2 us (24%)
  waiting for transfers between devices  34.5 us (22%)
  starting transfers between devices  7.4 us (5%)
  local copies, waits for them, and re-layouts  2.37 us (2%)
    all_to_all x2, blocking collectives, spread(): lax.all_to_all(rows.reshape(ctx * peers, slots, -1), ('ctx', 'exp'), spli...  60.4 us
    all_to_all x1, waiting for transfers between devices, body(): lax.all_to_all(moved.reshape(ctx * peers, slots, width), ('ctx', 'exp'),...  23.2 us
    pallas_call x1, Pallas kernels, body(): pl.pallas_call(partial(gate_up_kernel, width=width, block=block), in_spec...  14.1 us
    pallas_call x1, Pallas kernels, body(): pl.pallas_call(partial(back_kernel, width=width, block=block), in_specs=[...  13.7 us
    all_to_all x1, blocking collectives, body(): lax.all_to_all(packed, 'exp', split_axis=0, concat_axis=0, tiled=True)  10.8 us
    ppermute x3, waiting for transfers between devices, from_later(): lax.ppermute(window, 'ctx', [(i, i - k) for i in range(k, ctx)])  9.02 us
    ppermute x3, starting transfers between devices, from_later(): lax.ppermute(window, 'ctx', [(i, i - k) for i in range(k, ctx)])  3.88 us
  transfers between devices with their start and end apart: 7, of which 5 were waited for; matrix products, arithmetic and copies ran while one was open for 0% of the time, Pallas kernels for 12%

profile of v5, /device:TPU:0, one launch (start us, length us, event | category | flops | bytes accessed | tf_op | source)
XLA Modules:
  0.0 154.5 jit_solution(9956131948408053056)
XLA Ops:
  0.6 1.2 pack.1
  1.8 10.8 %all_to_all.20 = bf16[8,16,640]{2,1,0:T(8,128)(2,1)S(1)} all-to-all(bf16[8,16,640]{2,1,0:T(8,128)(2,1)S(1)} %get-tuple-element.28), channel_id=1, replica_groups=mesh['ctx'=4,'exp'=8] {'exp'}, dimensions={0} | all-to-all | bytes 327680 | tf_op jit(solution)/shard_map/all_to_all | solution.py:405
  12.7 1.0 dispatch.1
  13.7 41.8 %all_to_all.21 = bf16[32,32,768]{2,1,0:T(8,128)(2,1)S(1)} all-to-all(bf16[32,32,768]{2,1,0:T(8,128)(2,1)S(1)} %bitcast.19), channel_id=1, replica_groups=mesh['ctx'=4,'exp'=8] {'ctx','exp'}, dimensions={0} | all-to-all | bytes 3145728 | tf_op jit(solution)/shard_map/all_to_all | solution.py:442
  55.5 1.1 select.1
  56.7 18.5 %all_to_all.22 = bf16[32,32,256]{2,1,0:T(8,128)(2,1)S(1)} all-to-all(bf16[32,32,256]{2,1,0:T(8,128)(2,1)S(1)} %bitcast.21), channel_id=1, replica_groups=mesh['ctx'=4,'exp'=8] {'ctx','exp'}, dimensions={0} | all-to-all | bytes 1048576 | tf_op jit(solution)/shard_map/all_to_all | solution.py:442
  75.2 14.1 %gate_up.1 = (f32[256,1536]{1,0:T(8,128)}, f32[256,1536]{1,0:T(8,128)}, f32[256,1536]{1,0:T(8,128)}, f32[128,128]{1,0:T(8,128)S(1)}) custom-call(bf16[4,8,32,768]{3,2,1,0:T(8,128)(2,1)S(1)} %bitcast.14, bf16[4,8,32,768]{3,2,1,0:T(8,128)(2,1)S(1)} %collective-permute-done.1.other, f32[1,4096]{1,0:T(1,128)S(1)} %bitcast.22, bf16[1,1536,4096]{2,1,0:T(8,128)(2,1)} %gate_hbm.3, ...), custom_call_target="tpu_custom_call" | custom-call | flops 8053063680 | bytes 25165824 | tf_op jit(solution)/shard_map/gate_up/pallas_call | solution.py:459
  89.3 13.7 %back.1 = (bf16[128,4096]{1,0:T(8,128)(2,1)S(1)}, bf16[128,4096]{1,0:T(8,128)(2,1)S(1)}) custom-call(bf16[4,8,32,256]{3,2,1,0:T(8,128)(2,1)S(1)} %bitcast.18, bf16[4,8,32,256]{3,2,1,0:T(8,128)(2,1)S(1)} %collective-permute-done.other, f32[256,1536]{1,0:T(8,128)} %get-tuple-element.32.hidden_hbm, f32[256,1536]{1,0:T(8,128)} %get-tuple-element.33.coef_gate_hbm, ...), custom_call_target="tpu_custom_call" | custom-call | flops 8053063680 | bytes 37748736 | tf_op jit(solution)/shard_map/back/pallas_call | solution.py:480
  103.6 2.3 %collective-permute-done.2.swapped = bf16[128,4096]{1,0:T(8,128)(2,1)S(1)} collective-permute-done((bf16[128,4096]{1,0:T(8,128)(2,1)S(1)}, bf16[128,4096]{1,0:T(8,128)(2,1)S(1)}, u32[]{:S(2)}, u32[]{:S(2)}) %collective-permute-start.2) | collective-permute-done | bytes 1048608 | tf_op jit(solution)/shard_map/ppermute | solution.py:502
  105.9 1.9 %slot.1 = bf16[4,8,32,512]{3,2,1,0:T(8,128)(2,1)} custom-call(bf16[128,4096]{1,0:T(8,128)(2,1)S(1)} %get-tuple-element.35.own, bf16[128,4096]{1,0:T(8,128)(2,1)S(1)} %collective-permute-done.2.swapped, f32[1,4096]{1,0:T(1,128)S(1)} %bitcast.23, f32[128,128]{1,0:T(8,128)S(1)} %get-tuple-element.37.inverses, bf16[4,8,32,768]{3,2,1,0:T(8,128)(2,1)S(1)} %bitcast.15), custom_call_target="tpu_custom_call" | custom-call | tf_op jit(solution)/shard_map/slot/pallas_call | solution.py:503
  107.8 3.0 %all-to-all-start.3 = ((bf16[32,32,512]{2,1,0:T(8,128)(2,1)}), bf16[32,32,512]{2,1,0:T(8,128)(2,1)S(1)}, u32[]{:S(2)}, u32[]{:S(2)}) async-start(bf16[32,32,512]{2,1,0:T(8,128)(2,1)} %bitcast.8), calls=%async_computation.3 | async-start | bytes 2097152 | tf_op jit(solution)/shard_map/all_to_all | solution.py:510
  110.8 3.0 %mixer_setup.1 = (bf16[8,128,128]{2,1,0:T(8,128)(2,1)}, f32[8,128,128]{2,1,0:T(8,128)}, f32[128,512]{1,0:T(8,128)}, f32[128,512]{1,0:T(8,128)}, f32[128,512]{1,0...) custom-call(f32[8,128]{1,0:T(8,128)} %bitcast.26, f32[8,128]{1,0:T(8,128)} %bitcast.27, f32[1,8]{1,0:T(1,128)} %bitcast.28, ...), custom_call_target="tpu_custom_call" | custom-call | flops 2000000000 | bytes 2000000 | tf_op jit(solution)/shard_map/mixer_setup/pallas_call | solution.py:407
  113.8 23.2 %all-to-all-done.3 = bf16[32,32,512]{2,1,0:T(8,128)(2,1)S(1)} async-done(((bf16[32,32,512]{2,1,0:T(8,128)(2,1)}), bf16[32,32,512]{2,1,0:T(8,128)(2,1)S(1)}, u32[]{:S(2)}, u32[]{:S(2)}) %all-to-all-start.3) | async-done | bytes 1048608 | tf_op jit(solution)/shard_map/all_to_all | solution.py:510
  137.0 0.9 copy-done.2
  137.9 0.7 copy-done.8
  139.2 1.3 collective-permute-start.3
  140.5 1.3 collective-permute-start.5
  141.8 4.3 %collective-permute-done.3.later = bf16[136,512]{1,0:T(8,128)(2,1)S(1)} collective-permute-done((bf16[136,512]{1,0:T(8,128)(2,1)S(1)}, bf16[136,512]{1,0:T(8,128)(2,1)S(1)}, u32[]{:S(2)}, u32[]{:S(2)}) %collective-permute-start.3) | collective-permute-done | bytes 139296 | tf_op jit(solution)/shard_map/ppermute | solution.py:526
  146.2 1.3 collective-permute-start.4
  147.5 0.7 mixer_local.1
  148.2 0.7 copy.17
  148.9 1.8 %collective-permute-done.5.refs_1_ = bf16[136,512]{1,0:T(8,128)(2,1)S(1)} collective-permute-done((bf16[136,512]{1,0:T(8,128)(2,1)S(1)}, bf16[136,512]{1,0:T(8,128)(2,1)S(1)}, u32[]{:S(2)}, u32[]{:S(2)}) %collective-permute-start.5) | collective-permute-done | bytes 139296 | tf_op jit(solution)/shard_map/ppermute | solution.py:526
  150.7 2.9 %collective-permute-done.4.refs_0_ = bf16[136,512]{1,0:T(8,128)(2,1)S(1)} collective-permute-done((bf16[136,512]{1,0:T(8,128)(2,1)S(1)}, bf16[136,512]{1,0:T(8,128)(2,1)S(1)}, u32[]{:S(2)}, u32[]{:S(2)}) %collective-permute-start.4) | collective-permute-done | bytes 139296 | tf_op jit(solution)/shard_map/ppermute | solution.py:526
  153.6 0.9 mixer_far.1
  (31 shorter events, 1.2 us)
Async XLA Ops:
  55.5 19.7 %collective-permute-start.1 = (bf16[4,8,32,768]{3,2,1,0:T(8,128)(2,1)S(1)}, bf16[4,8,32,768]{3,2,1,0:T(8,128)(2,1)S(1)}, u32[]{:S(2)}, u32[]{:S(2)}) collective-permute-start(bf16[4,8,32,768]{3,2,1,0:T(8,128)(2,1)S(1)} %bitcast.13), channel_id=1, source_target_pairs={{0,1},{1,0},{2,3},{3,2},{4,5},{5,4},{6,7},{7,6},{8,9},{9,8},{10,11... | collective-permute-start | bytes 4718600 | tf_op jit(solution)/shard_map/ppermute | solution.py:445
  55.5 19.7 %copy-start.4 = (f32[4096]{0:T(1024)S(1)}, f32[4096]{0:T(1024)}, u32[]{:S(2)}) copy-start(f32[4096]{0:T(1024)} %param.15) | copy-start | bytes 49156
  75.2 14.1 %collective-permute-start = (bf16[4,8,32,256]{3,2,1,0:T(8,128)(2,1)S(1)}, bf16[4,8,32,256]{3,2,1,0:T(8,128)(2,1)S(1)}, u32[]{:S(2)}, u32[]{:S(2)}) collective-permute-start(bf16[4,8,32,256]{3,2,1,0:T(8,128)(2,1)S(1)} %bitcast.17), channel_id=1, source_target_pairs={{0,1},{1,0},{2,3},{3,2},{4,5},{5,4},{6,7},{7,6},{8,9},{9,8},{10,11... | collective-permute-start | bytes 1572872 | tf_op jit(solution)/shard_map/ppermute | solution.py:445
  103.0 2.8 %collective-permute-start.2 = (bf16[128,4096]{1,0:T(8,128)(2,1)S(1)}, bf16[128,4096]{1,0:T(8,128)(2,1)S(1)}, u32[]{:S(2)}, u32[]{:S(2)}) collective-permute-start(bf16[128,4096]{1,0:T(8,128)(2,1)S(1)} %get-tuple-element.36), channel_id=1, source_target_pairs={{0,1},{1,0},{2,3},{3,2},{4,5},{5,4},{6,7},{7,6},{8,9},{9,8},{10,11... | collective-permute-start | bytes 3145736 | tf_op jit(solution)/shard_map/ppermute | solution.py:502
  107.8 29.2 %all-to-all-start.3 = ((bf16[32,32,512]{2,1,0:T(8,128)(2,1)}), bf16[32,32,512]{2,1,0:T(8,128)(2,1)S(1)}, u32[]{:S(2)}, u32[]{:S(2)}) async-start(bf16[32,32,512]{2,1,0:T(8,128)(2,1)} %bitcast.8), calls=%async_computation.3 | async-start | bytes 2097152 | tf_op jit(solution)/shard_map/all_to_all | solution.py:510
  110.8 26.2 %copy-start = (bf16[128,512]{1,0:T(8,128)(2,1)S(1)}, bf16[128,512]{1,0:T(8,128)(2,1)}, u32[]{:S(2)}) copy-start(bf16[128,512]{1,0:T(8,128)(2,1)} %grad.5) | copy-start | bytes 393220
  110.8 26.2 %copy-start.5 = (bf16[128,256]{1,0:T(8,128)(2,1)S(1)}, bf16[128,256]{1,0:T(8,128)(2,1)}, u32[]{:S(2)}) copy-start(bf16[128,256]{1,0:T(8,128)(2,1)} %state_out.5) | copy-start | bytes 196612
  110.8 26.2 %copy-start.7 = (bf16[256,128]{1,0:T(8,128)(2,1)S(1)}, bf16[256,128]{1,0:T(8,128)(2,1)}, u32[]{:S(2)}) copy-start(bf16[256,128]{1,0:T(8,128)(2,1)} %get-tuple-element.38.shares) | copy-start | bytes 196612
  110.8 36.7 %copy-start.3 = (bf16[128,512]{1,0:T(8,128)(2,1)S(1)}, bf16[128,512]{1,0:T(8,128)(2,1)}, u32[]{:S(2)}) copy-start(bf16[128,512]{1,0:T(8,128)(2,1)} %refs_4_.1) | copy-start | bytes 393220
  137.0 1.0 copy-start.2
  137.9 0.7 copy-start.8
  138.6 8.8 %copy-start.9 = (f32[8,128,128]{2,1,0:T(8,128)S(1)}, f32[8,128,128]{2,1,0:T(8,128)}, u32[]{:S(2)}) copy-start(f32[8,128,128]{2,1,0:T(8,128)} %get-tuple-element.45.weigh) | copy-start | bytes 1572868
  138.6 8.8 %copy-start.10 = (bf16[8,128,128]{2,1,0:T(8,128)(2,1)S(1)}, bf16[8,128,128]{2,1,0:T(8,128)(2,1)}, u32[]{:S(2)}) copy-start(bf16[8,128,128]{2,1,0:T(8,128)(2,1)} %get-tuple-element.44.mix) | copy-start | bytes 786436
  138.6 8.9 %copy-start.11 = (f32[128,512]{1,0:T(8,128)S(1)}, f32[128,512]{1,0:T(8,128)}, u32[]{:S(2)}) copy-start(f32[128,512]{1,0:T(8,128)} %get-tuple-element.46.step_l) | copy-start | bytes 786436
  138.6 8.9 %copy-start.12 = (f32[8,512]{1,0:T(8,128)S(1)}, f32[8,512]{1,0:T(8,128)}, u32[]{:S(2)}) copy-start(f32[8,512]{1,0:T(8,128)} %get-tuple-element.47.skip_l) | copy-start | bytes 49156
  139.2 6.9 %collective-permute-start.3 = (bf16[136,512]{1,0:T(8,128)(2,1)S(1)}, bf16[136,512]{1,0:T(8,128)(2,1)S(1)}, u32[]{:S(2)}, u32[]{:S(2)}) collective-permute-start(bf16[136,512]{1,0:T(8,128)(2,1)S(1)} %get-tuple-element.42.first), channel_id=1, source_target_pairs={{8,0},{16,8},{24,16},{9,1},{17,9},{25,17},{10,2},{18,10},{26,18},{... | collective-permute-start | bytes 417800 | tf_op jit(solution)/shard_map/ppermute | solution.py:526
  140.5 10.2 %collective-permute-start.5 = (bf16[136,512]{1,0:T(8,128)(2,1)S(1)}, bf16[136,512]{1,0:T(8,128)(2,1)S(1)}, u32[]{:S(2)}, u32[]{:S(2)}) collective-permute-start(bf16[136,512]{1,0:T(8,128)(2,1)S(1)} %get-tuple-element.42.first), channel_id=1, source_target_pairs={{24,0},{25,1},{26,2},{27,3},{28,4},{29,5},{30,6},{31,7}} | collective-permute-start | bytes 417800 | tf_op jit(solution)/shard_map/ppermute | solution.py:526
  146.2 7.4 %collective-permute-start.4 = (bf16[136,512]{1,0:T(8,128)(2,1)S(1)}, bf16[136,512]{1,0:T(8,128)(2,1)S(1)}, u32[]{:S(2)}, u32[]{:S(2)}) collective-permute-start(bf16[136,512]{1,0:T(8,128)(2,1)S(1)} %join.1), channel_id=1, source_target_pairs={{8,0},{16,8},{24,16},{9,1},{17,9},{25,17},{10,2},{18,10},{26,18},{... | collective-permute-start | bytes 417800 | tf_op jit(solution)/shard_map/ppermute | solution.py:526
  147.5 6.0 %copy-start.1 = (f32[128,512]{1,0:T(8,128)S(1)}, f32[128,512]{1,0:T(8,128)}, u32[]{:S(2)}) copy-start(f32[128,512]{1,0:T(8,128)} %get-tuple-element.50.refs_6_) | copy-start | bytes 786436
  147.5 6.0 %copy-start.6 = (bf16[128,256]{1,0:T(8,128)(2,1)S(1)}, bf16[128,256]{1,0:T(8,128)(2,1)}, u32[]{:S(2)}) copy-start(bf16[128,256]{1,0:T(8,128)(2,1)} %refs_5_.1) | copy-start | bytes 196612

commit v6 on v5

--- a/solution.py
+++ b/solution.py
@@ -33,7 +33,7 @@
     )
 
 
-def pack_kernel(resid, ids_t, probs_t, grad, out, grad_early):
+def pack_kernel(resid, gain, ids_t, probs_t, grad, out, grad_early):
     grad_early[...] = grad[:, : grad_early.shape[1]]
     peers, rows = out.shape[0], out.shape[1]
     width = out.shape[2] - LANES
@@ -43,13 +43,21 @@
     lane = iota((rows, LANES), 1)
     meta = jnp.where(lane == 0, ids[:, 0:1], 0.0) + jnp.where(lane == 1, ids[:, 1:2], 0.0)
     meta = meta + jnp.where(lane == 2, probs[:, 0:1], 0.0) + jnp.where(lane == 3, probs[:, 1:2], 0.0)
+    total = jnp.zeros((rows, 1), f32)
+    for j in range(peers):
+        x = resid[:, j * width : (j + 1) * width].astype(f32)
+        total = total + jnp.sum(x * x, axis=1, keepdims=True)
+    inverse = lax.rsqrt(total * (1.0 / (peers * width)) + norm_epsilon)
+    high = inverse.astype(bf16).astype(f32)
+    meta = meta + jnp.where(lane == 4, high, 0.0) + jnp.where(lane == 5, inverse - high, 0.0)
     meta = meta.astype(bf16)
     for j in range(peers):
-        out[j, :, :width] = resid[:, j * width : (j + 1) * width]
+        cols = slice(j * width, (j + 1) * width)
+        out[j, :, :width] = (resid[:, cols].astype(f32) * inverse * gain[:, cols]).astype(bf16)
         out[j, :, width:] = meta
 
 
-def dispatch_kernel(packed, grad, table, shares, rows, *, experts, capacity):
+def dispatch_kernel(packed, grad, table, shares, inverses, rows, *, experts, capacity):
     tokens = packed.shape[0]
     width = packed.shape[1] - LANES
     meta = packed[:, width:].astype(f32)
@@ -65,6 +73,7 @@
     position = dot(member, before, 0, 0)
     member_t = dot(member, same, 0, 0)
     weight_t = dot(weight, same, 0, 0)
+    inverses[...] = jnp.broadcast_to(meta[:, 4:5] + meta[:, 5:6], (tokens, LANES))
     slot = iota((capacity, tokens), 0).astype(f32)
     for e in range(experts):
         hit = (slot == position[e : e + 1, :]) & (member_t[e : e + 1, :] > 0.5)
@@ -85,13 +94,11 @@
         rows[c] = out_g
 
 
-def gather_rows(own, other, start, stop, out):
-    ctx, peers, slots = own.shape[:3]
-    half = ctx * slots
-    for side, ref in enumerate((own, other)):
-        for j in range(peers):
-            at = slice(j * (stop - start), (j + 1) * (stop - start))
-            out[side * half : (side + 1) * half, at] = ref[:, j, :, start:stop].reshape(half, stop - start)
+def gather_rows(ref, first, start, stop, out):
+    ctx, peers, slots = ref.shape[:3]
+    for j in range(peers):
+        at = slice(j * (stop - start), (j + 1) * (stop - start))
+        out[first : first + ctx * slots, at] = ref[:, j, :, start:stop].reshape(ctx * slots, stop - start)
 
 
 def packed_copies(hbm, rows, width, start, stop, out, sems, base):
@@ -118,14 +125,14 @@
 
 
 def gate_up_kernel(
-    own, other, gain, gate_hbm, up_hbm, down_hbm, coef_gate_hbm, coef_up_hbm, hidden_hbm, inverses,
-    normed, grads, gate_w, up_w, down_w, coef_gate, coef_up, hidden_early, in_sems, out_sems, *, width, block,
+    own, other_hbm, gate_hbm, up_hbm, down_hbm, coef_gate_hbm, coef_up_hbm, hidden_hbm,
+    other, normed, grads, gate_w, up_w, down_w, coef_gate, coef_up, hidden_early, in_sems, out_sems, *, width, block,
 ):
     ctx, peers, slots, both = own.shape
     half = ctx * slots
-    model = peers * width
     blocks = gate_w.shape[0] // block
     parts = [slice(i * block, (i + 1) * block) for i in range(blocks)]
+    swap = launch([pltpu.make_async_copy(other_hbm, other, in_sems.at[2 * blocks + peers])])
     pairs = [
         launch(
             [
@@ -138,19 +145,11 @@
     downs = launch(
         packed_copies(down_hbm, slice(0, gate_w.shape[0]), width, 0, both - width, down_w, in_sems, 2 * blocks)
     )
-    for side, ref in enumerate((own, other)):
-        total = jnp.zeros((half, 1), f32)
-        for j in range(peers):
-            x = ref[:, j, :, :width].reshape(half, width).astype(f32)
-            total = total + jnp.sum(x * x, axis=1, keepdims=True)
-        inverse = lax.rsqrt(total * (1.0 / model) + norm_epsilon)
-        if side == 0:
-            inverses[...] = jnp.broadcast_to(inverse, (half, LANES))
-        for j in range(peers):
-            x = ref[:, j, :, :width].reshape(half, width).astype(f32)
-            cols = slice(j * width, (j + 1) * width)
-            normed[side * half : (side + 1) * half, cols] = (x * inverse * gain[:, cols]).astype(bf16)
-    gather_rows(own, other, width, both, grads)
+    gather_rows(own, 0, 0, width, normed)
+    gather_rows(own, 0, width, both, grads)
+    finish(swap)
+    gather_rows(other, half, 0, width, normed)
+    gather_rows(other, half, width, both, grads)
     outs = []
     for i, part in enumerate(parts):
         finish(pairs[i])
@@ -194,25 +193,25 @@
     for part in parts:
         downs = launch(packed_copies(down_hbm, part, width, width - late, width, down_w, sems, used))
         used += peers
-        waits.append(
-            downs
-            + launch(
-                [
-                    copy(hidden_hbm.at[:, part], hidden_early.at[:, part]),
-                    copy(coef_gate_hbm.at[:, part], coef_gate.at[:, part]),
-                    copy(coef_up_hbm.at[:, part], coef_up.at[:, part]),
-                ]
-            )
-        )
+        acts = [
+            copy(hidden_hbm.at[:, part], hidden_early.at[:, part]),
+            copy(coef_gate_hbm.at[:, part], coef_gate.at[:, part]),
+            copy(coef_up_hbm.at[:, part], coef_up.at[:, part]),
+        ]
+        waits.append((downs, launch(acts)))
     slabs = [slice(i * column, (i + 1) * column) for i in range(columns)]
     pairs = [
         launch([copy(gate_hbm.at[0, :, cols], gate_w.at[i]), copy(up_hbm.at[0, :, cols], up_w.at[i])])
         for i, cols in enumerate(slabs)
     ]
-    gather_rows(own, other, 0, late, grads)
+    gather_rows(own, 0, 0, late, grads)
+    gather_rows(other, half, 0, late, grads)
     for i, part in enumerate(parts):
-        finish(waits[i])
-        grad = hidden_early[:, part] + dot(grads[...], down_w[part, :], 1, 1)
+        downs, acts = waits[i]
+        finish(downs)
+        late_part = dot(grads[...], down_w[part, :], 1, 1)
+        finish(acts)
+        grad = hidden_early[:, part] + late_part
         gate_grad[:, part] = (grad * coef_gate[:, part]).astype(bf16)
         up_grad[:, part] = (grad * coef_up[:, part]).astype(bf16)
     for i, cols in enumerate(slabs):
@@ -222,23 +221,22 @@
         out_other[:, cols] = out[half:]
 
 
-def slot_kernel(own, swapped, gain, inverses, x_rows, out, sums):
+def slot_kernel(own, swapped, gain, rows, out, sums):
     ctx, peers, slots, width = out.shape
     half = ctx * slots
     model = peers * width
     product = jnp.zeros((half, 1), f32)
     for j in range(peers):
         cols = slice(j * width, (j + 1) * width)
-        total = (own[:, cols].astype(f32) + swapped[:, cols].astype(f32)) * gain[:, cols]
+        total = own[:, cols].astype(f32) + swapped[:, cols].astype(f32)
         sums[:, cols] = total
-        x = x_rows[:, j, :, :width].reshape(half, width).astype(f32)
-        product = product + jnp.sum(total * x, axis=1, keepdims=True)
-    inverse = inverses[:, 0:1]
-    shift = inverse * inverse * inverse * product * (1.0 / model)
+        normed = rows[:, j, :, :width].reshape(half, width).astype(f32)
+        product = product + jnp.sum(total * normed, axis=1, keepdims=True)
+    shift = product * (1.0 / model)
     for j in range(peers):
         cols = slice(j * width, (j + 1) * width)
-        x = x_rows[:, j, :, :width].reshape(half, width).astype(f32)
-        out[:, j] = (sums[:, cols] * inverse - x * shift).astype(bf16).reshape(ctx, slots, width)
+        scaled = rows[:, j, :, :width].reshape(half, width).astype(f32) * (1.0 / gain[:, cols])
+        out[:, j] = (sums[:, cols] * gain[:, cols] - scaled * shift).astype(bf16).reshape(ctx, slots, width)
 
 
 def mixer_setup_kernel(
@@ -272,14 +270,14 @@
             weigh[h] = decay * steps[:, h : h + 1]
 
 
-def upstream_kernel(moved, shares, grad, state_out, head_l, total_l, upstream, resid_grad, state):
+def upstream_kernel(moved, shares, inverses, grad, state_out, head_l, total_l, upstream, resid_grad, state):
     width = grad.shape[1]
     groups = state_out.shape[1] // N
     span = width // groups
     moe = dot(shares[...], moved[0], 0, 0)
     for c in range(1, moved.shape[0]):
         moe = moe + dot(shares[...], moved[c], 0, 0)
-    moe = moe.astype(bf16)
+    moe = (moe * inverses[:, 0:1]).astype(bf16)
     up = grad[...].astype(f32) + moe.astype(f32)
     upstream[...] = up
     resid_grad[...] = up.astype(bf16)
@@ -401,7 +399,7 @@
         ),
         compiler_params=params(),
         name="pack",
-    )(resid_input, expert_ids.T, route_probs.T, grad_output)
+    )(resid_input, gain, expert_ids.T, route_probs.T, grad_output)
     packed = lax.all_to_all(packed, "exp", split_axis=0, concat_axis=0, tiled=True)
 
     mix, weigh, step_l, tail_l, head_l, skip_l, total_l = pl.pallas_call(
@@ -420,11 +418,12 @@
         name="mixer_setup",
     )(log_retention.T, step_size.T, skip_gain.reshape(1, heads), state_input, state_output)
 
-    table, shares, rows_early = pl.pallas_call(
+    table, shares, inverses, rows_early = pl.pallas_call(
         partial(dispatch_kernel, experts=experts, capacity=capacity),
         out_shape=(
-            shape((experts * capacity, tokens), bf16),
-            shape((experts * capacity, tokens), bf16),
+            vmem_out((experts * capacity, tokens), bf16),
+            vmem_out((experts * capacity, tokens), bf16),
+            vmem_out((tokens, LANES), f32),
             vmem_out((ctx, experts * capacity, width + early), bf16),
         ),
         compiler_params=params(),
@@ -436,13 +435,13 @@
         compiler_params=params(),
         cost_estimate=cost(10**9, 2 * 10**6),
         name="select",
-    )(table, grad_output)
+    )(in_vmem(table), grad_output)
 
     def spread(rows):
         got = lax.all_to_all(
             rows.reshape(ctx * peers, slots, -1), ("ctx", "exp"), split_axis=0, concat_axis=0, tiled=True
         ).reshape(ctx, peers, slots, -1)
-        return in_vmem(got), in_vmem(lax.ppermute(got, "exp", partner))
+        return in_vmem(got), lax.ppermute(got, "exp", partner)
 
     own_x, other_x = spread(rows_early)
     own_g, other_g = spread(rows_late)
@@ -456,12 +455,13 @@
     any_spec = pl.BlockSpec(memory_space=pl.ANY)
     vmem_spec = pl.BlockSpec(memory_space=pltpu.VMEM)
     acts = pltpu.VMEM((rows, hidden), f32)
-    coef_gate, coef_up, hidden_early, inverses = pl.pallas_call(
+    coef_gate, coef_up, hidden_early = pl.pallas_call(
         partial(gate_up_kernel, width=width, block=block),
-        in_specs=[vmem_spec] * 3 + [any_spec] * 3,
-        out_specs=[any_spec] * 3 + [vmem_spec],
-        out_shape=[shape((rows, hidden), f32)] * 3 + [vmem_out((half, LANES), f32)],
+        in_specs=[vmem_spec] + [any_spec] * 4,
+        out_specs=[any_spec] * 3,
+        out_shape=[shape((rows, hidden), f32)] * 3,
         scratch_shapes=[
+            pltpu.VMEM((ctx, peers, slots, width + early), bf16),
             pltpu.VMEM((rows, model), bf16),
             pltpu.VMEM((rows, peers * early), bf16),
             pltpu.VMEM((hidden, model), bf16),
@@ -470,13 +470,13 @@
             acts,
             acts,
             acts,
-            pltpu.SemaphoreType.DMA((2 * blocks + peers,)),
+            pltpu.SemaphoreType.DMA((2 * blocks + peers + 1,)),
             pltpu.SemaphoreType.DMA((3 * blocks,)),
         ],
         compiler_params=params(),
         cost_estimate=cost(5 * product // 2, 4 * model * hidden),
         name="gate_up",
-    )(own_x, other_x, in_vmem(gain), gate_weight, up_weight, down_weight)
+    )(own_x, other_x, gate_weight, up_weight, down_weight)
     out_own, out_other = pl.pallas_call(
         partial(back_kernel, width=width, block=block),
         in_specs=[vmem_spec] * 2 + [any_spec] * 6,
@@ -497,7 +497,7 @@
         compiler_params=params(),
         cost_estimate=cost(5 * product // 2, 6 * model * hidden),
         name="back",
-    )(own_g, other_g, hidden_early, coef_gate, coef_up, gate_weight, up_weight, down_weight)
+    )(own_g, in_vmem(other_g), hidden_early, coef_gate, coef_up, gate_weight, up_weight, down_weight)
 
     swapped = lax.ppermute(out_other, "exp", partner)
     moved = pl.pallas_call(
@@ -506,7 +506,7 @@
         scratch_shapes=[pltpu.VMEM((half, model), f32)],
         compiler_params=params(),
         name="slot",
-    )(in_vmem(out_own), in_vmem(swapped), in_vmem(gain), in_vmem(inverses), own_x)
+    )(in_vmem(out_own), in_vmem(swapped), in_vmem(gain), own_x)
     moved = lax.all_to_all(
         moved.reshape(ctx * peers, slots, width), ("ctx", "exp"), split_axis=0, concat_axis=0, tiled=True
     ).reshape(ctx, experts * capacity, width)
@@ -520,7 +520,7 @@
         ),
         compiler_params=params(),
         name="upstream",
-    )(*map(in_vmem, (moved, shares, grad_output, state_output, head_l, total_l)))
+    )(*map(in_vmem, (moved, shares, inverses, grad_output, state_output, head_l, total_l)))
 
     def from_later(window, k):
         return in_vmem(lax.ppermute(window, "ctx", [(i, i - k) for i in range(k, ctx)]))

time: 156 us -> 157 us (level)
  no operation moved by 1% of the time
where the time goes in v6:
time: 157 us; the launch traced here: 156 us
  blocking collectives  71.2 us (45%)
  Pallas kernels  38 us (24%)
  waiting for transfers between devices  34.5 us (22%)
  starting transfers between devices  7.44 us (5%)
  local copies, waits for them, and re-layouts  3.55 us (2%)
    all_to_all x2, blocking collectives, spread(): lax.all_to_all(rows.reshape(ctx * peers, slots, -1), ('ctx', 'exp'), spli...  60.4 us
    all_to_all x1, waiting for transfers between devices, body(): lax.all_to_all(moved.reshape(ctx * peers, slots, width), ('ctx', 'exp'),...  23.2 us
    pallas_call x1, Pallas kernels, body(): pl.pallas_call(partial(gate_up_kernel, width=width, block=block), in_spec...  14.4 us
    pallas_call x1, Pallas kernels, body(): pl.pallas_call(partial(back_kernel, width=width, block=block), in_specs=[...  13.7 us
    all_to_all x1, blocking collectives, body(): lax.all_to_all(packed, 'exp', split_axis=0, concat_axis=0, tiled=True)  10.8 us
    ppermute x3, waiting for transfers between devices, from_later(): lax.ppermute(window, 'ctx', [(i, i - k) for i in range(k, ctx)])  9.02 us
    ppermute x3, starting transfers between devices, from_later(): lax.ppermute(window, 'ctx', [(i, i - k) for i in range(k, ctx)])  3.88 us
    unnamed x27, local copies, waits for them, and re-layouts  3.55 us
  transfers between devices with their start and end apart: 7, of which 5 were waited for; matrix products, arithmetic and copies ran while one was open for 0% of the time, Pallas kernels for 12%

profile of v6, /device:TPU:0, one launch (start us, length us, event | category | flops | bytes accessed | tf_op | source)
XLA Modules:
  0.0 155.5 jit_solution(11229455242251049206)
XLA Ops:
  0.6 1.2 pack.1
  1.9 10.8 %all_to_all.20 = bf16[8,16,640]{2,1,0:T(8,128)(2,1)S(1)} all-to-all(bf16[8,16,640]{2,1,0:T(8,128)(2,1)S(1)} %get-tuple-element.28), channel_id=1, replica_groups=mesh['ctx'=4,'exp'=8] {'exp'}, dimensions={0} | all-to-all | bytes 327680 | tf_op jit(solution)/shard_map/all_to_all | solution.py:403
  13.2 41.9 %all_to_all.21 = bf16[32,32,768]{2,1,0:T(8,128)(2,1)S(1)} all-to-all(bf16[32,32,768]{2,1,0:T(8,128)(2,1)S(1)} %bitcast.19), channel_id=1, replica_groups=mesh['ctx'=4,'exp'=8] {'ctx','exp'}, dimensions={0} | all-to-all | bytes 3145728 | tf_op jit(solution)/shard_map/all_to_all | solution.py:441
  55.1 1.1 select.1
  56.2 18.5 %all_to_all.22 = bf16[32,32,256]{2,1,0:T(8,128)(2,1)S(1)} all-to-all(bf16[32,32,256]{2,1,0:T(8,128)(2,1)S(1)} %bitcast.21), channel_id=1, replica_groups=mesh['ctx'=4,'exp'=8] {'ctx','exp'}, dimensions={0} | all-to-all | bytes 1048576 | tf_op jit(solution)/shard_map/all_to_all | solution.py:441
  74.7 1.2 copy-done.12
  75.9 14.4 %gate_up.1 = (f32[256,1536]{1,0:T(8,128)}, f32[256,1536]{1,0:T(8,128)}, f32[256,1536]{1,0:T(8,128)}) custom-call(bf16[4,8,32,768]{3,2,1,0:T(8,128)(2,1)S(1)} %bitcast.14, bf16[4,8,32,768]{3,2,1,0:T(8,128)(2,1)} %copy-done.12, bf16[1,1536,4096]{2,1,0:T(8,128)(2,1)} %gate_hbm.3, bf16[1,1536,4096]{2,1,0:T(8,128)(2,1)} %up_hbm.3, bf16[1,1536,4096]{2,1,0:T(8,128)(2,1)} %down_hbm.3), custom_call_target="tpu_custom_call" | custom-call | flops 8053063680 | bytes 25165824 | tf_op jit(solution)/shard_map/gate_up/pallas_call | solution.py:458
  90.3 13.7 %back.1 = (bf16[128,4096]{1,0:T(8,128)(2,1)S(1)}, bf16[128,4096]{1,0:T(8,128)(2,1)S(1)}) custom-call(bf16[4,8,32,256]{3,2,1,0:T(8,128)(2,1)S(1)} %bitcast.18, bf16[4,8,32,256]{3,2,1,0:T(8,128)(2,1)S(1)} %collective-permute-done.other, f32[256,1536]{1,0:T(8,128)} %get-tuple-element.32.hidden_hbm, f32[256,1536]{1,0:T(8,128)} %get-tuple-element.33.coef_gate_hbm, ...), custom_call_target="tpu_custom_call" | custom-call | flops 8053063680 | bytes 37748736 | tf_op jit(solution)/shard_map/back/pallas_call | solution.py:480
  104.5 2.3 %collective-permute-done.2.swapped = bf16[128,4096]{1,0:T(8,128)(2,1)S(1)} collective-permute-done((bf16[128,4096]{1,0:T(8,128)(2,1)S(1)}, bf16[128,4096]{1,0:T(8,128)(2,1)S(1)}, u32[]{:S(2)}, u32[]{:S(2)}) %collective-permute-start.2) | collective-permute-done | bytes 1048608 | tf_op jit(solution)/shard_map/ppermute | solution.py:502
  106.8 1.9 %slot.1 = bf16[4,8,32,512]{3,2,1,0:T(8,128)(2,1)} custom-call(bf16[128,4096]{1,0:T(8,128)(2,1)S(1)} %get-tuple-element.35.own, bf16[128,4096]{1,0:T(8,128)(2,1)S(1)} %collective-permute-done.2.swapped, f32[1,4096]{1,0:T(1,128)S(1)} %bitcast.23, bf16[4,8,32,768]{3,2,1,0:T(8,128)(2,1)S(1)} %bitcast.15), custom_call_target="tpu_custom_call" | custom-call | tf_op jit(solution)/shard_map/slot/pallas_call | solution.py:503
  108.8 3.0 %all-to-all-start.3 = ((bf16[32,32,512]{2,1,0:T(8,128)(2,1)}), bf16[32,32,512]{2,1,0:T(8,128)(2,1)S(1)}, u32[]{:S(2)}, u32[]{:S(2)}) async-start(bf16[32,32,512]{2,1,0:T(8,128)(2,1)} %bitcast.8), calls=%async_computation.3 | async-start | bytes 2097152 | tf_op jit(solution)/shard_map/all_to_all | solution.py:510
  111.8 3.0 %mixer_setup.1 = (bf16[8,128,128]{2,1,0:T(8,128)(2,1)}, f32[8,128,128]{2,1,0:T(8,128)}, f32[128,512]{1,0:T(8,128)}, f32[128,512]{1,0:T(8,128)}, f32[128,512]{1,0...) custom-call(f32[8,128]{1,0:T(8,128)} %bitcast.26, f32[8,128]{1,0:T(8,128)} %bitcast.27, f32[1,8]{1,0:T(1,128)} %bitcast.28, ...), custom_call_target="tpu_custom_call" | custom-call | flops 2000000000 | bytes 2000000 | tf_op jit(solution)/shard_map/mixer_setup/pallas_call | solution.py:405
  114.8 23.2 %all-to-all-done.3 = bf16[32,32,512]{2,1,0:T(8,128)(2,1)S(1)} async-done(((bf16[32,32,512]{2,1,0:T(8,128)(2,1)}), bf16[32,32,512]{2,1,0:T(8,128)(2,1)S(1)}, u32[]{:S(2)}, u32[]{:S(2)}) %all-to-all-start.3) | async-done | bytes 1048608 | tf_op jit(solution)/shard_map/all_to_all | solution.py:510
  138.0 0.9 copy-done.2
  138.9 0.7 copy-done.7
  140.2 1.3 collective-permute-start.3
  141.5 1.3 collective-permute-start.5
  142.8 4.3 %collective-permute-done.3.later = bf16[136,512]{1,0:T(8,128)(2,1)S(1)} collective-permute-done((bf16[136,512]{1,0:T(8,128)(2,1)S(1)}, bf16[136,512]{1,0:T(8,128)(2,1)S(1)}, u32[]{:S(2)}, u32[]{:S(2)}) %collective-permute-start.3) | collective-permute-done | bytes 139296 | tf_op jit(solution)/shard_map/ppermute | solution.py:526
  147.2 1.3 collective-permute-start.4
  148.6 0.7 mixer_local.1
  149.3 0.7 copy.17
  149.9 1.8 %collective-permute-done.5.refs_1_ = bf16[136,512]{1,0:T(8,128)(2,1)S(1)} collective-permute-done((bf16[136,512]{1,0:T(8,128)(2,1)S(1)}, bf16[136,512]{1,0:T(8,128)(2,1)S(1)}, u32[]{:S(2)}, u32[]{:S(2)}) %collective-permute-start.5) | collective-permute-done | bytes 139296 | tf_op jit(solution)/shard_map/ppermute | solution.py:526
  151.7 2.9 %collective-permute-done.4.refs_0_ = bf16[136,512]{1,0:T(8,128)(2,1)S(1)} collective-permute-done((bf16[136,512]{1,0:T(8,128)(2,1)S(1)}, bf16[136,512]{1,0:T(8,128)(2,1)S(1)}, u32[]{:S(2)}, u32[]{:S(2)}) %collective-permute-start.4) | collective-permute-done | bytes 139296 | tf_op jit(solution)/shard_map/ppermute | solution.py:526
  154.6 0.9 mixer_far.1
  (31 shorter events, 1.7 us)
Async XLA Ops:
  55.1 19.6 %collective-permute-start.1 = (bf16[4,8,32,768]{3,2,1,0:T(8,128)(2,1)S(1)}, bf16[4,8,32,768]{3,2,1,0:T(8,128)(2,1)S(1)}, u32[]{:S(2)}, u32[]{:S(2)}) collective-permute-start(bf16[4,8,32,768]{3,2,1,0:T(8,128)(2,1)S(1)} %bitcast.13), channel_id=1, source_target_pairs={{0,1},{1,0},{2,3},{3,2},{4,5},{5,4},{6,7},{7,6},{8,9},{9,8},{10,11... | collective-permute-start | bytes 4718600 | tf_op jit(solution)/shard_map/ppermute | solution.py:444
  74.7 15.5 %collective-permute-start = (bf16[4,8,32,256]{3,2,1,0:T(8,128)(2,1)S(1)}, bf16[4,8,32,256]{3,2,1,0:T(8,128)(2,1)S(1)}, u32[]{:S(2)}, u32[]{:S(2)}) collective-permute-start(bf16[4,8,32,256]{3,2,1,0:T(8,128)(2,1)S(1)} %bitcast.17), channel_id=1, source_target_pairs={{0,1},{1,0},{2,3},{3,2},{4,5},{5,4},{6,7},{7,6},{8,9},{9,8},{10,11... | collective-permute-start | bytes 1572872 | tf_op jit(solution)/shard_map/ppermute | solution.py:444
  74.7 1.2 copy-start.12
  90.2 16.6 %copy-start.4 = (f32[4096]{0:T(1024)S(1)}, f32[4096]{0:T(1024)}, u32[]{:S(2)}) copy-start(f32[4096]{0:T(1024)} %param.15) | copy-start | bytes 49156
  104.0 2.9 %collective-permute-start.2 = (bf16[128,4096]{1,0:T(8,128)(2,1)S(1)}, bf16[128,4096]{1,0:T(8,128)(2,1)S(1)}, u32[]{:S(2)}, u32[]{:S(2)}) collective-permute-start(bf16[128,4096]{1,0:T(8,128)(2,1)S(1)} %get-tuple-element.36), channel_id=1, source_target_pairs={{0,1},{1,0},{2,3},{3,2},{4,5},{5,4},{6,7},{7,6},{8,9},{9,8},{10,11... | collective-permute-start | bytes 3145736 | tf_op jit(solution)/shard_map/ppermute | solution.py:502
  108.8 29.2 %all-to-all-start.3 = ((bf16[32,32,512]{2,1,0:T(8,128)(2,1)}), bf16[32,32,512]{2,1,0:T(8,128)(2,1)S(1)}, u32[]{:S(2)}, u32[]{:S(2)}) async-start(bf16[32,32,512]{2,1,0:T(8,128)(2,1)} %bitcast.8), calls=%async_computation.3 | async-start | bytes 2097152 | tf_op jit(solution)/shard_map/all_to_all | solution.py:510
  111.8 26.2 %copy-start = (bf16[128,512]{1,0:T(8,128)(2,1)S(1)}, bf16[128,512]{1,0:T(8,128)(2,1)}, u32[]{:S(2)}) copy-start(bf16[128,512]{1,0:T(8,128)(2,1)} %grad.5) | copy-start | bytes 393220
  111.8 26.2 %copy-start.5 = (bf16[128,256]{1,0:T(8,128)(2,1)S(1)}, bf16[128,256]{1,0:T(8,128)(2,1)}, u32[]{:S(2)}) copy-start(bf16[128,256]{1,0:T(8,128)(2,1)} %state_out.5) | copy-start | bytes 196612
  111.8 36.7 %copy-start.3 = (bf16[128,512]{1,0:T(8,128)(2,1)S(1)}, bf16[128,512]{1,0:T(8,128)(2,1)}, u32[]{:S(2)}) copy-start(bf16[128,512]{1,0:T(8,128)(2,1)} %refs_4_.1) | copy-start | bytes 393220
  138.0 1.0 copy-start.2
  138.9 0.7 copy-start.7
  139.7 8.9 %copy-start.8 = (f32[8,128,128]{2,1,0:T(8,128)S(1)}, f32[8,128,128]{2,1,0:T(8,128)}, u32[]{:S(2)}) copy-start(f32[8,128,128]{2,1,0:T(8,128)} %get-tuple-element.45.weigh) | copy-start | bytes 1572868
  139.7 8.9 %copy-start.9 = (bf16[8,128,128]{2,1,0:T(8,128)(2,1)S(1)}, bf16[8,128,128]{2,1,0:T(8,128)(2,1)}, u32[]{:S(2)}) copy-start(bf16[8,128,128]{2,1,0:T(8,128)(2,1)} %get-tuple-element.44.mix) | copy-start | bytes 786436
  139.7 8.9 %copy-start.10 = (f32[128,512]{1,0:T(8,128)S(1)}, f32[128,512]{1,0:T(8,128)}, u32[]{:S(2)}) copy-start(f32[128,512]{1,0:T(8,128)} %get-tuple-element.46.step_l) | copy-start | bytes 786436
  139.7 8.9 %copy-start.11 = (f32[8,512]{1,0:T(8,128)S(1)}, f32[8,512]{1,0:T(8,128)}, u32[]{:S(2)}) copy-start(f32[8,512]{1,0:T(8,128)} %get-tuple-element.47.skip_l) | copy-start | bytes 49156
  140.2 6.9 %collective-permute-start.3 = (bf16[136,512]{1,0:T(8,128)(2,1)S(1)}, bf16[136,512]{1,0:T(8,128)(2,1)S(1)}, u32[]{:S(2)}, u32[]{:S(2)}) collective-permute-start(bf16[136,512]{1,0:T(8,128)(2,1)S(1)} %get-tuple-element.42.first), channel_id=1, source_target_pairs={{8,0},{16,8},{24,16},{9,1},{17,9},{25,17},{10,2},{18,10},{26,18},{... | collective-permute-start | bytes 417800 | tf_op jit(solution)/shard_map/ppermute | solution.py:526
  141.5 10.2 %collective-permute-start.5 = (bf16[136,512]{1,0:T(8,128)(2,1)S(1)}, bf16[136,512]{1,0:T(8,128)(2,1)S(1)}, u32[]{:S(2)}, u32[]{:S(2)}) collective-permute-start(bf16[136,512]{1,0:T(8,128)(2,1)S(1)} %get-tuple-element.42.first), channel_id=1, source_target_pairs={{24,0},{25,1},{26,2},{27,3},{28,4},{29,5},{30,6},{31,7}} | collective-permute-start | bytes 417800 | tf_op jit(solution)/shard_map/ppermute | solution.py:526
  147.2 7.4 %collective-permute-start.4 = (bf16[136,512]{1,0:T(8,128)(2,1)S(1)}, bf16[136,512]{1,0:T(8,128)(2,1)S(1)}, u32[]{:S(2)}, u32[]{:S(2)}) collective-permute-start(bf16[136,512]{1,0:T(8,128)(2,1)S(1)} %join.1), channel_id=1, source_target_pairs={{8,0},{16,8},{24,16},{9,1},{17,9},{25,17},{10,2},{18,10},{26,18},{... | collective-permute-start | bytes 417800 | tf_op jit(solution)/shard_map/ppermute | solution.py:526
  148.5 6.0 %copy-start.1 = (f32[128,512]{1,0:T(8,128)S(1)}, f32[128,512]{1,0:T(8,128)}, u32[]{:S(2)}) copy-start(f32[128,512]{1,0:T(8,128)} %get-tuple-element.50.refs_6_) | copy-start | bytes 786436
  148.6 6.0 %copy-start.6 = (bf16[128,256]{1,0:T(8,128)(2,1)S(1)}, bf16[128,256]{1,0:T(8,128)(2,1)}, u32[]{:S(2)}) copy-start(bf16[128,256]{1,0:T(8,128)(2,1)} %refs_5_.1) | copy-start | bytes 196612

commit v7 on v6

--- a/solution.py
+++ b/solution.py
@@ -57,29 +57,21 @@
         out[j, :, width:] = meta
 
 
-def dispatch_kernel(packed, grad, table, shares, inverses, rows, *, experts, capacity):
+def dispatch_kernel(packed, grad, table, rows, *, experts, capacity):
     tokens = packed.shape[0]
     width = packed.shape[1] - LANES
     meta = packed[:, width:].astype(f32)
     lane = iota((tokens, LANES), 1).astype(f32)
-    first = meta[:, 0:1] == lane
-    second = meta[:, 1:2] == lane
-    member = jnp.where(first | second, 1.0, 0.0).astype(bf16)
-    weight = (jnp.where(first, meta[:, 2:3], 0.0) + jnp.where(second, meta[:, 3:4], 0.0)).astype(bf16)
+    member = jnp.where((meta[:, 0:1] == lane) | (meta[:, 1:2] == lane), 1.0, 0.0).astype(bf16)
     row = iota((tokens, tokens), 0)
     col = iota((tokens, tokens), 1)
-    before = jnp.where(row < col, 1.0, 0.0).astype(bf16)
-    same = jnp.where(row == col, 1.0, 0.0).astype(bf16)
-    position = dot(member, before, 0, 0)
-    member_t = dot(member, same, 0, 0)
-    weight_t = dot(weight, same, 0, 0)
-    inverses[...] = jnp.broadcast_to(meta[:, 4:5] + meta[:, 5:6], (tokens, LANES))
+    position = dot(member, jnp.where(row < col, 1.0, 0.0).astype(bf16), 0, 0)
+    member_t = dot(member, jnp.where(row == col, 1.0, 0.0).astype(bf16), 0, 0)
+    position = jnp.where(member_t > 0.5, position, -1.0)
     slot = iota((capacity, tokens), 0).astype(f32)
     for e in range(experts):
-        hit = (slot == position[e : e + 1, :]) & (member_t[e : e + 1, :] > 0.5)
-        entry = jnp.where(hit, 1.0, 0.0)
-        table[e * capacity : (e + 1) * capacity, :] = entry.astype(bf16)
-        shares[e * capacity : (e + 1) * capacity, :] = (entry * weight_t[e : e + 1, :]).astype(bf16)
+        hit = slot == position[e : e + 1, :]
+        table[e * capacity : (e + 1) * capacity, :] = jnp.where(hit, 1.0, 0.0).astype(bf16)
     out_x = dot(table[...], packed[:, :width], 1, 0).astype(bf16)
     out_g = dot(table[...], grad[...], 1, 0).astype(bf16)
     for c in range(rows.shape[0]):
@@ -87,11 +79,21 @@
         rows[c, :, width:] = out_g
 
 
-def select_kernel(table, grad, rows):
+def select_kernel(packed, table, grad, shares, inverses, rows, *, experts, capacity):
+    tokens = packed.shape[0]
+    meta = packed[:, packed.shape[1] - LANES :].astype(f32)
     late = rows.shape[2]
     out_g = dot(table[...], grad[:, grad.shape[1] - late :], 1, 0).astype(bf16)
     for c in range(rows.shape[0]):
         rows[c] = out_g
+    inverses[...] = jnp.broadcast_to(meta[:, 4:5] + meta[:, 5:6], (tokens, LANES))
+    lane = iota((tokens, LANES), 1).astype(f32)
+    weight = jnp.where(meta[:, 0:1] == lane, meta[:, 2:3], 0.0) + jnp.where(meta[:, 1:2] == lane, meta[:, 3:4], 0.0)
+    same = jnp.where(iota((tokens, tokens), 0) == iota((tokens, tokens), 1), 1.0, 0.0).astype(bf16)
+    weight_t = dot(weight.astype(bf16), same, 0, 0)
+    for e in range(experts):
+        at = slice(e * capacity, (e + 1) * capacity)
+        shares[at, :] = (table[at, :].astype(f32) * weight_t[e : e + 1, :]).astype(bf16)
 
 
 def gather_rows(ref, first, start, stop, out):
@@ -386,7 +388,7 @@
     heads = skip_gain.shape[0]
     groups = state_input.shape[1] // N
     hidden = gate_weight.shape[1]
-    early = width // 2
+    early = max(LANES, width // 4)
     gain = norm_gain.reshape(1, model)
     partner = [(i, i ^ 1) for i in range(peers)]
     shape = jax.ShapeDtypeStruct
@@ -400,7 +402,9 @@
         compiler_params=params(),
         name="pack",
     )(resid_input, gain, expert_ids.T, route_probs.T, grad_output)
-    packed = lax.all_to_all(packed, "exp", split_axis=0, concat_axis=0, tiled=True)
+    packed = lax.all_to_all(packed, "exp", split_axis=0, concat_axis=0, tiled=True).reshape(
+        tokens, width + LANES
+    )
 
     mix, weigh, step_l, tail_l, head_l, skip_l, total_l = pl.pallas_call(
         partial(mixer_setup_kernel, groups=groups),
@@ -418,24 +422,26 @@
         name="mixer_setup",
     )(log_retention.T, step_size.T, skip_gain.reshape(1, heads), state_input, state_output)
 
-    table, shares, inverses, rows_early = pl.pallas_call(
+    table, rows_early = pl.pallas_call(
         partial(dispatch_kernel, experts=experts, capacity=capacity),
         out_shape=(
             vmem_out((experts * capacity, tokens), bf16),
+            vmem_out((ctx, experts * capacity, width + early), bf16),
+        ),
+        compiler_params=params(),
+        name="dispatch",
+    )(in_vmem(packed), in_vmem(grad_early))
+    shares, inverses, rows_late = pl.pallas_call(
+        partial(select_kernel, experts=experts, capacity=capacity),
+        out_shape=(
             vmem_out((experts * capacity, tokens), bf16),
             vmem_out((tokens, LANES), f32),
-            vmem_out((ctx, experts * capacity, width + early), bf16),
+            vmem_out((ctx, experts * capacity, width - early), bf16),
         ),
-        compiler_params=params(),
-        name="dispatch",
-    )(in_vmem(packed.reshape(tokens, width + LANES)), in_vmem(grad_early))
-    rows_late = pl.pallas_call(
-        select_kernel,
-        out_shape=vmem_out((ctx, experts * capacity, width - early), bf16),
         compiler_params=params(),
         cost_estimate=cost(10**9, 2 * 10**6),
         name="select",
-    )(in_vmem(table), grad_output)
+    )(in_vmem(packed), in_vmem(table), grad_output)
 
     def spread(rows):
         got = lax.all_to_all(

time: 157 us -> 157 us (level)
  blocking collectives: 71.2 us -> 10.8 us
  waiting for transfers between devices: 34.5 us -> 84.7 us
  starting transfers between devices: 7.44 us -> 16 us
  Pallas kernels: 38 us -> 40 us
    all_to_all x2 -> x0, blocking collectives: 60.4 us -> none  [spread(): lax.all_to_all(rows.reshape(ctx * peers, slots, -1), ('ctx', 'exp'), spli...]
    all_to_all x0 -> x2, waiting for transfers between devices: none -> 50.2 us  [spread(): lax.all_to_all(rows.reshape(ctx * peers, slots, -1), ('ctx', 'exp'), spli...]
    all_to_all x0 -> x2, starting transfers between devices: none -> 7.57 us  [spread(): lax.all_to_all(rows.reshape(ctx * peers, slots, -1), ('ctx', 'exp'), spli...]
    unnamed x27 -> x25, local copies, waits for them, and re-layouts: 3.55 us -> 2.38 us
  transfers between devices with their start and end apart: 7 -> 9, of which waited for: 5 -> 7; matrix products, arithmetic and copies ran while one was open for 0% -> 0% of each run, Pallas kernels for 12% -> 12%
where the time goes in v7:
time: 157 us; the launch traced here: 155 us
  waiting for transfers between devices  84.7 us (54%)
  Pallas kernels  40 us (25%)
  starting transfers between devices  16 us (10%)
  blocking collectives  10.8 us (7%)
  local copies, waits for them, and re-layouts  2.38 us (2%)
    all_to_all x2, waiting for transfers between devices, spread(): lax.all_to_all(rows.reshape(ctx * peers, slots, -1), ('ctx', 'exp'), spli...  50.2 us
    all_to_all x1, waiting for transfers between devices, body(): lax.all_to_all(moved.reshape(ctx * peers, slots, width), ('ctx', 'exp'),...  23.2 us
    pallas_call x1, Pallas kernels, body(): pl.pallas_call(partial(back_kernel, width=width, block=block), in_specs=[...  14.6 us
    pallas_call x1, Pallas kernels, body(): pl.pallas_call(partial(gate_up_kernel, width=width, block=block), in_spec...  13.5 us
    all_to_all x1, blocking collectives, body(): lax.all_to_all(packed, 'exp', split_axis=0, concat_axis=0, tiled=True)  10.8 us
    ppermute x3, waiting for transfers between devices, from_later(): lax.ppermute(window, 'ctx', [(i, i - k) for i in range(k, ctx)])  9.02 us
    all_to_all x2, starting transfers between devices, spread(): lax.all_to_all(rows.reshape(ctx * peers, slots, -1), ('ctx', 'exp'), spli...  7.57 us
    ppermute x3, starting transfers between devices, from_later(): lax.ppermute(window, 'ctx', [(i, i - k) for i in range(k, ctx)])  3.88 us
  transfers between devices with their start and end apart: 9, of which 7 were waited for; matrix products, arithmetic and copies ran while one was open for 0% of the time, Pallas kernels for 12%

profile of v7, /device:TPU:0, one launch (start us, length us, event | category | flops | bytes accessed | tf_op | source)
XLA Modules:
  0.0 154.7 jit_solution(11353965038097715662)
XLA Ops:
  0.6 1.2 pack.1
  1.9 10.8 %all_to_all.20 = bf16[8,16,640]{2,1,0:T(8,128)(2,1)S(1)} all-to-all(bf16[8,16,640]{2,1,0:T(8,128)(2,1)S(1)} %get-tuple-element.29), channel_id=1, replica_groups=mesh['ctx'=4,'exp'=8] {'exp'}, dimensions={0} | all-to-all | bytes 327680 | tf_op jit(solution)/shard_map/all_to_all | solution.py:405
  12.7 1.6 %dispatch.1 = (bf16[256,128]{1,0:T(8,128)(2,1)S(1)}, bf16[4,256,640]{2,1,0:T(8,128)(2,1)}) custom-call(bf16[128,640]{1,0:T(8,128)(2,1)S(1)} %bitcast.19, bf16[128,128]{1,0:T(8,128)(2,1)S(1)} %get-tuple-element.30.grad), custom_call_target="tpu_custom_call" | custom-call | tf_op jit(solution)/shard_map/dispatch/pallas_call | solution.py:425
  14.3 4.0 %all-to-all-start.2 = ((bf16[32,32,640]{2,1,0:T(8,128)(2,1)}), bf16[32,32,640]{2,1,0:T(8,128)(2,1)S(1)}, u32[]{:S(2)}, u32[]{:S(2)}) async-start(bf16[32,32,640]{2,1,0:T(8,128)(2,1)} %bitcast.6), calls=%async_computation.2 | async-start | bytes 2621440 | tf_op jit(solution)/shard_map/all_to_all | solution.py:447
  18.3 2.1 %select.1 = (bf16[256,128]{1,0:T(8,128)(2,1)S(1)}, f32[128,128]{1,0:T(8,128)S(1)}, bf16[4,256,384]{2,1,0:T(8,128)(2,1)}) custom-call(bf16[128,640]{1,0:T(8,128)(2,1)S(1)} %bitcast.20, bf16[256,128]{1,0:T(8,128)(2,1)S(1)} %get-tuple-element.31.table, bf16[128,512]{1,0:T(8,128)(2,1)} %grad.5), custom_call_target="tpu_custom_call" | custom-call | flops 1000000000 | bytes 2000000 | tf_op jit(solution)/shard_map/select/pallas_call | solution.py:434
  20.3 29.9 %all-to-all-done.2 = bf16[32,32,640]{2,1,0:T(8,128)(2,1)S(1)} async-done(((bf16[32,32,640]{2,1,0:T(8,128)(2,1)}), bf16[32,32,640]{2,1,0:T(8,128)(2,1)S(1)}, u32[]{:S(2)}, u32[]{:S(2)}) %all-to-all-start.2) | async-done | bytes 1310752 | tf_op jit(solution)/shard_map/all_to_all | solution.py:447
  50.2 3.6 %all-to-all-start.1 = ((bf16[32,32,384]{2,1,0:T(8,128)(2,1)}), bf16[32,32,384]{2,1,0:T(8,128)(2,1)S(1)}, u32[]{:S(2)}, u32[]{:S(2)}) async-start(bf16[32,32,384]{2,1,0:T(8,128)(2,1)} %bitcast.4), calls=%async_computation.1 | async-start | bytes 1572864 | tf_op jit(solution)/shard_map/all_to_all | solution.py:447
  54.2 20.3 %all-to-all-done.1 = bf16[32,32,384]{2,1,0:T(8,128)(2,1)S(1)} async-done(((bf16[32,32,384]{2,1,0:T(8,128)(2,1)}), bf16[32,32,384]{2,1,0:T(8,128)(2,1)S(1)}, u32[]{:S(2)}, u32[]{:S(2)}) %all-to-all-start.1) | async-done | bytes 786464 | tf_op jit(solution)/shard_map/all_to_all | solution.py:447
  74.4 13.5 %gate_up.1 = (f32[256,1536]{1,0:T(8,128)}, f32[256,1536]{1,0:T(8,128)}, f32[256,1536]{1,0:T(8,128)}) custom-call(bf16[4,8,32,640]{3,2,1,0:T(8,128)(2,1)S(1)} %bitcast.14, bf16[4,8,32,640]{3,2,1,0:T(8,128)(2,1)} %collective-permute-done.1.other_hbm, bf16[1,1536,4096]{2,1,0:T(8,128)(2,1)} %gate_hbm.3, bf16[1,1536,4096]{2,1,0:T(8,128)(2,1)} %up_hbm.3, ...), custom_call_target="tpu_custom_call" | custom-call | flops 8053063680 | bytes 25165824 | tf_op jit(solution)/shard_map/gate_up/pallas_call | solution.py:464
  87.9 14.6 %back.1 = (bf16[128,4096]{1,0:T(8,128)(2,1)S(1)}, bf16[128,4096]{1,0:T(8,128)(2,1)S(1)}) custom-call(bf16[4,8,32,384]{3,2,1,0:T(8,128)(2,1)S(1)} %bitcast.18, bf16[4,8,32,384]{3,2,1,0:T(8,128)(2,1)S(1)} %collective-permute-done.other, f32[256,1536]{1,0:T(8,128)} %get-tuple-element.34.hidden_hbm, f32[256,1536]{1,0:T(8,128)} %get-tuple-element.35.coef_gate_hbm, ...), custom_call_target="tpu_custom_call" | custom-call | flops 8053063680 | bytes 37748736 | tf_op jit(solution)/shard_map/back/pallas_call | solution.py:486
  103.1 2.3 %collective-permute-done.2.swapped = bf16[128,4096]{1,0:T(8,128)(2,1)S(1)} collective-permute-done((bf16[128,4096]{1,0:T(8,128)(2,1)S(1)}, bf16[128,4096]{1,0:T(8,128)(2,1)S(1)}, u32[]{:S(2)}, u32[]{:S(2)}) %collective-permute-start.2) | collective-permute-done | bytes 1048608 | tf_op jit(solution)/shard_map/ppermute | solution.py:508
  105.4 1.9 %slot.1 = bf16[4,8,32,512]{3,2,1,0:T(8,128)(2,1)} custom-call(bf16[128,4096]{1,0:T(8,128)(2,1)S(1)} %get-tuple-element.37.own, bf16[128,4096]{1,0:T(8,128)(2,1)S(1)} %collective-permute-done.2.swapped, f32[1,4096]{1,0:T(1,128)S(1)} %bitcast.22, bf16[4,8,32,640]{3,2,1,0:T(8,128)(2,1)S(1)} %bitcast.15), custom_call_target="tpu_custom_call" | custom-call | tf_op jit(solution)/shard_map/slot/pallas_call | solution.py:509
  107.3 3.6 %all-to-all-start.3 = ((bf16[32,32,512]{2,1,0:T(8,128)(2,1)}), bf16[32,32,512]{2,1,0:T(8,128)(2,1)S(1)}, u32[]{:S(2)}, u32[]{:S(2)}) async-start(bf16[32,32,512]{2,1,0:T(8,128)(2,1)} %bitcast.8), calls=%async_computation.3 | async-start | bytes 2097152 | tf_op jit(solution)/shard_map/all_to_all | solution.py:516
  111.0 3.0 %mixer_setup.1 = (bf16[8,128,128]{2,1,0:T(8,128)(2,1)}, f32[8,128,128]{2,1,0:T(8,128)}, f32[128,512]{1,0:T(8,128)}, f32[128,512]{1,0:T(8,128)}, f32[128,512]{1,0...) custom-call(f32[8,128]{1,0:T(8,128)} %bitcast.25, f32[8,128]{1,0:T(8,128)} %bitcast.26, f32[1,8]{1,0:T(1,128)} %bitcast.27, ...), custom_call_target="tpu_custom_call" | custom-call | flops 2000000000 | bytes 2000000 | tf_op jit(solution)/shard_map/mixer_setup/pallas_call | solution.py:409
  113.9 23.2 %all-to-all-done.3 = bf16[32,32,512]{2,1,0:T(8,128)(2,1)S(1)} async-done(((bf16[32,32,512]{2,1,0:T(8,128)(2,1)}), bf16[32,32,512]{2,1,0:T(8,128)(2,1)S(1)}, u32[]{:S(2)}, u32[]{:S(2)}) %all-to-all-start.3) | async-done | bytes 1048608 | tf_op jit(solution)/shard_map/all_to_all | solution.py:516
  137.2 0.9 copy-done.2
  138.1 0.7 copy-done.7
  139.4 1.3 collective-permute-start.3
  140.7 1.3 collective-permute-start.5
  142.0 4.3 %collective-permute-done.3.later = bf16[136,512]{1,0:T(8,128)(2,1)S(1)} collective-permute-done((bf16[136,512]{1,0:T(8,128)(2,1)S(1)}, bf16[136,512]{1,0:T(8,128)(2,1)S(1)}, u32[]{:S(2)}, u32[]{:S(2)}) %collective-permute-start.3) | collective-permute-done | bytes 139296 | tf_op jit(solution)/shard_map/ppermute | solution.py:532
  146.4 1.3 collective-permute-start.4
  149.1 1.8 %collective-permute-done.5.refs_1_ = bf16[136,512]{1,0:T(8,128)(2,1)S(1)} collective-permute-done((bf16[136,512]{1,0:T(8,128)(2,1)S(1)}, bf16[136,512]{1,0:T(8,128)(2,1)S(1)}, u32[]{:S(2)}, u32[]{:S(2)}) %collective-permute-start.5) | collective-permute-done | bytes 139296 | tf_op jit(solution)/shard_map/ppermute | solution.py:532
  150.9 2.9 %collective-permute-done.4.refs_0_ = bf16[136,512]{1,0:T(8,128)(2,1)S(1)} collective-permute-done((bf16[136,512]{1,0:T(8,128)(2,1)S(1)}, bf16[136,512]{1,0:T(8,128)(2,1)S(1)}, u32[]{:S(2)}, u32[]{:S(2)}) %collective-permute-start.4) | collective-permute-done | bytes 139296 | tf_op jit(solution)/shard_map/ppermute | solution.py:532
  153.8 0.9 mixer_far.1
  (31 shorter events, 2.9 us)
Async XLA Ops:
  14.3 35.9 %all-to-all-start.2 = ((bf16[32,32,640]{2,1,0:T(8,128)(2,1)}), bf16[32,32,640]{2,1,0:T(8,128)(2,1)S(1)}, u32[]{:S(2)}, u32[]{:S(2)}) async-start(bf16[32,32,640]{2,1,0:T(8,128)(2,1)} %bitcast.6), calls=%async_computation.2 | async-start | bytes 2621440 | tf_op jit(solution)/shard_map/all_to_all | solution.py:447
  50.2 24.2 %all-to-all-start.1 = ((bf16[32,32,384]{2,1,0:T(8,128)(2,1)}), bf16[32,32,384]{2,1,0:T(8,128)(2,1)S(1)}, u32[]{:S(2)}, u32[]{:S(2)}) async-start(bf16[32,32,384]{2,1,0:T(8,128)(2,1)} %bitcast.4), calls=%async_computation.1 | async-start | bytes 1572864 | tf_op jit(solution)/shard_map/all_to_all | solution.py:447
  53.8 20.6 %collective-permute-start.1 = (bf16[4,8,32,640]{3,2,1,0:T(8,128)(2,1)S(1)}, bf16[4,8,32,640]{3,2,1,0:T(8,128)(2,1)}, u32[]{:S(2)}, u32[]{:S(2)}) collective-permute-start(bf16[4,8,32,640]{3,2,1,0:T(8,128)(2,1)S(1)} %bitcast.13), channel_id=1, source_target_pairs={{0,1},{1,0},{2,3},{3,2},{4,5},{5,4},{6,7},{7,6},{8,9},{9,8},{10,11... | collective-permute-start | bytes 3932168 | tf_op jit(solution)/shard_map/ppermute | solution.py:450
  74.4 13.5 %collective-permute-start = (bf16[4,8,32,384]{3,2,1,0:T(8,128)(2,1)S(1)}, bf16[4,8,32,384]{3,2,1,0:T(8,128)(2,1)S(1)}, u32[]{:S(2)}, u32[]{:S(2)}) collective-permute-start(bf16[4,8,32,384]{3,2,1,0:T(8,128)(2,1)S(1)} %bitcast.17), channel_id=1, source_target_pairs={{0,1},{1,0},{2,3},{3,2},{4,5},{5,4},{6,7},{7,6},{8,9},{9,8},{10,11... | collective-permute-start | bytes 2359304 | tf_op jit(solution)/shard_map/ppermute | solution.py:450
  87.9 17.5 %copy-start.4 = (f32[4096]{0:T(1024)S(1)}, f32[4096]{0:T(1024)}, u32[]{:S(2)}) copy-start(f32[4096]{0:T(1024)} %param.15) | copy-start | bytes 49156
  102.5 2.9 %collective-permute-start.2 = (bf16[128,4096]{1,0:T(8,128)(2,1)S(1)}, bf16[128,4096]{1,0:T(8,128)(2,1)S(1)}, u32[]{:S(2)}, u32[]{:S(2)}) collective-permute-start(bf16[128,4096]{1,0:T(8,128)(2,1)S(1)} %get-tuple-element.38), channel_id=1, source_target_pairs={{0,1},{1,0},{2,3},{3,2},{4,5},{5,4},{6,7},{7,6},{8,9},{9,8},{10,11... | collective-permute-start | bytes 3145736 | tf_op jit(solution)/shard_map/ppermute | solution.py:508
  107.3 29.8 %all-to-all-start.3 = ((bf16[32,32,512]{2,1,0:T(8,128)(2,1)}), bf16[32,32,512]{2,1,0:T(8,128)(2,1)S(1)}, u32[]{:S(2)}, u32[]{:S(2)}) async-start(bf16[32,32,512]{2,1,0:T(8,128)(2,1)} %bitcast.8), calls=%async_computation.3 | async-start | bytes 2097152 | tf_op jit(solution)/shard_map/all_to_all | solution.py:516
  110.9 26.2 %copy-start = (bf16[128,512]{1,0:T(8,128)(2,1)S(1)}, bf16[128,512]{1,0:T(8,128)(2,1)}, u32[]{:S(2)}) copy-start(bf16[128,512]{1,0:T(8,128)(2,1)} %grad.5) | copy-start | bytes 393220
  111.0 26.2 %copy-start.5 = (bf16[128,256]{1,0:T(8,128)(2,1)S(1)}, bf16[128,256]{1,0:T(8,128)(2,1)}, u32[]{:S(2)}) copy-start(bf16[128,256]{1,0:T(8,128)(2,1)} %state_out.5) | copy-start | bytes 196612
  111.0 36.7 %copy-start.3 = (bf16[128,512]{1,0:T(8,128)(2,1)S(1)}, bf16[128,512]{1,0:T(8,128)(2,1)}, u32[]{:S(2)}) copy-start(bf16[128,512]{1,0:T(8,128)(2,1)} %refs_4_.1) | copy-start | bytes 393220
  137.2 1.0 copy-start.2
  138.1 0.7 copy-start.7
  138.8 8.9 %copy-start.8 = (f32[8,128,128]{2,1,0:T(8,128)S(1)}, f32[8,128,128]{2,1,0:T(8,128)}, u32[]{:S(2)}) copy-start(f32[8,128,128]{2,1,0:T(8,128)} %get-tuple-element.47.weigh) | copy-start | bytes 1572868
  138.8 8.9 %copy-start.9 = (bf16[8,128,128]{2,1,0:T(8,128)(2,1)S(1)}, bf16[8,128,128]{2,1,0:T(8,128)(2,1)}, u32[]{:S(2)}) copy-start(bf16[8,128,128]{2,1,0:T(8,128)(2,1)} %get-tuple-element.46.mix) | copy-start | bytes 786436
  138.8 8.9 %copy-start.10 = (f32[128,512]{1,0:T(8,128)S(1)}, f32[128,512]{1,0:T(8,128)}, u32[]{:S(2)}) copy-start(f32[128,512]{1,0:T(8,128)} %get-tuple-element.48.step_l) | copy-start | bytes 786436
  138.8 8.9 %copy-start.11 = (f32[8,512]{1,0:T(8,128)S(1)}, f32[8,512]{1,0:T(8,128)}, u32[]{:S(2)}) copy-start(f32[8,512]{1,0:T(8,128)} %get-tuple-element.49.skip_l) | copy-start | bytes 49156
  139.4 6.9 %collective-permute-start.3 = (bf16[136,512]{1,0:T(8,128)(2,1)S(1)}, bf16[136,512]{1,0:T(8,128)(2,1)S(1)}, u32[]{:S(2)}, u32[]{:S(2)}) collective-permute-start(bf16[136,512]{1,0:T(8,128)(2,1)S(1)} %get-tuple-element.44.first), channel_id=1, source_target_pairs={{8,0},{16,8},{24,16},{9,1},{17,9},{25,17},{10,2},{18,10},{26,18},{... | collective-permute-start | bytes 417800 | tf_op jit(solution)/shard_map/ppermute | solution.py:532
  140.7 10.2 %collective-permute-start.5 = (bf16[136,512]{1,0:T(8,128)(2,1)S(1)}, bf16[136,512]{1,0:T(8,128)(2,1)S(1)}, u32[]{:S(2)}, u32[]{:S(2)}) collective-permute-start(bf16[136,512]{1,0:T(8,128)(2,1)S(1)} %get-tuple-element.44.first), channel_id=1, source_target_pairs={{24,0},{25,1},{26,2},{27,3},{28,4},{29,5},{30,6},{31,7}} | collective-permute-start | bytes 417800 | tf_op jit(solution)/shard_map/ppermute | solution.py:532
  146.4 7.4 %collective-permute-start.4 = (bf16[136,512]{1,0:T(8,128)(2,1)S(1)}, bf16[136,512]{1,0:T(8,128)(2,1)S(1)}, u32[]{:S(2)}, u32[]{:S(2)}) collective-permute-start(bf16[136,512]{1,0:T(8,128)(2,1)S(1)} %join.1), channel_id=1, source_target_pairs={{8,0},{16,8},{24,16},{9,1},{17,9},{25,17},{10,2},{18,10},{26,18},{... | collective-permute-start | bytes 417800 | tf_op jit(solution)/shard_map/ppermute | solution.py:532
  147.7 6.0 %copy-start.1 = (f32[128,512]{1,0:T(8,128)S(1)}, f32[128,512]{1,0:T(8,128)}, u32[]{:S(2)}) copy-start(f32[128,512]{1,0:T(8,128)} %get-tuple-element.52.refs_6_) | copy-start | bytes 786436
  147.7 6.0 %copy-start.6 = (bf16[128,256]{1,0:T(8,128)(2,1)S(1)}, bf16[128,256]{1,0:T(8,128)(2,1)}, u32[]{:S(2)}) copy-start(bf16[128,256]{1,0:T(8,128)(2,1)} %refs_5_.1) | copy-start | bytes 196612

commit v8 on v7

--- a/solution.py
+++ b/solution.py
@@ -134,7 +134,13 @@
     half = ctx * slots
     blocks = gate_w.shape[0] // block
     parts = [slice(i * block, (i + 1) * block) for i in range(blocks)]
-    swap = launch([pltpu.make_async_copy(other_hbm, other, in_sems.at[2 * blocks + peers])])
+    swap = launch([pltpu.make_async_copy(other_hbm, other, in_sems.at[2 * blocks])])
+    downs = [
+        launch(
+            packed_copies(down_hbm, part, width, 0, both - width, down_w, in_sems, 2 * blocks + 1 + i * peers)
+        )
+        for i, part in enumerate(parts)
+    ]
     pairs = [
         launch(
             [
@@ -144,33 +150,30 @@
         )
         for i, part in enumerate(parts)
     ]
-    downs = launch(
-        packed_copies(down_hbm, slice(0, gate_w.shape[0]), width, 0, both - width, down_w, in_sems, 2 * blocks)
-    )
-    gather_rows(own, 0, 0, width, normed)
     gather_rows(own, 0, width, both, grads)
     finish(swap)
-    gather_rows(other, half, 0, width, normed)
     gather_rows(other, half, width, both, grads)
     outs = []
+    for i, part in enumerate(parts):
+        finish(downs[i])
+        hidden_early[:, part] = dot(grads[...], down_w[part, :], 1, 1)
+        outs += launch(
+            [pltpu.make_async_copy(hidden_early.at[:, part], hidden_hbm.at[:, part], out_sems.at[3 * i + 2])]
+        )
+    gather_rows(own, 0, 0, width, normed)
+    gather_rows(other, half, 0, width, normed)
     for i, part in enumerate(parts):
         finish(pairs[i])
         gate = dot(normed[...], gate_w[part, :], 1, 1)
         up = dot(normed[...], up_w[part, :], 1, 1)
         sig = jax.nn.sigmoid(gate)
-        coef_gate[:, part] = up * sig * (1.0 + gate * (1.0 - sig))
-        coef_up[:, part] = gate * sig
+        coef_gate[:, part] = (up * sig * (1.0 + gate * (1.0 - sig))).astype(coef_gate.dtype)
+        coef_up[:, part] = (gate * sig).astype(coef_up.dtype)
         outs += launch(
             [
                 pltpu.make_async_copy(coef_gate.at[:, part], coef_gate_hbm.at[:, part], out_sems.at[3 * i]),
                 pltpu.make_async_copy(coef_up.at[:, part], coef_up_hbm.at[:, part], out_sems.at[3 * i + 1]),
             ]
-        )
-    finish(downs)
-    for i, part in enumerate(parts):
-        hidden_early[:, part] = dot(grads[...], down_w[part, :], 1, 1)
-        outs += launch(
-            [pltpu.make_async_copy(hidden_early.at[:, part], hidden_hbm.at[:, part], out_sems.at[3 * i + 2])]
         )
     finish(outs)
 
@@ -214,8 +217,8 @@
         late_part = dot(grads[...], down_w[part, :], 1, 1)
         finish(acts)
         grad = hidden_early[:, part] + late_part
-        gate_grad[:, part] = (grad * coef_gate[:, part]).astype(bf16)
-        up_grad[:, part] = (grad * coef_up[:, part]).astype(bf16)
+        gate_grad[:, part] = (grad * coef_gate[:, part].astype(f32)).astype(bf16)
+        up_grad[:, part] = (grad * coef_up[:, part].astype(f32)).astype(bf16)
     for i, cols in enumerate(slabs):
         finish(pairs[i])
         out = (dot(gate_grad[...], gate_w[i], 1, 0) + dot(up_grad[...], up_w[i], 1, 0)).astype(bf16)
@@ -460,12 +463,14 @@
     product = 2 * rows * model * hidden
     any_spec = pl.BlockSpec(memory_space=pl.ANY)
     vmem_spec = pl.BlockSpec(memory_space=pltpu.VMEM)
-    acts = pltpu.VMEM((rows, hidden), f32)
+    coefs = shape((rows, hidden), bf16)
+    coef_buffer = pltpu.VMEM((rows, hidden), bf16)
+    hidden_buffer = pltpu.VMEM((rows, hidden), f32)
     coef_gate, coef_up, hidden_early = pl.pallas_call(
         partial(gate_up_kernel, width=width, block=block),
         in_specs=[vmem_spec] + [any_spec] * 4,
         out_specs=[any_spec] * 3,
-        out_shape=[shape((rows, hidden), f32)] * 3,
+        out_shape=[coefs, coefs, shape((rows, hidden), f32)],
         scratch_shapes=[
             pltpu.VMEM((ctx, peers, slots, width + early), bf16),
             pltpu.VMEM((rows, model), bf16),
@@ -473,10 +478,10 @@
             pltpu.VMEM((hidden, model), bf16),
             pltpu.VMEM((hidden, model), bf16),
             pltpu.VMEM((hidden, peers * early), bf16),
-            acts,
-            acts,
-            acts,
-            pltpu.SemaphoreType.DMA((2 * blocks + peers + 1,)),
+            coef_buffer,
+            coef_buffer,
+            hidden_buffer,
+            pltpu.SemaphoreType.DMA((blocks * (peers + 2) + 1,)),
             pltpu.SemaphoreType.DMA((3 * blocks,)),
         ],
         compiler_params=params(),
@@ -490,9 +495,9 @@
         out_shape=[vmem_out((half, model), bf16)] * 2,
         scratch_shapes=[
             pltpu.VMEM((rows, peers * (width - early)), bf16),
-            acts,
-            acts,
-            acts,
+            hidden_buffer,
+            coef_buffer,
+            coef_buffer,
             pltpu.VMEM((rows, hidden), bf16),
             pltpu.VMEM((rows, hidden), bf16),
             pltpu.VMEM((columns, hidden, column), bf16),

time: 157 us -> 157 us (level)
  transfers between devices with their start and end apart: 9 -> 9, of which waited for: 7 -> 7; matrix products, arithmetic and copies ran while one was open for 0% -> 0% of each run, Pallas kernels for 12% -> 13%
where the time goes in v8:
time: 157 us; the launch traced here: 155 us
  waiting for transfers between devices  84.7 us (54%)
  Pallas kernels  40.1 us (26%)
  starting transfers between devices  16 us (10%)
  blocking collectives  10.8 us (7%)
  local copies, waits for them, and re-layouts  2.38 us (2%)
    all_to_all x2, waiting for transfers between devices, spread(): lax.all_to_all(rows.reshape(ctx * peers, slots, -1), ('ctx', 'exp'), spli...  50.2 us
    all_to_all x1, waiting for transfers between devices, body(): lax.all_to_all(moved.reshape(ctx * peers, slots, width), ('ctx', 'exp'),...  23.2 us
    pallas_call x1, Pallas kernels, body(): pl.pallas_call(partial(back_kernel, width=width, block=block), in_specs=[...  14.1 us
    pallas_call x1, Pallas kernels, body(): pl.pallas_call(partial(gate_up_kernel, width=width, block=block), in_spec...  14 us
    all_to_all x1, blocking collectives, body(): lax.all_to_all(packed, 'exp', split_axis=0, concat_axis=0, tiled=True)  10.8 us
    ppermute x3, waiting for transfers between devices, from_later(): lax.ppermute(window, 'ctx', [(i, i - k) for i in range(k, ctx)])  9.02 us
    all_to_all x2, starting transfers between devices, spread(): lax.all_to_all(rows.reshape(ctx * peers, slots, -1), ('ctx', 'exp'), spli...  7.57 us
    ppermute x3, starting transfers between devices, from_later(): lax.ppermute(window, 'ctx', [(i, i - k) for i in range(k, ctx)])  3.88 us
  transfers between devices with their start and end apart: 9, of which 7 were waited for; matrix products, arithmetic and copies ran while one was open for 0% of the time, Pallas kernels for 13%

profile of v8, /device:TPU:0, one launch (start us, length us, event | category | flops | bytes accessed | tf_op | source)
XLA Modules:
  0.0 154.8 jit_solution(13790112671131156832)
XLA Ops:
  0.6 1.2 pack.1
  1.9 10.8 %all_to_all.20 = bf16[8,16,640]{2,1,0:T(8,128)(2,1)S(1)} all-to-all(bf16[8,16,640]{2,1,0:T(8,128)(2,1)S(1)} %get-tuple-element.29), channel_id=1, replica_groups=mesh['ctx'=4,'exp'=8] {'exp'}, dimensions={0} | all-to-all | bytes 327680 | tf_op jit(solution)/shard_map/all_to_all | solution.py:408
  12.7 1.6 %dispatch.1 = (bf16[256,128]{1,0:T(8,128)(2,1)S(1)}, bf16[4,256,640]{2,1,0:T(8,128)(2,1)}) custom-call(bf16[128,640]{1,0:T(8,128)(2,1)S(1)} %bitcast.19, bf16[128,128]{1,0:T(8,128)(2,1)S(1)} %get-tuple-element.30.grad), custom_call_target="tpu_custom_call" | custom-call | tf_op jit(solution)/shard_map/dispatch/pallas_call | solution.py:428
  14.3 4.0 %all-to-all-start.2 = ((bf16[32,32,640]{2,1,0:T(8,128)(2,1)}), bf16[32,32,640]{2,1,0:T(8,128)(2,1)S(1)}, u32[]{:S(2)}, u32[]{:S(2)}) async-start(bf16[32,32,640]{2,1,0:T(8,128)(2,1)} %bitcast.6), calls=%async_computation.2 | async-start | bytes 2621440 | tf_op jit(solution)/shard_map/all_to_all | solution.py:450
  18.3 2.1 %select.1 = (bf16[256,128]{1,0:T(8,128)(2,1)S(1)}, f32[128,128]{1,0:T(8,128)S(1)}, bf16[4,256,384]{2,1,0:T(8,128)(2,1)}) custom-call(bf16[128,640]{1,0:T(8,128)(2,1)S(1)} %bitcast.20, bf16[256,128]{1,0:T(8,128)(2,1)S(1)} %get-tuple-element.31.table, bf16[128,512]{1,0:T(8,128)(2,1)} %grad.5), custom_call_target="tpu_custom_call" | custom-call | flops 1000000000 | bytes 2000000 | tf_op jit(solution)/shard_map/select/pallas_call | solution.py:437
  20.4 29.9 %all-to-all-done.2 = bf16[32,32,640]{2,1,0:T(8,128)(2,1)S(1)} async-done(((bf16[32,32,640]{2,1,0:T(8,128)(2,1)}), bf16[32,32,640]{2,1,0:T(8,128)(2,1)S(1)}, u32[]{:S(2)}, u32[]{:S(2)}) %all-to-all-start.2) | async-done | bytes 1310752 | tf_op jit(solution)/shard_map/all_to_all | solution.py:450
  50.2 3.6 %all-to-all-start.1 = ((bf16[32,32,384]{2,1,0:T(8,128)(2,1)}), bf16[32,32,384]{2,1,0:T(8,128)(2,1)S(1)}, u32[]{:S(2)}, u32[]{:S(2)}) async-start(bf16[32,32,384]{2,1,0:T(8,128)(2,1)} %bitcast.4), calls=%async_computation.1 | async-start | bytes 1572864 | tf_op jit(solution)/shard_map/all_to_all | solution.py:450
  54.2 20.3 %all-to-all-done.1 = bf16[32,32,384]{2,1,0:T(8,128)(2,1)S(1)} async-done(((bf16[32,32,384]{2,1,0:T(8,128)(2,1)}), bf16[32,32,384]{2,1,0:T(8,128)(2,1)S(1)}, u32[]{:S(2)}, u32[]{:S(2)}) %all-to-all-start.1) | async-done | bytes 786464 | tf_op jit(solution)/shard_map/all_to_all | solution.py:450
  74.4 14.0 %gate_up.1 = (bf16[256,1536]{1,0:T(8,128)(2,1)}, bf16[256,1536]{1,0:T(8,128)(2,1)}, f32[256,1536]{1,0:T(8,128)}) custom-call(bf16[4,8,32,640]{3,2,1,0:T(8,128)(2,1)S(1)} %bitcast.14, bf16[4,8,32,640]{3,2,1,0:T(8,128)(2,1)} %collective-permute-done.1.other_hbm, bf16[1,1536,4096]{2,1,0:T(8,128)(2,1)} %gate_hbm.3, bf16[1,1536,4096]{2,1,0:T(8,128)(2,1)} %up_hbm.3, ...), custom_call_target="tpu_custom_call" | custom-call | flops 8053063680 | bytes 25165824 | tf_op jit(solution)/shard_map/gate_up/pallas_call | solution.py:469
  88.4 14.1 %back.1 = (bf16[128,4096]{1,0:T(8,128)(2,1)S(1)}, bf16[128,4096]{1,0:T(8,128)(2,1)S(1)}) custom-call(bf16[4,8,32,384]{3,2,1,0:T(8,128)(2,1)S(1)} %bitcast.18, bf16[4,8,32,384]{3,2,1,0:T(8,128)(2,1)S(1)} %collective-permute-done.other, f32[256,1536]{1,0:T(8,128)} %get-tuple-element.34.hidden_hbm, bf16[256,1536]{1,0:T(8,128)(2,1)} %get-tuple-element.35.coef_gate_hbm, ...), custom_call_target="tpu_custom_call" | custom-call | flops 8053063680 | bytes 37748736 | tf_op jit(solution)/shard_map/back/pallas_call | solution.py:491
  103.2 2.3 %collective-permute-done.2.swapped = bf16[128,4096]{1,0:T(8,128)(2,1)S(1)} collective-permute-done((bf16[128,4096]{1,0:T(8,128)(2,1)S(1)}, bf16[128,4096]{1,0:T(8,128)(2,1)S(1)}, u32[]{:S(2)}, u32[]{:S(2)}) %collective-permute-start.2) | collective-permute-done | bytes 1048608 | tf_op jit(solution)/shard_map/ppermute | solution.py:513
  105.4 1.9 %slot.1 = bf16[4,8,32,512]{3,2,1,0:T(8,128)(2,1)} custom-call(bf16[128,4096]{1,0:T(8,128)(2,1)S(1)} %get-tuple-element.37.own, bf16[128,4096]{1,0:T(8,128)(2,1)S(1)} %collective-permute-done.2.swapped, f32[1,4096]{1,0:T(1,128)S(1)} %bitcast.22, bf16[4,8,32,640]{3,2,1,0:T(8,128)(2,1)S(1)} %bitcast.15), custom_call_target="tpu_custom_call" | custom-call | tf_op jit(solution)/shard_map/slot/pallas_call | solution.py:514
  107.4 3.6 %all-to-all-start.3 = ((bf16[32,32,512]{2,1,0:T(8,128)(2,1)}), bf16[32,32,512]{2,1,0:T(8,128)(2,1)S(1)}, u32[]{:S(2)}, u32[]{:S(2)}) async-start(bf16[32,32,512]{2,1,0:T(8,128)(2,1)} %bitcast.8), calls=%async_computation.3 | async-start | bytes 2097152 | tf_op jit(solution)/shard_map/all_to_all | solution.py:521
  111.0 3.0 %mixer_setup.1 = (bf16[8,128,128]{2,1,0:T(8,128)(2,1)}, f32[8,128,128]{2,1,0:T(8,128)}, f32[128,512]{1,0:T(8,128)}, f32[128,512]{1,0:T(8,128)}, f32[128,512]{1,0...) custom-call(f32[8,128]{1,0:T(8,128)} %bitcast.25, f32[8,128]{1,0:T(8,128)} %bitcast.26, f32[1,8]{1,0:T(1,128)} %bitcast.27, ...), custom_call_target="tpu_custom_call" | custom-call | flops 2000000000 | bytes 2000000 | tf_op jit(solution)/shard_map/mixer_setup/pallas_call | solution.py:412
  114.0 23.2 %all-to-all-done.3 = bf16[32,32,512]{2,1,0:T(8,128)(2,1)S(1)} async-done(((bf16[32,32,512]{2,1,0:T(8,128)(2,1)}), bf16[32,32,512]{2,1,0:T(8,128)(2,1)S(1)}, u32[]{:S(2)}, u32[]{:S(2)}) %all-to-all-start.3) | async-done | bytes 1048608 | tf_op jit(solution)/shard_map/all_to_all | solution.py:521
  137.2 0.9 copy-done.2
  138.2 0.7 copy-done.7
  139.4 1.3 collective-permute-start.3
  140.7 1.3 collective-permute-start.5
  142.0 4.3 %collective-permute-done.3.later = bf16[136,512]{1,0:T(8,128)(2,1)S(1)} collective-permute-done((bf16[136,512]{1,0:T(8,128)(2,1)S(1)}, bf16[136,512]{1,0:T(8,128)(2,1)S(1)}, u32[]{:S(2)}, u32[]{:S(2)}) %collective-permute-start.3) | collective-permute-done | bytes 139296 | tf_op jit(solution)/shard_map/ppermute | solution.py:537
  146.4 1.3 collective-permute-start.4
  149.1 1.8 %collective-permute-done.5.refs_1_ = bf16[136,512]{1,0:T(8,128)(2,1)S(1)} collective-permute-done((bf16[136,512]{1,0:T(8,128)(2,1)S(1)}, bf16[136,512]{1,0:T(8,128)(2,1)S(1)}, u32[]{:S(2)}, u32[]{:S(2)}) %collective-permute-start.5) | collective-permute-done | bytes 139296 | tf_op jit(solution)/shard_map/ppermute | solution.py:537
  150.9 2.9 %collective-permute-done.4.refs_0_ = bf16[136,512]{1,0:T(8,128)(2,1)S(1)} collective-permute-done((bf16[136,512]{1,0:T(8,128)(2,1)S(1)}, bf16[136,512]{1,0:T(8,128)(2,1)S(1)}, u32[]{:S(2)}, u32[]{:S(2)}) %collective-permute-start.4) | collective-permute-done | bytes 139296 | tf_op jit(solution)/shard_map/ppermute | solution.py:537
  153.8 0.9 mixer_far.1
  (31 shorter events, 2.9 us)
Async XLA Ops:
  14.3 35.9 %all-to-all-start.2 = ((bf16[32,32,640]{2,1,0:T(8,128)(2,1)}), bf16[32,32,640]{2,1,0:T(8,128)(2,1)S(1)}, u32[]{:S(2)}, u32[]{:S(2)}) async-start(bf16[32,32,640]{2,1,0:T(8,128)(2,1)} %bitcast.6), calls=%async_computation.2 | async-start | bytes 2621440 | tf_op jit(solution)/shard_map/all_to_all | solution.py:450
  50.2 24.2 %all-to-all-start.1 = ((bf16[32,32,384]{2,1,0:T(8,128)(2,1)}), bf16[32,32,384]{2,1,0:T(8,128)(2,1)S(1)}, u32[]{:S(2)}, u32[]{:S(2)}) async-start(bf16[32,32,384]{2,1,0:T(8,128)(2,1)} %bitcast.4), calls=%async_computation.1 | async-start | bytes 1572864 | tf_op jit(solution)/shard_map/all_to_all | solution.py:450
  53.8 20.6 %collective-permute-start.1 = (bf16[4,8,32,640]{3,2,1,0:T(8,128)(2,1)S(1)}, bf16[4,8,32,640]{3,2,1,0:T(8,128)(2,1)}, u32[]{:S(2)}, u32[]{:S(2)}) collective-permute-start(bf16[4,8,32,640]{3,2,1,0:T(8,128)(2,1)S(1)} %bitcast.13), channel_id=1, source_target_pairs={{0,1},{1,0},{2,3},{3,2},{4,5},{5,4},{6,7},{7,6},{8,9},{9,8},{10,11... | collective-permute-start | bytes 3932168 | tf_op jit(solution)/shard_map/ppermute | solution.py:453
  74.4 14.0 %collective-permute-start = (bf16[4,8,32,384]{3,2,1,0:T(8,128)(2,1)S(1)}, bf16[4,8,32,384]{3,2,1,0:T(8,128)(2,1)S(1)}, u32[]{:S(2)}, u32[]{:S(2)}) collective-permute-start(bf16[4,8,32,384]{3,2,1,0:T(8,128)(2,1)S(1)} %bitcast.17), channel_id=1, source_target_pairs={{0,1},{1,0},{2,3},{3,2},{4,5},{5,4},{6,7},{7,6},{8,9},{9,8},{10,11... | collective-permute-start | bytes 2359304 | tf_op jit(solution)/shard_map/ppermute | solution.py:453
  88.4 17.0 %copy-start.4 = (f32[4096]{0:T(1024)S(1)}, f32[4096]{0:T(1024)}, u32[]{:S(2)}) copy-start(f32[4096]{0:T(1024)} %param.15) | copy-start | bytes 49156
  102.6 2.9 %collective-permute-start.2 = (bf16[128,4096]{1,0:T(8,128)(2,1)S(1)}, bf16[128,4096]{1,0:T(8,128)(2,1)S(1)}, u32[]{:S(2)}, u32[]{:S(2)}) collective-permute-start(bf16[128,4096]{1,0:T(8,128)(2,1)S(1)} %get-tuple-element.38), channel_id=1, source_target_pairs={{0,1},{1,0},{2,3},{3,2},{4,5},{5,4},{6,7},{7,6},{8,9},{9,8},{10,11... | collective-permute-start | bytes 3145736 | tf_op jit(solution)/shard_map/ppermute | solution.py:513
  107.4 29.8 %all-to-all-start.3 = ((bf16[32,32,512]{2,1,0:T(8,128)(2,1)}), bf16[32,32,512]{2,1,0:T(8,128)(2,1)S(1)}, u32[]{:S(2)}, u32[]{:S(2)}) async-start(bf16[32,32,512]{2,1,0:T(8,128)(2,1)} %bitcast.8), calls=%async_computation.3 | async-start | bytes 2097152 | tf_op jit(solution)/shard_map/all_to_all | solution.py:521
  111.0 26.2 %copy-start = (bf16[128,512]{1,0:T(8,128)(2,1)S(1)}, bf16[128,512]{1,0:T(8,128)(2,1)}, u32[]{:S(2)}) copy-start(bf16[128,512]{1,0:T(8,128)(2,1)} %grad.5) | copy-start | bytes 393220
  111.0 26.2 %copy-start.5 = (bf16[128,256]{1,0:T(8,128)(2,1)S(1)}, bf16[128,256]{1,0:T(8,128)(2,1)}, u32[]{:S(2)}) copy-start(bf16[128,256]{1,0:T(8,128)(2,1)} %state_out.5) | copy-start | bytes 196612
  111.0 36.7 %copy-start.3 = (bf16[128,512]{1,0:T(8,128)(2,1)S(1)}, bf16[128,512]{1,0:T(8,128)(2,1)}, u32[]{:S(2)}) copy-start(bf16[128,512]{1,0:T(8,128)(2,1)} %refs_4_.1) | copy-start | bytes 393220
  137.2 1.0 copy-start.2
  138.2 0.7 copy-start.7
  138.9 8.9 %copy-start.8 = (f32[8,128,128]{2,1,0:T(8,128)S(1)}, f32[8,128,128]{2,1,0:T(8,128)}, u32[]{:S(2)}) copy-start(f32[8,128,128]{2,1,0:T(8,128)} %get-tuple-element.47.weigh) | copy-start | bytes 1572868
  138.9 8.9 %copy-start.9 = (bf16[8,128,128]{2,1,0:T(8,128)(2,1)S(1)}, bf16[8,128,128]{2,1,0:T(8,128)(2,1)}, u32[]{:S(2)}) copy-start(bf16[8,128,128]{2,1,0:T(8,128)(2,1)} %get-tuple-element.46.mix) | copy-start | bytes 786436
  138.9 8.9 %copy-start.10 = (f32[128,512]{1,0:T(8,128)S(1)}, f32[128,512]{1,0:T(8,128)}, u32[]{:S(2)}) copy-start(f32[128,512]{1,0:T(8,128)} %get-tuple-element.48.step_l) | copy-start | bytes 786436
  138.9 8.9 %copy-start.11 = (f32[8,512]{1,0:T(8,128)S(1)}, f32[8,512]{1,0:T(8,128)}, u32[]{:S(2)}) copy-start(f32[8,512]{1,0:T(8,128)} %get-tuple-element.49.skip_l) | copy-start | bytes 49156
  139.4 6.9 %collective-permute-start.3 = (bf16[136,512]{1,0:T(8,128)(2,1)S(1)}, bf16[136,512]{1,0:T(8,128)(2,1)S(1)}, u32[]{:S(2)}, u32[]{:S(2)}) collective-permute-start(bf16[136,512]{1,0:T(8,128)(2,1)S(1)} %get-tuple-element.44.first), channel_id=1, source_target_pairs={{8,0},{16,8},{24,16},{9,1},{17,9},{25,17},{10,2},{18,10},{26,18},{... | collective-permute-start | bytes 417800 | tf_op jit(solution)/shard_map/ppermute | solution.py:537
  140.7 10.2 %collective-permute-start.5 = (bf16[136,512]{1,0:T(8,128)(2,1)S(1)}, bf16[136,512]{1,0:T(8,128)(2,1)S(1)}, u32[]{:S(2)}, u32[]{:S(2)}) collective-permute-start(bf16[136,512]{1,0:T(8,128)(2,1)S(1)} %get-tuple-element.44.first), channel_id=1, source_target_pairs={{24,0},{25,1},{26,2},{27,3},{28,4},{29,5},{30,6},{31,7}} | collective-permute-start | bytes 417800 | tf_op jit(solution)/shard_map/ppermute | solution.py:537
  146.4 7.4 %collective-permute-start.4 = (bf16[136,512]{1,0:T(8,128)(2,1)S(1)}, bf16[136,512]{1,0:T(8,128)(2,1)S(1)}, u32[]{:S(2)}, u32[]{:S(2)}) collective-permute-start(bf16[136,512]{1,0:T(8,128)(2,1)S(1)} %join.1), channel_id=1, source_target_pairs={{8,0},{16,8},{24,16},{9,1},{17,9},{25,17},{10,2},{18,10},{26,18},{... | collective-permute-start | bytes 417800 | tf_op jit(solution)/shard_map/ppermute | solution.py:537
  147.8 6.1 %copy-start.1 = (f32[128,512]{1,0:T(8,128)S(1)}, f32[128,512]{1,0:T(8,128)}, u32[]{:S(2)}) copy-start(f32[128,512]{1,0:T(8,128)} %get-tuple-element.52.refs_6_) | copy-start | bytes 786436
  147.8 6.0 %copy-start.6 = (bf16[128,256]{1,0:T(8,128)(2,1)S(1)}, bf16[128,256]{1,0:T(8,128)(2,1)}, u32[]{:S(2)}) copy-start(bf16[128,256]{1,0:T(8,128)(2,1)} %refs_5_.1) | copy-start | bytes 196612

commit v9 on v8

--- a/solution.py
+++ b/solution.py
@@ -156,7 +156,7 @@
     outs = []
     for i, part in enumerate(parts):
         finish(downs[i])
-        hidden_early[:, part] = dot(grads[...], down_w[part, :], 1, 1)
+        hidden_early[:, part] = dot(grads[...], down_w[part, :], 1, 1).astype(hidden_early.dtype)
         outs += launch(
             [pltpu.make_async_copy(hidden_early.at[:, part], hidden_hbm.at[:, part], out_sems.at[3 * i + 2])]
         )
@@ -216,7 +216,7 @@
         finish(downs)
         late_part = dot(grads[...], down_w[part, :], 1, 1)
         finish(acts)
-        grad = hidden_early[:, part] + late_part
+        grad = hidden_early[:, part].astype(f32) + late_part
         gate_grad[:, part] = (grad * coef_gate[:, part].astype(f32)).astype(bf16)
         up_grad[:, part] = (grad * coef_up[:, part].astype(f32)).astype(bf16)
     for i, cols in enumerate(slabs):
@@ -465,12 +465,12 @@
     vmem_spec = pl.BlockSpec(memory_space=pltpu.VMEM)
     coefs = shape((rows, hidden), bf16)
     coef_buffer = pltpu.VMEM((rows, hidden), bf16)
-    hidden_buffer = pltpu.VMEM((rows, hidden), f32)
+    hidden_buffer = pltpu.VMEM((rows, hidden), bf16)
     coef_gate, coef_up, hidden_early = pl.pallas_call(
         partial(gate_up_kernel, width=width, block=block),
         in_specs=[vmem_spec] + [any_spec] * 4,
         out_specs=[any_spec] * 3,
-        out_shape=[coefs, coefs, shape((rows, hidden), f32)],
+        out_shape=[coefs, coefs, coefs],
         scratch_shapes=[
             pltpu.VMEM((ctx, peers, slots, width + early), bf16),
             pltpu.VMEM((rows, model), bf16),

time: 157 us -> 157 us (level)
  local copies, waits for them, and re-layouts: 2.38 us -> 6.01 us
  waiting for transfers between devices: 84.7 us -> 81.2 us
    unnamed x25, local copies, waits for them, and re-layouts: 2.38 us -> 6.01 us
    ppermute x3, waiting for transfers between devices: 9.02 us -> 5.42 us  [from_later(): lax.ppermute(window, 'ctx', [(i, i - k) for i in range(k, ctx)])]
  transfers between devices with their start and end apart: 9 -> 9, of which waited for: 7 -> 6; matrix products, arithmetic and copies ran while one was open for 0% -> 0% of each run, Pallas kernels for 13% -> 13%
where the time goes in v9:
time: 157 us; the launch traced here: 154 us
  waiting for transfers between devices  81.2 us (52%)
  Pallas kernels  39.6 us (25%)
  starting transfers between devices  16 us (10%)
  blocking collectives  10.8 us (7%)
  local copies, waits for them, and re-layouts  6.01 us (4%)
    all_to_all x2, waiting for transfers between devices, spread(): lax.all_to_all(rows.reshape(ctx * peers, slots, -1), ('ctx', 'exp'), spli...  50.2 us
    all_to_all x1, waiting for transfers between devices, body(): lax.all_to_all(moved.reshape(ctx * peers, slots, width), ('ctx', 'exp'),...  23.3 us
    pallas_call x1, Pallas kernels, body(): pl.pallas_call(partial(back_kernel, width=width, block=block), in_specs=[...  14 us
    pallas_call x1, Pallas kernels, body(): pl.pallas_call(partial(gate_up_kernel, width=width, block=block), in_spec...  13.8 us
    all_to_all x1, blocking collectives, body(): lax.all_to_all(packed, 'exp', split_axis=0, concat_axis=0, tiled=True)  10.8 us
    all_to_all x2, starting transfers between devices, spread(): lax.all_to_all(rows.reshape(ctx * peers, slots, -1), ('ctx', 'exp'), spli...  7.57 us
    unnamed x25, local copies, waits for them, and re-layouts  6.01 us
    ppermute x3, waiting for transfers between devices, from_later(): lax.ppermute(window, 'ctx', [(i, i - k) for i in range(k, ctx)])  5.42 us
  transfers between devices with their start and end apart: 9, of which 6 were waited for; matrix products, arithmetic and copies ran while one was open for 0% of the time, Pallas kernels for 13%

profile of v9, /device:TPU:0, one launch (start us, length us, event | category | flops | bytes accessed | tf_op | source)
XLA Modules:
  0.0 154.4 jit_solution(4810680932223512463)
XLA Ops:
  0.6 1.2 pack.1
  1.9 10.8 %all_to_all.20 = bf16[8,16,640]{2,1,0:T(8,128)(2,1)S(1)} all-to-all(bf16[8,16,640]{2,1,0:T(8,128)(2,1)S(1)} %get-tuple-element.29), channel_id=1, replica_groups=mesh['ctx'=4,'exp'=8] {'exp'}, dimensions={0} | all-to-all | bytes 327680 | tf_op jit(solution)/shard_map/all_to_all | solution.py:408
  12.7 1.6 %dispatch.1 = (bf16[256,128]{1,0:T(8,128)(2,1)S(1)}, bf16[4,256,640]{2,1,0:T(8,128)(2,1)}) custom-call(bf16[128,640]{1,0:T(8,128)(2,1)S(1)} %bitcast.19, bf16[128,128]{1,0:T(8,128)(2,1)S(1)} %get-tuple-element.30.grad), custom_call_target="tpu_custom_call" | custom-call | tf_op jit(solution)/shard_map/dispatch/pallas_call | solution.py:428
  14.3 4.0 %all-to-all-start.2 = ((bf16[32,32,640]{2,1,0:T(8,128)(2,1)}), bf16[32,32,640]{2,1,0:T(8,128)(2,1)S(1)}, u32[]{:S(2)}, u32[]{:S(2)}) async-start(bf16[32,32,640]{2,1,0:T(8,128)(2,1)} %bitcast.6), calls=%async_computation.2 | async-start | bytes 2621440 | tf_op jit(solution)/shard_map/all_to_all | solution.py:450
  18.3 2.1 %select.1 = (bf16[256,128]{1,0:T(8,128)(2,1)S(1)}, f32[128,128]{1,0:T(8,128)S(1)}, bf16[4,256,384]{2,1,0:T(8,128)(2,1)}) custom-call(bf16[128,640]{1,0:T(8,128)(2,1)S(1)} %bitcast.20, bf16[256,128]{1,0:T(8,128)(2,1)S(1)} %get-tuple-element.31.table, bf16[128,512]{1,0:T(8,128)(2,1)} %grad.5), custom_call_target="tpu_custom_call" | custom-call | flops 1000000000 | bytes 2000000 | tf_op jit(solution)/shard_map/select/pallas_call | solution.py:437
  20.3 29.9 %all-to-all-done.2 = bf16[32,32,640]{2,1,0:T(8,128)(2,1)S(1)} async-done(((bf16[32,32,640]{2,1,0:T(8,128)(2,1)}), bf16[32,32,640]{2,1,0:T(8,128)(2,1)S(1)}, u32[]{:S(2)}, u32[]{:S(2)}) %all-to-all-start.2) | async-done | bytes 1310752 | tf_op jit(solution)/shard_map/all_to_all | solution.py:450
  50.2 3.6 %all-to-all-start.1 = ((bf16[32,32,384]{2,1,0:T(8,128)(2,1)}), bf16[32,32,384]{2,1,0:T(8,128)(2,1)S(1)}, u32[]{:S(2)}, u32[]{:S(2)}) async-start(bf16[32,32,384]{2,1,0:T(8,128)(2,1)} %bitcast.4), calls=%async_computation.1 | async-start | bytes 1572864 | tf_op jit(solution)/shard_map/all_to_all | solution.py:450
  54.2 20.3 %all-to-all-done.1 = bf16[32,32,384]{2,1,0:T(8,128)(2,1)S(1)} async-done(((bf16[32,32,384]{2,1,0:T(8,128)(2,1)}), bf16[32,32,384]{2,1,0:T(8,128)(2,1)S(1)}, u32[]{:S(2)}, u32[]{:S(2)}) %all-to-all-start.1) | async-done | bytes 786464 | tf_op jit(solution)/shard_map/all_to_all | solution.py:450
  74.4 13.8 %gate_up.1 = (bf16[256,1536]{1,0:T(8,128)(2,1)}, bf16[256,1536]{1,0:T(8,128)(2,1)}, bf16[256,1536]{1,0:T(8,128)(2,1)}) custom-call(bf16[4,8,32,640]{3,2,1,0:T(8,128)(2,1)S(1)} %bitcast.14, bf16[4,8,32,640]{3,2,1,0:T(8,128)(2,1)} %collective-permute-done.1.other_hbm, bf16[1,1536,4096]{2,1,0:T(8,128)(2,1)} %gate_hbm.3, bf16[1,1536,4096]{2,1,0:T(8,128)(2,1)} %up_hbm.3, ...), custom_call_target="tpu_custom_call" | custom-call | flops 8053063680 | bytes 25165824 | tf_op jit(solution)/shard_map/gate_up/pallas_call | solution.py:469
  88.2 14.0 %back.1 = (bf16[128,4096]{1,0:T(8,128)(2,1)S(1)}, bf16[128,4096]{1,0:T(8,128)(2,1)S(1)}) custom-call(bf16[4,8,32,384]{3,2,1,0:T(8,128)(2,1)S(1)} %bitcast.18, bf16[4,8,32,384]{3,2,1,0:T(8,128)(2,1)S(1)} %collective-permute-done.other, bf16[256,1536]{1,0:T(8,128)(2,1)} %get-tuple-element.34.hidden_hbm, bf16[256,1536]{1,0:T(8,128)(2,1)} %get-tuple-element.35.coef_gate_hbm, ...), custom_call_target="tpu_custom_call" | custom-call | flops 8053063680 | bytes 37748736 | tf_op jit(solution)/shard_map/back/pallas_call | solution.py:491
  102.8 2.3 %collective-permute-done.2.swapped = bf16[128,4096]{1,0:T(8,128)(2,1)S(1)} collective-permute-done((bf16[128,4096]{1,0:T(8,128)(2,1)S(1)}, bf16[128,4096]{1,0:T(8,128)(2,1)S(1)}, u32[]{:S(2)}, u32[]{:S(2)}) %collective-permute-start.2) | collective-permute-done | bytes 1048608 | tf_op jit(solution)/shard_map/ppermute | solution.py:513
  105.1 1.9 %slot.1 = bf16[4,8,32,512]{3,2,1,0:T(8,128)(2,1)} custom-call(bf16[128,4096]{1,0:T(8,128)(2,1)S(1)} %get-tuple-element.37.own, bf16[128,4096]{1,0:T(8,128)(2,1)S(1)} %collective-permute-done.2.swapped, f32[1,4096]{1,0:T(1,128)S(1)} %bitcast.22, bf16[4,8,32,640]{3,2,1,0:T(8,128)(2,1)S(1)} %bitcast.15), custom_call_target="tpu_custom_call" | custom-call | tf_op jit(solution)/shard_map/slot/pallas_call | solution.py:514
  107.1 3.6 %all-to-all-start.3 = ((bf16[32,32,512]{2,1,0:T(8,128)(2,1)}), bf16[32,32,512]{2,1,0:T(8,128)(2,1)S(1)}, u32[]{:S(2)}, u32[]{:S(2)}) async-start(bf16[32,32,512]{2,1,0:T(8,128)(2,1)} %bitcast.8), calls=%async_computation.3 | async-start | bytes 2097152 | tf_op jit(solution)/shard_map/all_to_all | solution.py:521
  110.7 2.9 %mixer_setup.1 = (bf16[8,128,128]{2,1,0:T(8,128)(2,1)}, f32[8,128,128]{2,1,0:T(8,128)}, f32[128,512]{1,0:T(8,128)}, f32[128,512]{1,0:T(8,128)}, f32[128,512]{1,0...) custom-call(f32[8,128]{1,0:T(8,128)} %bitcast.25, f32[8,128]{1,0:T(8,128)} %bitcast.26, f32[1,8]{1,0:T(1,128)} %bitcast.27, ...), custom_call_target="tpu_custom_call" | custom-call | flops 2000000000 | bytes 2000000 | tf_op jit(solution)/shard_map/mixer_setup/pallas_call | solution.py:412
  113.6 23.3 %all-to-all-done.3 = bf16[32,32,512]{2,1,0:T(8,128)(2,1)S(1)} async-done(((bf16[32,32,512]{2,1,0:T(8,128)(2,1)}), bf16[32,32,512]{2,1,0:T(8,128)(2,1)S(1)}, u32[]{:S(2)}, u32[]{:S(2)}) %all-to-all-start.3) | async-done | bytes 1048608 | tf_op jit(solution)/shard_map/all_to_all | solution.py:521
  136.9 0.9 copy-done.2
  139.1 1.3 collective-permute-start.3
  140.4 1.3 collective-permute-start.5
  141.7 4.3 %collective-permute-done.3.later = bf16[136,512]{1,0:T(8,128)(2,1)S(1)} collective-permute-done((bf16[136,512]{1,0:T(8,128)(2,1)S(1)}, bf16[136,512]{1,0:T(8,128)(2,1)S(1)}, u32[]{:S(2)}, u32[]{:S(2)}) %collective-permute-start.3) | collective-permute-done | bytes 139296 | tf_op jit(solution)/shard_map/ppermute | solution.py:537
  146.1 1.3 collective-permute-start.4
  147.4 1.0 copy-done.8
  148.4 0.9 copy-done.9
  149.4 0.9 copy-done.10
  152.4 1.1 collective-permute-done.4.refs_0_
  (31 shorter events, 5.2 us)
Async XLA Ops:
  14.3 35.9 %all-to-all-start.2 = ((bf16[32,32,640]{2,1,0:T(8,128)(2,1)}), bf16[32,32,640]{2,1,0:T(8,128)(2,1)S(1)}, u32[]{:S(2)}, u32[]{:S(2)}) async-start(bf16[32,32,640]{2,1,0:T(8,128)(2,1)} %bitcast.6), calls=%async_computation.2 | async-start | bytes 2621440 | tf_op jit(solution)/shard_map/all_to_all | solution.py:450
  50.2 24.2 %all-to-all-start.1 = ((bf16[32,32,384]{2,1,0:T(8,128)(2,1)}), bf16[32,32,384]{2,1,0:T(8,128)(2,1)S(1)}, u32[]{:S(2)}, u32[]{:S(2)}) async-start(bf16[32,32,384]{2,1,0:T(8,128)(2,1)} %bitcast.4), calls=%async_computation.1 | async-start | bytes 1572864 | tf_op jit(solution)/shard_map/all_to_all | solution.py:450
  53.8 20.6 %collective-permute-start.1 = (bf16[4,8,32,640]{3,2,1,0:T(8,128)(2,1)S(1)}, bf16[4,8,32,640]{3,2,1,0:T(8,128)(2,1)}, u32[]{:S(2)}, u32[]{:S(2)}) collective-permute-start(bf16[4,8,32,640]{3,2,1,0:T(8,128)(2,1)S(1)} %bitcast.13), channel_id=1, source_target_pairs={{0,1},{1,0},{2,3},{3,2},{4,5},{5,4},{6,7},{7,6},{8,9},{9,8},{10,11... | collective-permute-start | bytes 3932168 | tf_op jit(solution)/shard_map/ppermute | solution.py:453
  74.4 13.8 %collective-permute-start = (bf16[4,8,32,384]{3,2,1,0:T(8,128)(2,1)S(1)}, bf16[4,8,32,384]{3,2,1,0:T(8,128)(2,1)S(1)}, u32[]{:S(2)}, u32[]{:S(2)}) collective-permute-start(bf16[4,8,32,384]{3,2,1,0:T(8,128)(2,1)S(1)} %bitcast.17), channel_id=1, source_target_pairs={{0,1},{1,0},{2,3},{3,2},{4,5},{5,4},{6,7},{7,6},{8,9},{9,8},{10,11... | collective-permute-start | bytes 2359304 | tf_op jit(solution)/shard_map/ppermute | solution.py:453
  88.2 16.9 %copy-start.4 = (f32[4096]{0:T(1024)S(1)}, f32[4096]{0:T(1024)}, u32[]{:S(2)}) copy-start(f32[4096]{0:T(1024)} %param.15) | copy-start | bytes 49156
  102.2 34.7 %copy-start = (bf16[128,512]{1,0:T(8,128)(2,1)S(1)}, bf16[128,512]{1,0:T(8,128)(2,1)}, u32[]{:S(2)}) copy-start(bf16[128,512]{1,0:T(8,128)(2,1)} %grad.5) | copy-start | bytes 393220
  102.2 34.6 %copy-start.5 = (bf16[128,256]{1,0:T(8,128)(2,1)S(1)}, bf16[128,256]{1,0:T(8,128)(2,1)}, u32[]{:S(2)}) copy-start(bf16[128,256]{1,0:T(8,128)(2,1)} %state_out.5) | copy-start | bytes 196612
  102.3 45.1 %copy-start.3 = (bf16[128,512]{1,0:T(8,128)(2,1)S(1)}, bf16[128,512]{1,0:T(8,128)(2,1)}, u32[]{:S(2)}) copy-start(bf16[128,512]{1,0:T(8,128)(2,1)} %refs_4_.1) | copy-start | bytes 393220
  102.3 2.9 %collective-permute-start.2 = (bf16[128,4096]{1,0:T(8,128)(2,1)S(1)}, bf16[128,4096]{1,0:T(8,128)(2,1)S(1)}, u32[]{:S(2)}, u32[]{:S(2)}) collective-permute-start(bf16[128,4096]{1,0:T(8,128)(2,1)S(1)} %get-tuple-element.38), channel_id=1, source_target_pairs={{0,1},{1,0},{2,3},{3,2},{4,5},{5,4},{6,7},{7,6},{8,9},{9,8},{10,11... | collective-permute-start | bytes 3145736 | tf_op jit(solution)/shard_map/ppermute | solution.py:513
  107.0 46.4 %copy-start.6 = (bf16[128,256]{1,0:T(8,128)(2,1)S(1)}, bf16[128,256]{1,0:T(8,128)(2,1)}, u32[]{:S(2)}) copy-start(bf16[128,256]{1,0:T(8,128)(2,1)} %refs_5_.1) | copy-start | bytes 196612
  107.1 29.8 %all-to-all-start.3 = ((bf16[32,32,512]{2,1,0:T(8,128)(2,1)}), bf16[32,32,512]{2,1,0:T(8,128)(2,1)S(1)}, u32[]{:S(2)}, u32[]{:S(2)}) async-start(bf16[32,32,512]{2,1,0:T(8,128)(2,1)} %bitcast.8), calls=%async_computation.3 | async-start | bytes 2097152 | tf_op jit(solution)/shard_map/all_to_all | solution.py:521
  113.6 39.9 %copy-start.1 = (f32[128,512]{1,0:T(8,128)S(1)}, f32[128,512]{1,0:T(8,128)}, u32[]{:S(2)}) copy-start(f32[128,512]{1,0:T(8,128)} %get-tuple-element.52.refs_6_) | copy-start | bytes 786436
  136.9 1.0 copy-start.2
  137.8 0.7 copy-start.7
  139.1 6.9 %collective-permute-start.3 = (bf16[136,512]{1,0:T(8,128)(2,1)S(1)}, bf16[136,512]{1,0:T(8,128)(2,1)S(1)}, u32[]{:S(2)}, u32[]{:S(2)}) collective-permute-start(bf16[136,512]{1,0:T(8,128)(2,1)S(1)} %get-tuple-element.44.first), channel_id=1, source_target_pairs={{8,0},{16,8},{24,16},{9,1},{17,9},{25,17},{10,2},{18,10},{26,18},{... | collective-permute-start | bytes 417800 | tf_op jit(solution)/shard_map/ppermute | solution.py:537
  140.4 12.0 %collective-permute-start.5 = (bf16[136,512]{1,0:T(8,128)(2,1)S(1)}, bf16[136,512]{1,0:T(8,128)(2,1)S(1)}, u32[]{:S(2)}, u32[]{:S(2)}) collective-permute-start(bf16[136,512]{1,0:T(8,128)(2,1)S(1)} %get-tuple-element.44.first), channel_id=1, source_target_pairs={{24,0},{25,1},{26,2},{27,3},{28,4},{29,5},{30,6},{31,7}} | collective-permute-start | bytes 417800 | tf_op jit(solution)/shard_map/ppermute | solution.py:537
  146.1 7.4 %collective-permute-start.4 = (bf16[136,512]{1,0:T(8,128)(2,1)S(1)}, bf16[136,512]{1,0:T(8,128)(2,1)S(1)}, u32[]{:S(2)}, u32[]{:S(2)}) collective-permute-start(bf16[136,512]{1,0:T(8,128)(2,1)S(1)} %join.1), channel_id=1, source_target_pairs={{8,0},{16,8},{24,16},{9,1},{17,9},{25,17},{10,2},{18,10},{26,18},{... | collective-permute-start | bytes 417800 | tf_op jit(solution)/shard_map/ppermute | solution.py:537
  147.4 1.0 copy-start.8
  148.4 0.9 copy-start.9
  149.4 0.9 copy-start.10
  150.3 0.7 copy-start.11
